TPU v7x, 512 devices: a whole 4x4x16 slice. The times are simulated.
512 devices in a mesh: seq: 128 (over z, y, x_hi), branch: 4 (over x_lo, core).
Axes of the slice: x: 4 (x_hi: 2, x_lo: 2; x = x_hi * 2 + x_lo), y: 4, z: 16, core: 2. Of those that a mesh axis runs over, the one named last changes fastest.
Arguments:
- q_ctl: bfloat16 [4, 24576, 2048], P('branch', 'seq'), may hold values from -64 to 64
- k_ctl: bfloat16 [4, 24576, 2048], P('branch', 'seq'), may hold values from -64 to 64
- v_ctl: bfloat16 [4, 24576, 2048], P('branch', 'seq'), may hold values from -6 to 6
- positions: int32 [24576], P('seq'), may hold values from 0 to 12287
- branch_ids: int32 [4], P('branch'), may hold values from 0 to 63
- cond_scale: float32 [64], replicated, may hold values from 0.25 to 2
- out_weight: bfloat16 [2048, 3072], P('branch', 'seq'), may hold values from -0.125 to 0.125
- frozen: bfloat16 [24576, 3072], P(('seq', 'branch')), may hold values from -2.390625 to 2.390625
- norm_gain: float32 [3072], replicated, may hold values from 0.5 to 1.5
- cotangent: bfloat16 [24576, 3072], P('seq'), may hold values from -6 to 6
Outputs:
- normed: bfloat16 [24576, 3072], P(('seq', 'branch'))
- grad_attn: bfloat16 [4, 24576, 2048], P('branch', 'seq')
All inputs are finite; a program needn't handle non-finite values.
Results may differ from a plain program's by a relative error of at most 0.014.
Values may be sent and summed in bfloat16 or wider, within the bound.
No kernel may reach another device: no remote copies, remote signals or barrier semaphores. Data moves between devices by JAX's collectives and lax.ppermute only.
A program may use at most 64 MiB of HBM per device.

v0:
```python
import math

import jax
import jax.numpy as jnp
from jax import lax
from jax.sharding import PartitionSpec as P

HEADS = 16
HEAD_DIM = 128


EPS = 1e-06


def from_partner(shard, axis, distance):
    return lax.ppermute(shard, axis, [(i, i ^ 1 << distance) for i in range(lax.axis_size(axis))])


def rope_tables(positions, head_dim):
    exponents = jnp.arange(head_dim // 2, dtype=jnp.float32) * (2.0 / head_dim)
    frequencies = 10000.0 ** (-exponents)
    angles = positions.astype(jnp.float32)[..., None] * frequencies
    return (jnp.cos(angles), jnp.sin(angles))


def rotate(values_in, cosines, sines):
    half_dim = values_in.shape[-1] // 2
    front_half = values_in[..., :half_dim]
    back_half = values_in[..., half_dim:]
    return jnp.concatenate(
        [front_half * cosines - back_half * sines, back_half * cosines + front_half * sines],
        axis=-1,
    )


def normalize(hidden, norm_gain):
    inverse = lax.rsqrt(jnp.mean(hidden * hidden, axis=-1, keepdims=True) + EPS)
    return (hidden * inverse * norm_gain).astype(jnp.bfloat16)


def norm_grad(hidden, norm_gain, cotangent):
    inverse = lax.rsqrt(jnp.mean(hidden * hidden, axis=-1, keepdims=True) + EPS)
    upstream = cotangent.astype(jnp.float32) * norm_gain
    inner_mean = jnp.mean(upstream * hidden, axis=-1, keepdims=True)
    return (inverse * upstream - hidden * (inverse * inverse * inverse) * inner_mean).astype(
        jnp.bfloat16
    )


def attend_head(packed):
    query_rows, key_rows, value_rows = packed
    clip_len = query_rows.shape[0]
    block_rows = min(512, clip_len)
    factor = 1.0 / math.sqrt(query_rows.shape[-1])

    def one_block(query_block):
        scores = jnp.dot(query_block, key_rows.T, preferred_element_type=jnp.float32) * factor
        row_max = jnp.max(scores, axis=-1, keepdims=True)
        weights = jnp.exp(scores - row_max)
        row_total = jnp.sum(weights, axis=-1, keepdims=True)
        weights_low = (weights / row_total).astype(jnp.bfloat16)
        return jnp.dot(weights_low, value_rows, preferred_element_type=jnp.float32).astype(
            jnp.bfloat16
        )

    blocks = query_rows.reshape(clip_len // block_rows, block_rows, query_rows.shape[-1])
    return lax.map(one_block, blocks).reshape(clip_len, query_rows.shape[-1])


def regroup(buffer, group_bits, seq_index, forward):
    full_shape = buffer.shape
    split = buffer.reshape(full_shape[:1] + (2,) * group_bits + full_shape[2:])
    for bit in range(group_bits):
        axis_here = group_bits - bit
        mine = jnp.bitwise_and(jnp.right_shift(seq_index, bit), 1)
        other = 1 - mine
        outgoing = lax.dynamic_index_in_dim(split, other, axis_here, keepdims=True)
        if forward:
            incoming = from_partner(outgoing, "seq", bit)
        else:
            incoming = from_partner(outgoing, "seq", bit)
        split = lax.dynamic_update_index_in_dim(split, incoming, other, axis_here)
    return split.reshape(full_shape)


def on_device(
    q_ctl, k_ctl, v_ctl, positions, branch_ids, cond_scale, out_weight, frozen, norm_gain, cotangent
):
    branch_index = lax.axis_index("branch")
    quarters = lax.axis_size("branch")
    seq_index = lax.axis_index("seq")
    seq_devices = lax.axis_size("seq")
    group = min(HEADS, seq_devices)
    group_bits = group.bit_length() - 1
    local_len = q_ctl.shape[1]
    feature_width = q_ctl.shape[2]
    head_dim = HEAD_DIM
    head_count = feature_width // head_dim
    heads_here = head_count // group
    clip_len = group * local_len
    quarter_len = local_len // quarters
    model_width = cotangent.shape[1]
    cosines, sines = rope_tables(positions, head_dim)
    cosines = cosines[:, None, :]
    sines = sines[:, None, :]

    def heads_first(source, rotated):
        split_heads = source[0].reshape(local_len, head_count, head_dim)
        if rotated:
            split_heads = rotate(split_heads.astype(jnp.float32), cosines, sines).astype(
                jnp.bfloat16
            )
        split_heads = split_heads.reshape(local_len, group, heads_here, head_dim)
        return jnp.transpose(split_heads, (1, 0, 2, 3))

    stacked = jnp.stack(
        [heads_first(q_ctl, True), heads_first(k_ctl, True), heads_first(v_ctl, False)]
    )
    arrived = regroup(stacked, group_bits, seq_index, True)

    def per_head(member):
        return jnp.transpose(member, (2, 0, 1, 3)).reshape(heads_here, clip_len, head_dim)

    attended_heads = lax.map(
        attend_head, (per_head(arrived[0]), per_head(arrived[1]), per_head(arrived[2]))
    )
    going_back = jnp.transpose(
        attended_heads.reshape(heads_here, group, local_len, head_dim), (1, 2, 0, 3)
    )[None]
    returned = regroup(going_back, group_bits, seq_index, False)[0]
    attended = jnp.transpose(returned, (1, 0, 2, 3)).reshape(local_len, feature_width)
    branch_scale = jnp.sum(
        jnp.where(jnp.arange(cond_scale.shape[0]) == branch_ids[0], cond_scale, 0.0)
    )
    weight_rows = lax.all_gather(out_weight, "seq", axis=1, tiled=True)
    mixed = lax.psum_scatter(
        (branch_scale * attended.astype(jnp.float32)).astype(jnp.bfloat16),
        "branch",
        scatter_dimension=1,
        tiled=True,
    ).astype(jnp.float32)
    mixed_high = mixed.astype(jnp.bfloat16)
    mixed_rest = (mixed - mixed_high.astype(jnp.float32)).astype(jnp.bfloat16)
    partial_stream = jnp.dot(mixed_high, weight_rows, preferred_element_type=jnp.float32)
    partial_stream = partial_stream + jnp.dot(
        mixed_rest, weight_rows, preferred_element_type=jnp.float32
    )
    owner = (jnp.arange(quarters) == branch_index).astype(jnp.float32)[:, None, None]
    term = (
        partial_stream.reshape(quarters, quarter_len, model_width)
        + owner * frozen.astype(jnp.float32)[None]
    )
    hidden = (
        lax.psum(term.astype(jnp.bfloat16), "branch")
        .astype(jnp.float32)
        .reshape(local_len, model_width)
    )
    hidden_share = lax.dynamic_slice_in_dim(hidden, branch_index * quarter_len, quarter_len, 0)
    normed = normalize(hidden_share, norm_gain)
    grad_hidden = norm_grad(hidden, norm_gain, cotangent)
    cot_block = jnp.einsum(
        "td,hd->th", grad_hidden, weight_rows, preferred_element_type=jnp.float32
    ).astype(jnp.bfloat16)
    cot_attn = lax.all_gather(cot_block, "branch", axis=1, tiled=True)
    grad_attn = (branch_scale * cot_attn.astype(jnp.float32)).astype(jnp.bfloat16)
    return (normed, grad_attn.reshape(1, local_len, feature_width))


def solution(mesh):
    return jax.shard_map(
        on_device,
        mesh=mesh,
        in_specs=(
            P("branch", "seq", None),
            P("branch", "seq", None),
            P("branch", "seq", None),
            P("seq"),
            P("branch"),
            P(),
            P("branch", "seq"),
            P(("seq", "branch"), None),
            P(),
            P("seq", None),
        ),
        out_specs=(P(("seq", "branch"), None), P("branch", "seq", None)),
        check_vma=False,
    )
```

profile of v0, /device:TPU:1, one launch (start us, length us, event | category | flops | bytes accessed | tf_op | source)
XLA Modules:
  0.0 424.5 jit_solution(8821610244191821590)
XLA Ops:
  18.6 5.4 %collective-permute-start = (bf16[3,2,2,2,1,192,1,128]{7,5,4,3,2,1,6,0:T(8,128)(2,1)}, bf16[3,2,2,2,1,192,1,128]{7,5,4,3,2,1,6,0:T(8,128)(2,1)S(1)}, u32[]{:S(2)}, u32[]{:S(2)}) collective-permute-start(bf16[3,2,2,2,1,192,1,128]{7,5,4,3,2,1,6,0:T(8,128)(2,1)} %constant_dynamic-slice_fusion.7), channel_id=1, source_target_pairs={{0,4},{4,0},{8,12},{12,8},{16,20},{20,16},{24,28},{28,24},{32,36},... | collective-permute-start | bytes 3538952 | tf_op jit(solution)/shard_map/ppermute | solution.py:16
  24.1 22.6 %collective-permute-done = bf16[3,2,2,2,1,192,1,128]{7,5,4,3,2,1,6,0:T(8,128)(2,1)S(1)} collective-permute-done((bf16[3,2,2,2,1,192,1,128]{7,5,4,3,2,1,6,0:T(8,128)(2,1)}, bf16[3,2,2,2,1,192,1,128]{7,5,4,3,2,1,6,0:T(8,128)(2,1)S(1)}, u32[]{:S(2)}, u32[]{:S(2)}) %collective-permute-start) | collective-permute-done | bytes 1179680 | tf_op jit(solution)/shard_map/ppermute | solution.py:16
  47.9 6.5 %collective-permute-start.1 = (bf16[3,2,2,1,2,192,1,128]{7,5,4,3,2,1,6,0:T(8,128)(2,1)}, bf16[3,2,2,1,2,192,1,128]{7,5,4,3,2,1,6,0:T(8,128)(2,1)S(1)}, u32[]{:S(2)}, u32[]{:S(2)}) collective-permute-start(bf16[3,2,2,1,2,192,1,128]{7,5,4,3,2,1,6,0:T(8,128)(2,1)} %constant_dynamic-slice_fusion.6), channel_id=1, source_target_pairs={{0,8},{4,12},{8,0},{12,4},{16,24},{20,28},{24,16},{28,20},{32,40},... | collective-permute-start | bytes 3538952 | tf_op jit(solution)/shard_map/ppermute | solution.py:16
  54.4 24.8 %collective-permute-done.1 = bf16[3,2,2,1,2,192,1,128]{7,5,4,3,2,1,6,0:T(8,128)(2,1)S(1)} collective-permute-done((bf16[3,2,2,1,2,192,1,128]{7,5,4,3,2,1,6,0:T(8,128)(2,1)}, bf16[3,2,2,1,2,192,1,128]{7,5,4,3,2,1,6,0:T(8,128)(2,1)S(1)}, u32[]{:S(2)}, u32[]{:S(2)}) %collective-permute-start.1) | collective-permute-done | bytes 1179680 | tf_op jit(solution)/shard_map/ppermute | solution.py:16
  80.5 4.9 %collective-permute-start.2 = (bf16[3,2,1,2,2,192,1,128]{7,5,4,3,2,1,6,0:T(8,128)(2,1)}, bf16[3,2,1,2,2,192,1,128]{7,5,4,3,2,1,6,0:T(8,128)(2,1)S(1)}, u32[]{:S(2)}, u32[]{:S(2)}) collective-permute-start(bf16[3,2,1,2,2,192,1,128]{7,5,4,3,2,1,6,0:T(8,128)(2,1)} %constant_dynamic-slice_fusion.5), channel_id=1, source_target_pairs={{0,16},{4,20},{8,24},{12,28},{16,0},{20,4},{24,8},{28,12},{32,48},... | collective-permute-start | bytes 3538952 | tf_op jit(solution)/shard_map/ppermute | solution.py:16
  85.4 24.0 %collective-permute-done.2 = bf16[3,2,1,2,2,192,1,128]{7,5,4,3,2,1,6,0:T(8,128)(2,1)S(1)} collective-permute-done((bf16[3,2,1,2,2,192,1,128]{7,5,4,3,2,1,6,0:T(8,128)(2,1)}, bf16[3,2,1,2,2,192,1,128]{7,5,4,3,2,1,6,0:T(8,128)(2,1)S(1)}, u32[]{:S(2)}, u32[]{:S(2)}) %collective-permute-start.2) | collective-permute-done | bytes 1179680 | tf_op jit(solution)/shard_map/ppermute | solution.py:16
  110.8 3.5 collective-permute-start.3
  114.3 23.2 %collective-permute-done.3 = bf16[3,1,2,2,2,192,1,128]{7,5,4,3,2,1,6,0:T(8,128)(2,1)S(1)} collective-permute-done((bf16[3,1,2,2,2,192,1,128]{7,5,4,3,2,1,6,0:T(8,128)(2,1)}, bf16[3,1,2,2,2,192,1,128]{7,5,4,3,2,1,6,0:T(8,128)(2,1)S(1)}, u32[]{:S(2)}, u32[]{:S(2)}) %collective-permute-start.3) | collective-permute-done | bytes 1179680 | tf_op jit(solution)/shard_map/ppermute | solution.py:16
  139.0 31.2 %while.17 = (s32[]{:T(128)}, bf16[6,512,128]{2,1,0:T(8,128)(2,1)}, bf16[6,512,128]{2,1,0:T(8,128)(2,1)}, bf16[3072,128]{1,0:T(8,128)(2,1)S(1)}, bf16[3072,128]{1,0:T(8,128)(2,1)}, /*index=5*/s32[]{:T(128)}) while((s32[]{:T(128)}, bf16[6,512,128]{2,1,0:T(8,128)(2,1)}, bf16[6,512,128]{2,1,0:T(8,128)(2,1)}, bf16[3072,128]{1,0:T(8,128)(2,1)S(1)}, ...), condition=%wide.region_4.5_spmd, body=%wide.region_1.4_spmd.sunk | while | flops 819526656 | bytes 23866464 | solution.py:67
  142.2 2.1 fusion.37
  147.4 2.1 fusion.37
  152.6 2.1 fusion.37
  154.6 2.0 multiply_reduce_fusion.5
  157.8 2.1 fusion.37
  159.8 2.0 multiply_reduce_fusion.5
  163.0 2.1 fusion.37
  168.2 2.1 fusion.37
  171.3 4.6 %collective-permute-start.4 = (bf16[1,2,2,2,1,192,1,128]{7,5,4,3,2,1,6,0:T(8,128)(2,1)S(1)}, bf16[1,2,2,2,1,192,1,128]{7,5,4,3,2,1,6,0:T(8,128)(2,1)S(1)}, u32[]{:S(2)}, u32[]{:S(2)}) collective-permute-start(bf16[1,2,2,2,1,192,1,128]{7,5,4,3,2,1,6,0:T(8,128)(2,1)S(1)} %constant_dynamic-slice_fusion.3), channel_id=1, source_target_pairs={{0,4},{4,0},{8,12},{12,8},{16,20},{20,16},{24,28},{28,24},{32,36},... | collective-permute-start | bytes 1179656 | tf_op jit(solution)/shard_map/ppermute | solution.py:16
  175.9 5.4 %collective-permute-done.4 = bf16[1,2,2,2,1,192,1,128]{7,5,4,3,2,1,6,0:T(8,128)(2,1)S(1)} collective-permute-done((bf16[1,2,2,2,1,192,1,128]{7,5,4,3,2,1,6,0:T(8,128)(2,1)S(1)}, bf16[1,2,2,2,1,192,1,128]{7,5,4,3,2,1,6,0:T(8,128)(2,1)S(1)}, u32[]{:S(2)}, u32[]{:S(2)}) %collective-permute-start.4) | collective-permute-done | bytes 393248 | tf_op jit(solution)/shard_map/ppermute | solution.py:16
  183.2 3.2 collective-permute-start.5
  186.3 5.7 %collective-permute-done.5 = bf16[1,2,2,1,2,192,1,128]{7,5,4,3,2,1,6,0:T(8,128)(2,1)S(1)} collective-permute-done((bf16[1,2,2,1,2,192,1,128]{7,5,4,3,2,1,6,0:T(8,128)(2,1)S(1)}, bf16[1,2,2,1,2,192,1,128]{7,5,4,3,2,1,6,0:T(8,128)(2,1)S(1)}, u32[]{:S(2)}, u32[]{:S(2)}) %collective-permute-start.5) | collective-permute-done | bytes 393248 | tf_op jit(solution)/shard_map/ppermute | solution.py:16
  193.9 4.8 %collective-permute-start.6 = (bf16[1,2,1,2,2,192,1,128]{7,5,4,3,2,1,6,0:T(8,128)(2,1)S(1)}, bf16[1,2,1,2,2,192,1,128]{7,5,4,3,2,1,6,0:T(8,128)(2,1)S(1)}, u32[]{:S(2)}, u32[]{:S(2)}) collective-permute-start(bf16[1,2,1,2,2,192,1,128]{7,5,4,3,2,1,6,0:T(8,128)(2,1)S(1)} %constant_dynamic-slice_fusion.1), channel_id=1, source_target_pairs={{0,16},{4,20},{8,24},{12,28},{16,0},{20,4},{24,8},{28,12},{32,48},... | collective-permute-start | bytes 1179656 | tf_op jit(solution)/shard_map/ppermute | solution.py:16
  198.7 5.2 %collective-permute-done.6 = bf16[1,2,1,2,2,192,1,128]{7,5,4,3,2,1,6,0:T(8,128)(2,1)S(1)} collective-permute-done((bf16[1,2,1,2,2,192,1,128]{7,5,4,3,2,1,6,0:T(8,128)(2,1)S(1)}, bf16[1,2,1,2,2,192,1,128]{7,5,4,3,2,1,6,0:T(8,128)(2,1)S(1)}, u32[]{:S(2)}, u32[]{:S(2)}) %collective-permute-start.6) | collective-permute-done | bytes 393248 | tf_op jit(solution)/shard_map/ppermute | solution.py:16
  205.8 3.5 collective-permute-start.7
  210.6 4.3 %collective-permute-done.7 = bf16[1,1,2,2,2,192,1,128]{7,5,4,3,2,1,6,0:T(8,128)(2,1)S(1)} collective-permute-done((bf16[1,1,2,2,2,192,1,128]{7,5,4,3,2,1,6,0:T(8,128)(2,1)S(1)}, bf16[1,1,2,2,2,192,1,128]{7,5,4,3,2,1,6,0:T(8,128)(2,1)S(1)}, u32[]{:S(2)}, u32[]{:S(2)}) %collective-permute-start.7) | collective-permute-done | bytes 393248 | tf_op jit(solution)/shard_map/ppermute | solution.py:16
  215.6 2.0 multiply_convert_fusion.1
  220.4 109.9 %all-gather.2.cloned.1.call-done = bf16[512,3072]{0,1:T(8,128)(2,1)} async-done(((bf16[512,24]{0,1:T(8,128)(2,1)}), bf16[512,3072]{0,1:T(8,128)(2,1)}) %all-gather.2.cloned.1.call-update) | async-done | bytes 3145744 | tf_op jit(solution)/shard_map/all_gather | solution.py:135
  330.4 3.3 fusion.23
  336.3 62.4 %all-reduce.2.cloned.1.call-done = bf16[4,48,3072]{2,1,0:T(8,128)(2,1)} async-done(((bf16[4,48,3072]{2,1,0:T(8,128)(2,1)}), bf16[4,48,3072]{2,1,0:T(8,128)(2,1)}) %all-reduce.2.cloned.1.call-update) | async-done | bytes 1179664 | tf_op jit(solution)/shard_map/psum | solution.py:154
  398.7 3.5 multiply_reduce_fusion.1
  402.7 2.8 fusion.15
  405.5 8.8 %all_gather.7 = bf16[192,2048]{1,0:T(8,128)(2,1)S(1)} all-gather(bf16[192,512]{1,0:T(8,128)(2,1)S(1)} %fusion.15), channel_id=1, replica_groups=mesh['seq'=128,'branch'=4] {'branch'}, dimensions={1}, use_global_device_ids=true | all-gather | bytes 983040 | tf_op jit(solution)/shard_map/all_gather | solution.py:164
  (97 shorter events, 47.4 us)
Async XLA Ops:
  8.0 322.4 %all-gather.2.cloned.1.call-start = ((), (), s32[]{:S(2)}) async-start(), calls=%async_computation.2 | async-start | bytes 3170304 | tf_op jit(solution)/shard_map/all_gather | solution.py:135
  8.7 1.7 copy-start.7
  13.3 1.3 copy-start.6
  18.6 28.0 %collective-permute-start = (bf16[3,2,2,2,1,192,1,128]{7,5,4,3,2,1,6,0:T(8,128)(2,1)}, bf16[3,2,2,2,1,192,1,128]{7,5,4,3,2,1,6,0:T(8,128)(2,1)S(1)}, u32[]{:S(2)}, u32[]{:S(2)}) collective-permute-start(bf16[3,2,2,2,1,192,1,128]{7,5,4,3,2,1,6,0:T(8,128)(2,1)} %constant_dynamic-slice_fusion.7), channel_id=1, source_target_pairs={{0,4},{4,0},{8,12},{12,8},{16,20},{20,16},{24,28},{28,24},{32,36},... | collective-permute-start | bytes 3538952 | tf_op jit(solution)/shard_map/ppermute | solution.py:16
  47.9 31.3 %collective-permute-start.1 = (bf16[3,2,2,1,2,192,1,128]{7,5,4,3,2,1,6,0:T(8,128)(2,1)}, bf16[3,2,2,1,2,192,1,128]{7,5,4,3,2,1,6,0:T(8,128)(2,1)S(1)}, u32[]{:S(2)}, u32[]{:S(2)}) collective-permute-start(bf16[3,2,2,1,2,192,1,128]{7,5,4,3,2,1,6,0:T(8,128)(2,1)} %constant_dynamic-slice_fusion.6), channel_id=1, source_target_pairs={{0,8},{4,12},{8,0},{12,4},{16,24},{20,28},{24,16},{28,20},{32,40},... | collective-permute-start | bytes 3538952 | tf_op jit(solution)/shard_map/ppermute | solution.py:16
  80.5 28.9 %collective-permute-start.2 = (bf16[3,2,1,2,2,192,1,128]{7,5,4,3,2,1,6,0:T(8,128)(2,1)}, bf16[3,2,1,2,2,192,1,128]{7,5,4,3,2,1,6,0:T(8,128)(2,1)S(1)}, u32[]{:S(2)}, u32[]{:S(2)}) collective-permute-start(bf16[3,2,1,2,2,192,1,128]{7,5,4,3,2,1,6,0:T(8,128)(2,1)} %constant_dynamic-slice_fusion.5), channel_id=1, source_target_pairs={{0,16},{4,20},{8,24},{12,28},{16,0},{20,4},{24,8},{28,12},{32,48},... | collective-permute-start | bytes 3538952 | tf_op jit(solution)/shard_map/ppermute | solution.py:16
  110.8 26.7 %collective-permute-start.3 = (bf16[3,1,2,2,2,192,1,128]{7,5,4,3,2,1,6,0:T(8,128)(2,1)}, bf16[3,1,2,2,2,192,1,128]{7,5,4,3,2,1,6,0:T(8,128)(2,1)S(1)}, u32[]{:S(2)}, u32[]{:S(2)}) collective-permute-start(bf16[3,1,2,2,2,192,1,128]{7,5,4,3,2,1,6,0:T(8,128)(2,1)} %constant_dynamic-slice_fusion.4), channel_id=1, source_target_pairs={{0,32},{4,36},{8,40},{12,44},{16,48},{20,52},{24,56},{28,60},{32,0... | collective-permute-start | bytes 3538952 | tf_op jit(solution)/shard_map/ppermute | solution.py:16
  114.3 216.1 %reduce-scatter.2.cloned.1.call-start = ((), (), s32[]{:S(2)}) async-start(), calls=%async_computation.1 | async-start | bytes 983040 | tf_op jit(solution)/shard_map/reduce_scatter | solution.py:136
  141.0 1.2 copy-start.4
  146.2 1.2 copy-start.4
  151.4 1.2 copy-start.4
  156.6 1.2 copy-start.4
  161.8 1.2 copy-start.4
  167.0 1.2 copy-start.4
  171.3 38.6 %copy-start.10 = (f32[64]{0:T(128)S(1)}, f32[64]{0:T(128)}, u32[]{:S(2)}) copy-start(f32[64]{0:T(128)} %param.17) | copy-start | bytes 772
  171.3 10.0 %collective-permute-start.4 = (bf16[1,2,2,2,1,192,1,128]{7,5,4,3,2,1,6,0:T(8,128)(2,1)S(1)}, bf16[1,2,2,2,1,192,1,128]{7,5,4,3,2,1,6,0:T(8,128)(2,1)S(1)}, u32[]{:S(2)}, u32[]{:S(2)}) collective-permute-start(bf16[1,2,2,2,1,192,1,128]{7,5,4,3,2,1,6,0:T(8,128)(2,1)S(1)} %constant_dynamic-slice_fusion.3), channel_id=1, source_target_pairs={{0,4},{4,0},{8,12},{12,8},{16,20},{20,16},{24,28},{28,24},{32,36},... | collective-permute-start | bytes 1179656 | tf_op jit(solution)/shard_map/ppermute | solution.py:16
  183.2 8.9 %collective-permute-start.5 = (bf16[1,2,2,1,2,192,1,128]{7,5,4,3,2,1,6,0:T(8,128)(2,1)S(1)}, bf16[1,2,2,1,2,192,1,128]{7,5,4,3,2,1,6,0:T(8,128)(2,1)S(1)}, u32[]{:S(2)}, u32[]{:S(2)}) collective-permute-start(bf16[1,2,2,1,2,192,1,128]{7,5,4,3,2,1,6,0:T(8,128)(2,1)S(1)} %constant_dynamic-slice_fusion.2), channel_id=1, source_target_pairs={{0,8},{4,12},{8,0},{12,4},{16,24},{20,28},{24,16},{28,20},{32,40},... | collective-permute-start | bytes 1179656 | tf_op jit(solution)/shard_map/ppermute | solution.py:16
  193.9 10.0 %collective-permute-start.6 = (bf16[1,2,1,2,2,192,1,128]{7,5,4,3,2,1,6,0:T(8,128)(2,1)S(1)}, bf16[1,2,1,2,2,192,1,128]{7,5,4,3,2,1,6,0:T(8,128)(2,1)S(1)}, u32[]{:S(2)}, u32[]{:S(2)}) collective-permute-start(bf16[1,2,1,2,2,192,1,128]{7,5,4,3,2,1,6,0:T(8,128)(2,1)S(1)} %constant_dynamic-slice_fusion.1), channel_id=1, source_target_pairs={{0,16},{4,20},{8,24},{12,28},{16,0},{20,4},{24,8},{28,12},{32,48},... | collective-permute-start | bytes 1179656 | tf_op jit(solution)/shard_map/ppermute | solution.py:16
  205.8 9.1 %collective-permute-start.7 = (bf16[1,1,2,2,2,192,1,128]{7,5,4,3,2,1,6,0:T(8,128)(2,1)S(1)}, bf16[1,1,2,2,2,192,1,128]{7,5,4,3,2,1,6,0:T(8,128)(2,1)S(1)}, u32[]{:S(2)}, u32[]{:S(2)}) collective-permute-start(bf16[1,1,2,2,2,192,1,128]{7,5,4,3,2,1,6,0:T(8,128)(2,1)S(1)} %constant_dynamic-slice_fusion), channel_id=1, source_target_pairs={{0,32},{4,36},{8,40},{12,44},{16,48},{20,52},{24,56},{28,60},{32,0... | collective-permute-start | bytes 1179656 | tf_op jit(solution)/shard_map/ppermute | solution.py:16
  217.6 2.0 copy-start.8
  219.5 179.2 %all-reduce.2.cloned.1.call-start = ((), (), s32[]{:S(2)}) async-start(), calls=%async_computation.3 | async-start | bytes 2359296 | tf_op jit(solution)/shard_map/psum | solution.py:154
  330.4 3.3 copy-start
  330.4 3.3 copy-start.5
  333.7 1.2 copy-start.3
  334.9 63.8 %copy-start.9 = (f32[3072]{0:T(1024)S(1)}, f32[3072]{0:T(1024)}, u32[]{:S(2)}) copy-start(f32[3072]{0:T(1024)} %param.20) | copy-start | bytes 36868
  398.7 3.5 copy-start.2
  405.5 10.5 %copy-start.1 = (f32[192,3072]{1,0:T(8,128)S(1)}, f32[192,3072]{1,0:T(8,128)}, u32[]{:S(2)}) copy-start(f32[192,3072]{1,0:T(8,128)} %get-tuple-element.56) | copy-start | bytes 7077892
Sparse Core Ops, SparseCore 0:
  114.4 215.9 all-gather.1
Sparse Core Ops, SparseCore 1:
  219.6 39.7 reduce-scatter.1
  336.4 62.3 all-reduce.1
where the time goes:
time: 425 us; the launch traced here: 424 us
  waiting for transfers between devices  288 us (68%)
  starting transfers between devices  36.4 us (9%)
  matrix products  31.5 us (7%)
  other arithmetic  24.5 us (6%)
  local copies, waits for them, and re-layouts  19.1 us (4%)
  between operations  16.5 us (4%)
  blocking collectives  8.84 us (2%)
    ppermute x8, waiting for transfers between devices, from_partner(): lax.ppermute(shard, axis, [(i, i ^ 1 << distance) for i in range(lax.axis...  115 us
    all_gather x1, waiting for transfers between devices, on_device(): weight_rows = lax.all_gather(out_weight, 'seq', axis=1, tiled=True)  110 us
    psum x1, waiting for transfers between devices, on_device(): lax.psum(term.astype(jnp.bfloat16), 'branch').astype(jnp.float32)  62.4 us
    ppermute x8, starting transfers between devices, from_partner(): lax.ppermute(shard, axis, [(i, i ^ 1 << distance) for i in range(lax.axis...  36.3 us
    dot_general x6, matrix products, one_block(): jnp.dot(weights_low, value_rows, preferred_element_type=jnp.float32)  12.4 us
    dot_general x6, matrix products, one_block(): jnp.dot(query_block, key_rows.T, preferred_element_type=jnp.float32)  11.8 us
    all_gather x1, blocking collectives, on_device(): cot_attn = lax.all_gather(cot_block, 'branch', axis=1, tiled=True)  8.84 us
    dynamic_slice x8, local copies, waits for them, and re-layouts, regroup(): outgoing = lax.dynamic_index_in_dim(split, other, axis_here, keepdims=True)  8.65 us
  transfers between devices with their start and end apart: 11, of which 10 were waited for; matrix products, arithmetic and copies ran while one was open for 11% of the time, Pallas kernels for 0%

commit v1 on v0

v1 whole, which is shorter than its diff:
```python
import math

import jax
import jax.numpy as jnp
from jax import lax
from jax.experimental import pallas as pl
from jax.experimental.pallas import tpu as pltpu
from jax.sharding import Mesh
from jax.sharding import PartitionSpec as P

HEADS = 16
HEAD_DIM = 128
EPS = 1e-06
CLIP = ("z", "y", "h")
SEQ = ("c", "z", "y", "h")
BRANCH = ("l", "k")
F32 = jnp.float32
BF16 = jnp.bfloat16
NT = (((1,), (1,)), ((), ()))


def rope_tables(positions):
    exponents = jnp.arange(HEAD_DIM // 2, dtype=F32) * (2.0 / HEAD_DIM)
    angles = positions.astype(F32)[:, None] * (10000.0 ** (-exponents))
    cosines, sines = jnp.cos(angles), jnp.sin(angles)
    return (
        jnp.concatenate([cosines, cosines], axis=1),
        jnp.concatenate([-sines, sines], axis=1),
    )


def prepare(q, k, v, cosines, sines):
    rows = q.shape[0]
    factor = math.log2(math.e) / math.sqrt(HEAD_DIM)

    def kernel(q_ref, k_ref, v_ref, c_ref, s_ref, o_ref):
        c, s = c_ref[...], s_ref[...]

        def rotated(x):
            x = x.astype(F32)
            return x * c + pltpu.roll(x, HEAD_DIM // 2, 1) * s

        o_ref[0, 0:rows, :] = (rotated(q_ref[...]) * factor).astype(BF16)
        o_ref[0, rows : 2 * rows, :] = rotated(k_ref[...]).astype(BF16)
        o_ref[0, 2 * rows :, :] = v_ref[...]

    column = pl.BlockSpec((rows, HEAD_DIM), lambda i: (0, i))
    whole = pl.BlockSpec((rows, HEAD_DIM), lambda i: (0, 0))
    return pl.pallas_call(
        kernel,
        out_shape=jax.ShapeDtypeStruct((HEADS, 3 * rows, HEAD_DIM), BF16),
        grid=(HEADS,),
        in_specs=[column, column, column, whole, whole],
        out_specs=pl.BlockSpec((1, 3 * rows, HEAD_DIM), lambda i: (i, 0, 0)),
        name="prepare",
    )(q, k, v, cosines, sines)


def attend(blocks, scale):
    sources, three_rows, _ = blocks.shape
    rows = three_rows // 3
    length = sources * rows
    bq, kc, kt = 512, 512, 256
    steps = length // bq

    def kernel(scale_ref, b_ref, o_ref, q_ref, k_ref, v_ref, s_ref, m_ref):
        for j in range(sources):
            at = slice(j * rows, (j + 1) * rows)
            q_ref[at, :] = b_ref[j, 0:rows, :]
            k_ref[at, :] = b_ref[j, rows : 2 * rows, :]
            v_ref[at, 0:HEAD_DIM] = b_ref[j, 2 * rows :, :]
        v_ref[:, HEAD_DIM:] = jnp.ones((length, HEAD_DIM), BF16)

        def scores(i, slot):
            q = q_ref[pl.ds(pl.multiple_of(i * bq, bq), bq), :]
            top = None
            for j in range(length // kt):
                s = lax.dot_general(
                    q, k_ref[j * kt : (j + 1) * kt, :], NT, preferred_element_type=F32
                )
                s_ref[slot, :, j * kt : (j + 1) * kt] = s
                for half in range(kt // 128):
                    part = s[:, half * 128 : (half + 1) * 128]
                    top = part if top is None else jnp.maximum(top, part)
            m_ref[slot] = jnp.broadcast_to(jnp.max(top, axis=1, keepdims=True), (bq, 128))

        def mix(i, slot):
            top = jnp.concatenate([m_ref[slot]] * (kc // 128), axis=1)
            total = None
            for j in range(length // kc):
                p = jnp.exp2(s_ref[slot, :, j * kc : (j + 1) * kc] - top).astype(BF16)
                part = jnp.dot(p, v_ref[j * kc : (j + 1) * kc, :], preferred_element_type=F32)
                total = part if total is None else total + part
            out = total[:, :HEAD_DIM] * (scale_ref[0] / total[:, HEAD_DIM:])
            o_ref[pl.ds(pl.multiple_of(i * bq, bq), bq), :] = out.astype(BF16)

        scores(0, 0)

        def pair(t, carry):
            i = 2 * t
            scores(i + 1, 1)
            mix(i, 0)
            scores(i + 2, 0)
            mix(i + 1, 1)
            return carry

        lax.fori_loop(0, (steps - 2) // 2, pair, 0)
        scores(steps - 1, 1)
        mix(steps - 2, 0)
        mix(steps - 1, 1)

    return pl.pallas_call(
        kernel,
        out_shape=jax.ShapeDtypeStruct((length, HEAD_DIM), BF16),
        in_specs=[
            pl.BlockSpec(memory_space=pltpu.SMEM),
            pl.BlockSpec(memory_space=pltpu.VMEM),
        ],
        out_specs=pl.BlockSpec(memory_space=pltpu.VMEM),
        scratch_shapes=[
            pltpu.VMEM((length, HEAD_DIM), BF16),
            pltpu.VMEM((length, HEAD_DIM), BF16),
            pltpu.VMEM((length, 2 * HEAD_DIM), BF16),
            pltpu.VMEM((2, bq, length), F32),
            pltpu.VMEM((2, bq, 128), F32),
        ],
        compiler_params=pltpu.CompilerParams(vmem_limit_bytes=48 << 20),
        name="attend",
    )(scale, blocks)


def on_device(
    q_ctl, k_ctl, v_ctl, positions, branch_ids, cond_scale, out_weight, frozen, norm_gain, cotangent
):
    branch = lax.axis_index(BRANCH)
    share = frozen.shape[0]
    width = frozen.shape[1]
    scale = jnp.sum(jnp.where(jnp.arange(cond_scale.shape[0]) == branch_ids[0], cond_scale, 0.0))

    weight_t = lax.all_gather(out_weight.T, SEQ + BRANCH, axis=0, tiled=True)
    weight_t = weight_t.reshape(width // out_weight.shape[1], 4, out_weight.shape[1], -1)
    weight_t = jnp.transpose(weight_t, (0, 2, 1, 3)).reshape(width, -1)

    cosines, sines = rope_tables(positions)
    blocks = prepare(q_ctl[0], k_ctl[0], v_ctl[0], cosines, sines)
    blocks = lax.all_to_all(blocks, CLIP, 0, 0, tiled=True)
    attended = attend(blocks, scale.reshape(1))
    pieces = lax.all_to_all(
        attended.reshape(HEADS * 4, share, HEAD_DIM), CLIP + BRANCH, 0, 0, tiled=True
    )
    mixed = jnp.sum(pieces.reshape(HEADS, 4, share, HEAD_DIM).astype(F32), axis=1)
    mixed = jnp.transpose(mixed, (1, 0, 2)).reshape(share, -1).astype(BF16)

    hidden = frozen.astype(F32) + lax.dot_general(mixed, weight_t, NT, preferred_element_type=F32)
    inverse = lax.rsqrt(jnp.mean(hidden * hidden, axis=-1, keepdims=True) + EPS)
    normed = (hidden * inverse * norm_gain).astype(BF16)
    upstream = lax.dynamic_slice_in_dim(cotangent, branch * share, share, 0).astype(F32) * norm_gain
    inner = jnp.mean(upstream * hidden, axis=-1, keepdims=True)
    grad = (inverse * upstream - hidden * (inverse * inverse * inverse) * inner).astype(BF16)
    cot = jnp.dot(grad, weight_t, preferred_element_type=F32).astype(BF16)
    cot = lax.all_gather(cot, BRANCH, axis=0, tiled=True)
    grad_attn = (scale * cot.astype(F32)).astype(BF16)
    return normed, grad_attn[None]


def solution(mesh):
    fine = Mesh(mesh.devices.reshape(8, 2, 4, 2, 2, 2), SEQ + BRANCH)
    return jax.shard_map(
        on_device,
        mesh=fine,
        in_specs=(
            P(BRANCH, SEQ, None),
            P(BRANCH, SEQ, None),
            P(BRANCH, SEQ, None),
            P(SEQ),
            P(BRANCH),
            P(),
            P(BRANCH, SEQ),
            P(SEQ + BRANCH, None),
            P(),
            P(SEQ, None),
        ),
        out_specs=(P(SEQ + BRANCH, None), P(BRANCH, SEQ, None)),
        check_vma=False,
    )
```

time: 425 us -> 290 us (0.68)
  waiting for transfers between devices: 288 us -> 193 us
  matrix products: 31.5 us -> 6.47 us
  Pallas kernels: 0 us -> 22.6 us
  other arithmetic: 24.5 us -> 5.93 us
  starting transfers between devices: 36.4 us -> 21.9 us
    ppermute x8 -> x0, waiting for transfers between devices: 115 us -> none  [from_partner(): lax.ppermute(shard, axis, [(i, i ^ 1 << distance) for i in range(lax.axis...]
    psum x1 -> x0, waiting for transfers between devices: 62.4 us -> none  [on_device(): lax.psum(term.astype(jnp.bfloat16), 'branch').astype(jnp.float32)]
    all_to_all x0 -> x2, waiting for transfers between devices: none -> 42.3 us  [the longest x1 27.5 us: on_device(): blocks = lax.all_to_all(blocks, CLIP, 0, 0, tiled=True)]
    all_gather x1, waiting for transfers between devices: 110 us -> 150 us  [on_device(): weight_t = lax.all_gather(out_weight.T, SEQ + BRANCH, axis=0, tiled=True)]
    ppermute x8 -> x0, starting transfers between devices: 36.3 us -> none  [from_partner(): lax.ppermute(shard, axis, [(i, i ^ 1 << distance) for i in range(lax.axis...]
    dot_general x15 -> x2, matrix products: 31.5 us -> 6.47 us  [the longest x1 4.08 us: on_device(): lax.dot_general(mixed, weight_t, NT, preferred_element_type=F32)]
    pallas_call x0 -> x2, Pallas kernels: none -> 22.6 us  [the longest x1 12.7 us: attend(): pl.pallas_call(kernel, out_shape=jax.ShapeDtypeStruct((length, HEAD_DIM),...]
    all_to_all x0 -> x2, starting transfers between devices: none -> 21.9 us  [the longest x1 13 us: on_device(): lax.all_to_all(attended.reshape(HEADS * 4, share, HEAD_DIM), CLIP + BRANC...]
  transfers between devices with their start and end apart: 11 -> 3, of which waited for: 10 -> 3; matrix products, arithmetic and copies ran while one was open for 11% -> 1% of each run, Pallas kernels for 0% -> 8%
where the time goes in v1:
time: 290 us; the launch traced here: 288 us
  waiting for transfers between devices  193 us (67%)
  Pallas kernels  22.6 us (8%)
  starting transfers between devices  21.9 us (8%)
  local copies, waits for them, and re-layouts  15.1 us (5%)
  between operations  14.8 us (5%)
  blocking collectives  8.71 us (3%)
  matrix products  6.47 us (2%)
  other arithmetic  5.93 us (2%)
    all_gather x1, waiting for transfers between devices, on_device(): weight_t = lax.all_gather(out_weight.T, SEQ + BRANCH, axis=0, tiled=True)  150 us
    all_to_all x1, waiting for transfers between devices, on_device(): blocks = lax.all_to_all(blocks, CLIP, 0, 0, tiled=True)  27.5 us
    all_to_all x1, waiting for transfers between devices, on_device(): lax.all_to_all(attended.reshape(HEADS * 4, share, HEAD_DIM), CLIP + BRANC...  14.8 us
    all_to_all x1, starting transfers between devices, on_device(): lax.all_to_all(attended.reshape(HEADS * 4, share, HEAD_DIM), CLIP + BRANC...  13 us
    pallas_call x1, Pallas kernels, attend(): pl.pallas_call(kernel, out_shape=jax.ShapeDtypeStruct((length, HEAD_DIM),...  12.7 us
    reshape x1, local copies, waits for them, and re-layouts, on_device(): weight_t.reshape(width // out_weight.shape[1], 4, out_weight.shape[1], -1)  12 us
    pallas_call x1, Pallas kernels, prepare(): pl.pallas_call(kernel, out_shape=jax.ShapeDtypeStruct((HEADS, 3 * rows, H...  9.91 us
    all_to_all x1, starting transfers between devices, on_device(): blocks = lax.all_to_all(blocks, CLIP, 0, 0, tiled=True)  8.93 us
  transfers between devices with their start and end apart: 3, of which 3 were waited for; matrix products, arithmetic and copies ran while one was open for 1% of the time, Pallas kernels for 8%

profile of v1, /device:TPU:1, one launch (start us, length us, event | category | flops | bytes accessed | tf_op | source)
XLA Modules:
  0.0 288.5 jit_solution(4539845046169518848)
XLA Ops:
  7.2 0.0 all-gather.2.cloned.1.call-start
  7.2 0.7 all-gather.2.cloned.1.call-update
  7.9 0.7 convert_element_type.40
  8.6 0.4 fusion.8
  9.0 0.8 pad_maximum_fusion
  9.8 9.9 %prepare.1 = bf16[16,576,128]{2,1,0:T(8,128)(2,1)} custom-call(bf16[192,2048]{1,0:T(8,128)(2,1)} %bitcast.33, bf16[192,2048]{1,0:T(8,128)(2,1)} %bitcast.34, bf16[192,2048]{1,0:T(8,128)(2,1)} %bitcast.35, f32[192,128]{1,0:T(8,128)} %get-tuple-element.10.c_ref, f32[192,128]{1,0:T(8,128)} %get-tuple-element.11.s_ref), custom_call_target="tpu_custom_call" | custom-call | tf_op jit(solution)/shard_map/prepare/pallas_call | solution.py:49
  19.7 8.9 %all-to-all-start = ((bf16[16,576,128]{2,1,0:T(8,128)(2,1)}), bf16[16,576,128]{2,1,0:T(8,128)(2,1)S(1)}, u32[]{:S(2)}, u32[]{:S(2)}) async-start(bf16[16,576,128]{2,1,0:T(8,128)(2,1)} %prepare.1), calls=%async_computation | async-start | bytes 4718592 | tf_op jit(solution)/shard_map/all_to_all | solution.py:146
  29.3 1.3 fusion.9
  30.7 27.5 %all-to-all-done.b_ref = bf16[16,576,128]{2,1,0:T(8,128)(2,1)S(1)} async-done(((bf16[16,576,128]{2,1,0:T(8,128)(2,1)}), bf16[16,576,128]{2,1,0:T(8,128)(2,1)S(1)}, u32[]{:S(2)}, u32[]{:S(2)}) %all-to-all-start) | async-done | bytes 2359328 | tf_op jit(solution)/shard_map/all_to_all | solution.py:146
  58.1 12.7 %attend.1 = bf16[3072,128]{1,0:T(8,128)(2,1)} custom-call(f32[1]{0:T(128)} %bitcast.1.scale_ref, bf16[16,576,128]{2,1,0:T(8,128)(2,1)S(1)} %all-to-all-done.b_ref), custom_call_target="tpu_custom_call" | custom-call | tf_op jit(solution)/shard_map/attend/pallas_call | solution.py:112
  70.8 13.0 %all-to-all-start.1 = ((bf16[64,48,128]{2,1,0:T(8,128)(2,1)}), bf16[64,48,128]{2,1,0:T(8,128)(2,1)S(1)}, u32[]{:S(2)}, u32[]{:S(2)}) async-start(bf16[64,48,128]{2,1,0:T(8,128)(2,1)} %bitcast.5), calls=%async_computation.1 | async-start | bytes 1572864 | tf_op jit(solution)/shard_map/all_to_all | solution.py:148
  83.8 14.8 %all-to-all-done.1 = bf16[64,48,128]{2,1,0:T(8,128)(2,1)S(1)} async-done(((bf16[64,48,128]{2,1,0:T(8,128)(2,1)}), bf16[64,48,128]{2,1,0:T(8,128)(2,1)S(1)}, u32[]{:S(2)}, u32[]{:S(2)}) %all-to-all-start.1) | async-done | bytes 786464 | tf_op jit(solution)/shard_map/all_to_all | solution.py:148
  98.6 0.1 bitcast_reduce_fusion
  98.7 149.9 %all-gather.2.cloned.1.call-done = bf16[12288,512]{1,0:T(8,128)(2,1)} async-done(((bf16[24,512]{1,0:T(8,128)(2,1)}), bf16[12288,512]{1,0:T(8,128)(2,1)}) %all-gather.2.cloned.1.call-update) | async-done | bytes 12582928 | tf_op jit(solution)/shard_map/all_gather | solution.py:140
  248.6 12.0 %copy.14 = bf16[128,4,24,512]{3,1,2,0:T(4,128)(2,1)S(1)} copy(bf16[128,4,24,512]{3,2,1,0:T(8,128)(2,1)} %bitcast.32) | data formatting | bytes 25165824 | tf_op jit(solution)/shard_map/reshape | solution.py:141
  260.7 0.0 copy-start
  260.7 0.0 copy-start.1
  260.7 0.0 copy-start.2
  260.7 3.1 %copy.16 = bf16[384,8,4,512]{3,1,2,0:T(8,128)(2,1)S(1)} copy(bf16[384,8,4,512]{3,2,1,0:T(4,128)(2,1)S(1)} %bitcast.31) | data formatting | bytes 25165824
  263.8 0.0 copy-done
  263.8 0.0 copy-done.1
  263.8 0.0 copy-done.2
  263.8 4.1 %multiply_reduce_fusion = (f32[48]{0:T(128)S(1)}, f32[48]{0:T(128)S(1)}, f32[48,3072]{1,0:T(8,128)S(1)}) fusion(f32[3072]{0:T(1024)S(1)} %copy-done.2, bf16[192,3072]{1,0:T(8,128)(2,1)S(1)} %copy-done.1, s32[]{:T(128)S(6)} %select_n.8, bf16[3072,2048]{1,0:T(8,128)(2,1)S(1)} %bitcast.29, bf16[48,3072]{1,0:T(8,128)(2,1)S(1)} %copy-done, ...), kind=kOutput, calls=%fused_computation.6 | convolution fusion | flops 605159296 | bytes 13971844 | tf_op jit(solution)/shard_map/dot_general | solution.py:154
  268.0 0.8 multiply_convert_fusion.1
  268.8 2.4 convolution_convert_fusion
  271.2 8.7 %all_gather.7 = bf16[192,2048]{1,0:T(8,128)(2,1)S(1)} all-gather(bf16[48,2048]{1,0:T(8,128)(2,1)S(1)} %convolution_convert_fusion), channel_id=1, replica_groups=mesh['c'=8,'z'=2,'y'=4,'h'=2,'l'=2,'k'=2] {'l','k'}, dimensions={0}, use_global_device_ids=true | all-gather | bytes 983040 | tf_op jit(solution)/shard_map/all_gather | solution.py:161
  279.9 1.7 fusion
  (3 shorter events, 0.0 us)
Async XLA Ops:
  7.2 241.5 %all-gather.2.cloned.1.call-start = ((), (), s32[]{:S(2)}) async-start(), calls=%async_computation.2 | async-start | bytes 12607488 | tf_op jit(solution)/shard_map/all_gather | solution.py:140
  19.7 38.4 %all-to-all-start = ((bf16[16,576,128]{2,1,0:T(8,128)(2,1)}), bf16[16,576,128]{2,1,0:T(8,128)(2,1)S(1)}, u32[]{:S(2)}, u32[]{:S(2)}) async-start(bf16[16,576,128]{2,1,0:T(8,128)(2,1)} %prepare.1), calls=%async_computation | async-start | bytes 4718592 | tf_op jit(solution)/shard_map/all_to_all | solution.py:146
  70.8 27.8 %all-to-all-start.1 = ((bf16[64,48,128]{2,1,0:T(8,128)(2,1)}), bf16[64,48,128]{2,1,0:T(8,128)(2,1)S(1)}, u32[]{:S(2)}, u32[]{:S(2)}) async-start(bf16[64,48,128]{2,1,0:T(8,128)(2,1)} %bitcast.5), calls=%async_computation.1 | async-start | bytes 1572864 | tf_op jit(solution)/shard_map/all_to_all | solution.py:148
  260.7 3.1 %copy-start = (bf16[48,3072]{1,0:T(8,128)(2,1)S(1)}, bf16[48,3072]{1,0:T(8,128)(2,1)}, u32[]{:S(2)}) copy-start(bf16[48,3072]{1,0:T(8,128)(2,1)} %param.17) | copy-start | bytes 884740
  260.7 3.1 %copy-start.1 = (bf16[192,3072]{1,0:T(8,128)(2,1)S(1)}, bf16[192,3072]{1,0:T(8,128)(2,1)}, u32[]{:S(2)}) copy-start(bf16[192,3072]{1,0:T(8,128)(2,1)} %param.19) | copy-start | bytes 3538948
  260.7 3.1 %copy-start.2 = (f32[3072]{0:T(1024)S(1)}, f32[3072]{0:T(1024)}, u32[]{:S(2)}) copy-start(f32[3072]{0:T(1024)} %param.18) | copy-start | bytes 36868
Sparse Core Ops, SparseCore 0:
  12.7 235.8 all-gather.1

commit v2 on v1

--- a/solution.py
+++ b/solution.py
@@ -7,6 +7,7 @@
 from jax.experimental.pallas import tpu as pltpu
 from jax.sharding import Mesh
 from jax.sharding import PartitionSpec as P
+
 
 HEADS = 16
 HEAD_DIM = 128
@@ -32,26 +33,27 @@
 def prepare(q, k, v, cosines, sines):
     rows = q.shape[0]
     factor = math.log2(math.e) / math.sqrt(HEAD_DIM)
+    group = 4
 
     def kernel(q_ref, k_ref, v_ref, c_ref, s_ref, o_ref):
         c, s = c_ref[...], s_ref[...]
-
-        def rotated(x):
-            x = x.astype(F32)
-            return x * c + pltpu.roll(x, HEAD_DIM // 2, 1) * s
-
-        o_ref[0, 0:rows, :] = (rotated(q_ref[...]) * factor).astype(BF16)
-        o_ref[0, rows : 2 * rows, :] = rotated(k_ref[...]).astype(BF16)
-        o_ref[0, 2 * rows :, :] = v_ref[...]
-
-    column = pl.BlockSpec((rows, HEAD_DIM), lambda i: (0, i))
+        cq, sq = c * factor, s * factor
+        for g in range(group):
+            at = slice(g * HEAD_DIM, (g + 1) * HEAD_DIM)
+            x = q_ref[:, at].astype(F32)
+            o_ref[g, 0:rows, :] = (x * cq + pltpu.roll(x, HEAD_DIM // 2, 1) * sq).astype(BF16)
+            x = k_ref[:, at].astype(F32)
+            o_ref[g, rows : 2 * rows, :] = (x * c + pltpu.roll(x, HEAD_DIM // 2, 1) * s).astype(BF16)
+            o_ref[g, 2 * rows :, :] = v_ref[:, at]
+
+    column = pl.BlockSpec((rows, group * HEAD_DIM), lambda i: (0, i))
     whole = pl.BlockSpec((rows, HEAD_DIM), lambda i: (0, 0))
     return pl.pallas_call(
         kernel,
         out_shape=jax.ShapeDtypeStruct((HEADS, 3 * rows, HEAD_DIM), BF16),
-        grid=(HEADS,),
+        grid=(HEADS // group,),
         in_specs=[column, column, column, whole, whole],
-        out_specs=pl.BlockSpec((1, 3 * rows, HEAD_DIM), lambda i: (i, 0, 0)),
+        out_specs=pl.BlockSpec((group, 3 * rows, HEAD_DIM), lambda i: (i, 0, 0)),
         name="prepare",
     )(q, k, v, cosines, sines)
 
@@ -129,42 +131,227 @@
     )(scale, blocks)
 
 
+def exchange(x, partner):
+    count = math.prod(lax.axis_size(name) for name in SEQ + BRANCH)
+    return lax.ppermute(x, SEQ + BRANCH, [(i, partner(i)) for i in range(count)])
+
+
+def sum_pieces(pieces, core):
+    _, share, _ = pieces.shape
+
+    def kernel(core_ref, p_ref, keep_ref, send_ref):
+        for out, part in ((keep_ref, core_ref[0]), (send_ref, 1 - core_ref[0])):
+            for block in range(2):
+                for r in range(4):
+                    head = (2 * block + part) * 4 + r
+                    total = jnp.sum(p_ref[pl.ds(head * 4, 4)].astype(F32), axis=0)
+                    at = (block * 4 + r) * HEAD_DIM
+                    out[:, at : at + HEAD_DIM] = total.astype(BF16)
+
+    shape = jax.ShapeDtypeStruct((share, HEADS // 2 * HEAD_DIM), BF16)
+    return pl.pallas_call(
+        kernel,
+        out_shape=(shape, shape),
+        in_specs=[
+            pl.BlockSpec(memory_space=pltpu.SMEM),
+            pl.BlockSpec(memory_space=pltpu.VMEM),
+        ],
+        out_specs=(pl.BlockSpec(memory_space=pltpu.VMEM),) * 2,
+        name="sum_pieces",
+    )(core, pieces)
+
+
+def weight_block(place_ref, outer, inner):
+    core, x, y = place_ref[0], place_ref[1], place_ref[2]
+    first = core == 0
+    x_there = x ^ jnp.where(first, outer, inner)
+    y_there = y ^ jnp.where(first, inner, outer)
+    return x_there % 2, y_there * 2 + x_there // 2
+
+
+def project(place, keep, received, weights):
+    share, rows = keep.shape
+    _, columns, features = weights[0].shape
+
+    def kernel(place_ref, keep_ref, received_ref, w0, w1, w2, w3, own_ref, send_ref, m_ref, a_ref):
+        m_ref[0:share, :] = keep_ref[...]
+        m_ref[share:, :] = received_ref[...]
+        a_ref[...] = jnp.zeros_like(a_ref)
+        for outer, w_ref in enumerate((w0, w1, w2, w3)):
+            for inner in range(4):
+                row, column = weight_block(place_ref, outer, inner)
+                m = m_ref[:, pl.ds(pl.multiple_of(row * features, features), features)]
+                at = pl.ds(pl.multiple_of(column * columns, columns), columns)
+                a_ref[:, at] += lax.dot_general(
+                    m, w_ref[inner], NT, preferred_element_type=F32
+                )
+        own_ref[...] = a_ref[0:share, :]
+        send_ref[...] = a_ref[share:, :].astype(BF16)
+
+    return pl.pallas_call(
+        kernel,
+        out_shape=(
+            jax.ShapeDtypeStruct((share, 8 * columns), F32),
+            jax.ShapeDtypeStruct((share, 8 * columns), BF16),
+        ),
+        in_specs=[pl.BlockSpec(memory_space=pltpu.SMEM)]
+        + [pl.BlockSpec(memory_space=pltpu.VMEM)] * 6,
+        out_specs=(pl.BlockSpec(memory_space=pltpu.VMEM),) * 2,
+        scratch_shapes=[
+            pltpu.VMEM((2 * share, rows), BF16),
+            pltpu.VMEM((2 * share, 8 * columns), F32),
+        ],
+        compiler_params=pltpu.CompilerParams(vmem_limit_bytes=32 << 20),
+        name="project",
+    )(place, keep, received, *weights)
+
+
+def normalize(own, received, frozen, upstream, gain):
+    share, width = own.shape
+
+    def kernel(own_ref, received_ref, frozen_ref, upstream_ref, gain_ref, normed_ref, grad_ref):
+        hidden = own_ref[...] + received_ref[...].astype(F32) + frozen_ref[...].astype(F32)
+        gain = gain_ref[...]
+        up = upstream_ref[...].astype(F32) * gain
+        inverse = lax.rsqrt(jnp.mean(hidden * hidden, axis=-1, keepdims=True) + EPS)
+        inner = jnp.mean(up * hidden, axis=-1, keepdims=True)
+        normed_ref[...] = (hidden * inverse * gain).astype(BF16)
+        grad_ref[...] = (
+            inverse * up - hidden * (inverse * inverse * inverse) * inner
+        ).astype(BF16)
+
+    shape = jax.ShapeDtypeStruct((share, width), BF16)
+    return pl.pallas_call(
+        kernel,
+        out_shape=(shape, shape),
+        in_specs=[pl.BlockSpec(memory_space=pltpu.VMEM)] * 5,
+        out_specs=(pl.BlockSpec(memory_space=pltpu.VMEM),) * 2,
+        name="normalize",
+    )(own, received, frozen, upstream, gain)
+
+
+def project_back(place, grad, received, weights):
+    share, width = grad.shape
+    _, columns, features = weights[0].shape
+
+    def kernel(place_ref, grad_ref, received_ref, w0, w1, w2, w3, o_ref, g_ref, a_ref):
+        core = place_ref[0]
+        g_ref[pl.ds(pl.multiple_of(core * share, share), share), :] = grad_ref[...]
+        g_ref[pl.ds(pl.multiple_of((1 - core) * share, share), share), :] = received_ref[...]
+        a_ref[...] = jnp.zeros_like(a_ref)
+        for outer, w_ref in enumerate((w0, w1, w2, w3)):
+            for inner in range(4):
+                row, column = weight_block(place_ref, outer, inner)
+                g = g_ref[:, pl.ds(pl.multiple_of(column * columns, columns), columns)]
+                a_ref[row] += jnp.dot(g, w_ref[inner], preferred_element_type=F32)
+        for row in range(2):
+            o_ref[:, row * features : (row + 1) * features] = a_ref[row].astype(BF16)
+
+    return pl.pallas_call(
+        kernel,
+        out_shape=jax.ShapeDtypeStruct((2 * share, 2 * features), BF16),
+        in_specs=[pl.BlockSpec(memory_space=pltpu.SMEM)]
+        + [pl.BlockSpec(memory_space=pltpu.VMEM)] * 6,
+        out_specs=pl.BlockSpec(memory_space=pltpu.VMEM),
+        scratch_shapes=[
+            pltpu.VMEM((2 * share, width), BF16),
+            pltpu.VMEM((2, 2 * share, features), F32),
+        ],
+        compiler_params=pltpu.CompilerParams(vmem_limit_bytes=32 << 20),
+        name="project_back",
+    )(place, grad, received, *weights)
+
+
+def scatter_scaled(parts, scale):
+    _, tokens, rows = parts.shape
+    features = rows // 2
+
+    def kernel(scale_ref, p_ref, o_ref):
+        for l in range(2):
+            for k in range(2):
+                for row in range(2):
+                    at = (2 * row + k) * features
+                    part = p_ref[2 * l + k, :, row * features : (row + 1) * features]
+                    o_ref[l * tokens : (l + 1) * tokens, at : at + features] = (
+                        scale_ref[0] * part.astype(F32)
+                    ).astype(BF16)
+
+    return pl.pallas_call(
+        kernel,
+        out_shape=jax.ShapeDtypeStruct((2 * tokens, 2 * rows), BF16),
+        in_specs=[
+            pl.BlockSpec(memory_space=pltpu.SMEM),
+            pl.BlockSpec(memory_space=pltpu.VMEM),
+        ],
+        out_specs=pl.BlockSpec(memory_space=pltpu.VMEM),
+        name="scatter_scaled",
+    )(scale, parts)
+
+
 def on_device(
     q_ctl, k_ctl, v_ctl, positions, branch_ids, cond_scale, out_weight, frozen, norm_gain, cotangent
 ):
-    branch = lax.axis_index(BRANCH)
-    share = frozen.shape[0]
-    width = frozen.shape[1]
-    scale = jnp.sum(jnp.where(jnp.arange(cond_scale.shape[0]) == branch_ids[0], cond_scale, 0.0))
-
-    weight_t = lax.all_gather(out_weight.T, SEQ + BRANCH, axis=0, tiled=True)
-    weight_t = weight_t.reshape(width // out_weight.shape[1], 4, out_weight.shape[1], -1)
-    weight_t = jnp.transpose(weight_t, (0, 2, 1, 3)).reshape(width, -1)
+    branch, core = lax.axis_index(BRANCH), lax.axis_index("k")
+    z, y, x = lax.axis_index(("c", "z")), lax.axis_index("y"), lax.axis_index(("h", "l"))
+    share, _ = frozen.shape
+    features, own = out_weight.shape
+    place = jnp.stack([core, x, y]).astype(jnp.int32)
+    scale = jnp.sum(
+        jnp.where(jnp.arange(cond_scale.shape[0]) == branch_ids[0], cond_scale, 0.0)
+    ).reshape(1)
+
+    def to_partner(v):
+        return exchange(v, lambda i: i ^ 1)
+
+    w = out_weight.T
+    for stage in range(4):
+        bit = 3 - stage
+        other = exchange(w, lambda i: i ^ (32 << bit))
+        mine_high = (z >> bit) & 1 == 1
+        w = jnp.stack(
+            [jnp.where(mine_high, other, w), jnp.where(mine_high, w, other)], axis=stage
+        )
+    w = w.reshape(16 * own, features)
+    w = jnp.stack(
+        [w]
+        + [exchange(w, lambda i: i ^ (r << (3 if i % 2 == 0 else 1))) for r in range(1, 4)]
+    )
+    weights = [w] + [
+        exchange(w, lambda i: i ^ (r << (1 if i % 2 == 0 else 3))) for r in range(1, 4)
+    ]
+
+    def columns_first(v):
+        v = v.reshape(v.shape[0], 16, 8, own)
+        return jnp.transpose(v, (0, 2, 1, 3)).reshape(v.shape[0], -1)
+
+    def columns_back(v):
+        v = v.reshape(v.shape[0], 8, 16, own)
+        return jnp.transpose(v, (0, 2, 1, 3)).reshape(v.shape[0], -1)
+
+    frozen = columns_first(frozen)
+    gain = columns_first(norm_gain[None])
+    upstream = columns_first(lax.dynamic_slice_in_dim(cotangent, branch * share, share, 0))
 
     cosines, sines = rope_tables(positions)
     blocks = prepare(q_ctl[0], k_ctl[0], v_ctl[0], cosines, sines)
     blocks = lax.all_to_all(blocks, CLIP, 0, 0, tiled=True)
-    attended = attend(blocks, scale.reshape(1))
+    blocks, frozen, gain, upstream = lax.optimization_barrier((blocks, frozen, gain, upstream))
+    attended = attend(blocks, scale)
     pieces = lax.all_to_all(
         attended.reshape(HEADS * 4, share, HEAD_DIM), CLIP + BRANCH, 0, 0, tiled=True
     )
-    mixed = jnp.sum(pieces.reshape(HEADS, 4, share, HEAD_DIM).astype(F32), axis=1)
-    mixed = jnp.transpose(mixed, (1, 0, 2)).reshape(share, -1).astype(BF16)
-
-    hidden = frozen.astype(F32) + lax.dot_general(mixed, weight_t, NT, preferred_element_type=F32)
-    inverse = lax.rsqrt(jnp.mean(hidden * hidden, axis=-1, keepdims=True) + EPS)
-    normed = (hidden * inverse * norm_gain).astype(BF16)
-    upstream = lax.dynamic_slice_in_dim(cotangent, branch * share, share, 0).astype(F32) * norm_gain
-    inner = jnp.mean(upstream * hidden, axis=-1, keepdims=True)
-    grad = (inverse * upstream - hidden * (inverse * inverse * inverse) * inner).astype(BF16)
-    cot = jnp.dot(grad, weight_t, preferred_element_type=F32).astype(BF16)
-    cot = lax.all_gather(cot, BRANCH, axis=0, tiled=True)
-    grad_attn = (scale * cot.astype(F32)).astype(BF16)
-    return normed, grad_attn[None]
+    keep, send = sum_pieces(pieces, core.reshape(1))
+    own_part, send = project(place, keep, to_partner(send), weights)
+    normed, grad = normalize(own_part, to_partner(send), frozen, upstream, gain)
+    cot = project_back(place, grad, to_partner(grad), weights)
+    parts = lax.all_gather(cot, BRANCH, axis=0, tiled=False)
+    grad_attn = scatter_scaled(parts, scale)
+    return columns_back(normed), grad_attn[None]
 
 
 def solution(mesh):
     fine = Mesh(mesh.devices.reshape(8, 2, 4, 2, 2, 2), SEQ + BRANCH)
+
     return jax.shard_map(
         on_device,
         mesh=fine,

time: 290 us -> 233 us (0.80)
  waiting for transfers between devices: 193 us -> 78.7 us
  starting transfers between devices: 21.9 us -> 75.9 us
  local copies, waits for them, and re-layouts: 15.1 us -> 28.4 us
  between operations: 14.8 us -> 1.63 us
  Pallas kernels: 22.6 us -> 31.5 us
  matrix products: 6.47 us -> 0 us
    all_gather x1 -> x0, waiting for transfers between devices: 150 us -> none  [on_device(): weight_t = lax.all_gather(out_weight.T, SEQ + BRANCH, axis=0, tiled=True)]
    ppermute x0 -> x13, waiting for transfers between devices: none -> 78.7 us  [exchange(): lax.ppermute(x, SEQ + BRANCH, [(i, partner(i)) for i in range(count)])]
    ppermute x0 -> x13, starting transfers between devices: none -> 58.4 us  [exchange(): lax.ppermute(x, SEQ + BRANCH, [(i, partner(i)) for i in range(count)])]
    all_to_all x1, waiting for transfers between devices: 27.5 us -> 0.01 us  [on_device(): blocks = lax.all_to_all(blocks, CLIP, 0, 0, tiled=True)]
    pallas_call x0 -> x5, Pallas kernels: none -> 15.3 us  [the longest x1 4.43 us: project(): pl.pallas_call(kernel, out_shape=(jax.ShapeDtypeStruct((share, 8 * column...]
    all_to_all x1, waiting for transfers between devices: 14.8 us -> 0.01 us  [on_device(): lax.all_to_all(attended.reshape(HEADS * 4, share, HEAD_DIM), CLIP + BRANC...]
    reshape x1, local copies, waits for them, and re-layouts: 12 us -> 1.55 us  [columns_first(): return jnp.transpose(v, (0, 2, 1, 3)).reshape(v.shape[0], -1)]
    unnamed x7 -> x29, local copies, waits for them, and re-layouts: 3.1 us -> 11.1 us
  transfers between devices with their start and end apart: 3 -> 15, of which waited for: 3 -> 9; matrix products, arithmetic and copies ran while one was open for 1% -> 12% of each run, Pallas kernels for 8% -> 1%
where the time goes in v2:
time: 233 us; the launch traced here: 231 us
  waiting for transfers between devices  78.7 us (34%)
  starting transfers between devices  75.9 us (33%)
  Pallas kernels  31.5 us (14%)
  local copies, waits for them, and re-layouts  28.4 us (12%)
  blocking collectives  9.16 us (4%)
  other arithmetic  5.82 us (2%)
    ppermute x13, waiting for transfers between devices, exchange(): lax.ppermute(x, SEQ + BRANCH, [(i, partner(i)) for i in range(count)])  78.7 us
    ppermute x13, starting transfers between devices, exchange(): lax.ppermute(x, SEQ + BRANCH, [(i, partner(i)) for i in range(count)])  58.4 us
    pallas_call x1, Pallas kernels, attend(): pl.pallas_call(kernel, out_shape=jax.ShapeDtypeStruct((length, HEAD_DIM),...  11.7 us
    unnamed x29, local copies, waits for them, and re-layouts  11.1 us
    all_gather x1, blocking collectives, on_device(): parts = lax.all_gather(cot, BRANCH, axis=0, tiled=False)  9.16 us
    all_to_all x1, starting transfers between devices, on_device(): blocks = lax.all_to_all(blocks, CLIP, 0, 0, tiled=True)  9.06 us
    all_to_all x1, starting transfers between devices, on_device(): lax.all_to_all(attended.reshape(HEADS * 4, share, HEAD_DIM), CLIP + BRANC...  8.46 us
    transpose x3, local copies, waits for them, and re-layouts, columns_first(): return jnp.transpose(v, (0, 2, 1, 3)).reshape(v.shape[0], -1)  5.74 us
  transfers between devices with their start and end apart: 15, of which 9 were waited for; matrix products, arithmetic and copies ran while one was open for 12% of the time, Pallas kernels for 1%

profile of v2, /device:TPU:1, one launch (start us, length us, event | category | flops | bytes accessed | tf_op | source)
XLA Modules:
  0.0 231.1 jit_solution(774658015203446723)
XLA Ops:
  2.7 4.6 %prepare.1 = bf16[16,576,128]{2,1,0:T(8,128)(2,1)} custom-call(bf16[192,2048]{1,0:T(8,128)(2,1)} %bitcast.63, bf16[192,2048]{1,0:T(8,128)(2,1)} %bitcast.64, bf16[192,2048]{1,0:T(8,128)(2,1)} %bitcast.65, f32[192,128]{1,0:T(8,128)} %get-tuple-element.35.c_ref, f32[192,128]{1,0:T(8,128)} %get-tuple-element.36.s_ref), custom_call_target="tpu_custom_call" | custom-call | tf_op jit(solution)/shard_map/prepare/pallas_call | solution.py:51
  7.2 9.1 %all-to-all-start = ((bf16[16,576,128]{2,1,0:T(8,128)(2,1)}), bf16[16,576,128]{2,1,0:T(8,128)(2,1)S(1)}, u32[]{:S(2)}, u32[]{:S(2)}) async-start(bf16[16,576,128]{2,1,0:T(8,128)(2,1)} %prepare.1), calls=%async_computation | async-start | bytes 4718592 | tf_op jit(solution)/shard_map/all_to_all | solution.py:337
  16.3 14.5 %collective-permute-start.1 = (bf16[24,512]{1,0:T(8,128)(2,1)}, bf16[24,512]{1,0:T(8,128)(2,1)}, u32[]{:S(2)}, u32[]{:S(2)}) collective-permute-start(bf16[24,512]{1,0:T(8,128)(2,1)} %bitcast.71), channel_id=1, source_target_pairs={{0,256},{1,257},{2,258},{3,259},{4,260},{5,261},{6,262},{7,263},{8... | collective-permute-start | bytes 73736 | tf_op jit(solution)/shard_map/ppermute | solution.py:136
  32.3 30.4 %collective-permute-done.1 = bf16[24,512]{1,0:T(8,128)(2,1)} collective-permute-done((bf16[24,512]{1,0:T(8,128)(2,1)}, bf16[24,512]{1,0:T(8,128)(2,1)}, u32[]{:S(2)}, u32[]{:S(2)}) %collective-permute-start.1) | collective-permute-done | bytes 24608 | tf_op jit(solution)/shard_map/ppermute | solution.py:136
  64.6 3.2 %collective-permute-start.2 = (bf16[2,24,512]{2,1,0:T(8,128)(2,1)}, bf16[2,24,512]{2,1,0:T(8,128)(2,1)}, u32[]{:S(2)}, u32[]{:S(2)}) collective-permute-start(bf16[2,24,512]{2,1,0:T(8,128)(2,1)} %pad_maximum_fusion.6), channel_id=1, source_target_pairs={{0,128},{1,129},{2,130},{3,131},{4,132},{5,133},{6,134},{7,135},{8... | collective-permute-start | bytes 147464 | tf_op jit(solution)/shard_map/ppermute | solution.py:136
  68.4 2.1 copy.16
  70.5 2.1 copy.17
  78.5 2.1 copy.20
  82.1 11.7 %attend.1 = bf16[3072,128]{1,0:T(8,128)(2,1)S(1)} custom-call(f32[1]{0:T(128)} %bitcast.4.scale_ref, bf16[16,576,128]{2,1,0:T(8,128)(2,1)S(1)} %all-to-all-done.b_ref), custom_call_target="tpu_custom_call" | custom-call | tf_op jit(solution)/shard_map/attend/pallas_call | solution.py:114
  94.7 8.5 %all-to-all-start.1 = ((bf16[64,48,128]{2,1,0:T(8,128)(2,1)}), bf16[64,48,128]{2,1,0:T(8,128)(2,1)S(1)}, u32[]{:S(2)}, u32[]{:S(2)}) async-start(bf16[64,48,128]{2,1,0:T(8,128)(2,1)} %bitcast.51), calls=%async_computation.1 | async-start | bytes 1572864 | tf_op jit(solution)/shard_map/all_to_all | solution.py:340
  103.2 3.4 %collective-permute-start.3 = (bf16[2,2,24,512]{3,2,0,1:T(8,128)(2,1)S(1)}, bf16[2,2,24,512]{3,2,0,1:T(8,128)(2,1)S(1)}, u32[]{:S(2)}, u32[]{:S(2)}) collective-permute-start(bf16[2,2,24,512]{3,2,0,1:T(8,128)(2,1)S(1)} %pad_maximum_fusion.5), channel_id=1, source_target_pairs={{0,64},{1,65},{2,66},{3,67},{4,68},{5,69},{6,70},{7,71},{8,72},{9,... | collective-permute-start | bytes 294920 | tf_op jit(solution)/shard_map/ppermute | solution.py:136
  106.6 7.0 %collective-permute-done.3 = bf16[2,2,24,512]{3,2,0,1:T(8,128)(2,1)S(1)} collective-permute-done((bf16[2,2,24,512]{3,2,0,1:T(8,128)(2,1)S(1)}, bf16[2,2,24,512]{3,2,0,1:T(8,128)(2,1)S(1)}, u32[]{:S(2)}, u32[]{:S(2)}) %collective-permute-start.3) | collective-permute-done | bytes 98336 | tf_op jit(solution)/shard_map/ppermute | solution.py:136
  113.6 5.5 %collective-permute-start.4 = (bf16[2,2,2,24,512]{4,3,0,1,2:T(8,128)(2,1)S(1)}, bf16[2,2,2,24,512]{4,3,0,1,2:T(8,128)(2,1)S(1)}, u32[]{:S(2)}, u32[]{:S(2)}) collective-permute-start(bf16[2,2,2,24,512]{4,3,0,1,2:T(8,128)(2,1)S(1)} %pad_maximum_fusion.2), channel_id=1, source_target_pairs={{0,32},{1,33},{2,34},{3,35},{4,36},{5,37},{6,38},{7,39},{8,40},{9,... | collective-permute-start | bytes 589832 | tf_op jit(solution)/shard_map/ppermute | solution.py:136
  119.1 4.3 %collective-permute-done.4 = bf16[2,2,2,24,512]{4,3,0,1,2:T(8,128)(2,1)S(1)} collective-permute-done((bf16[2,2,2,24,512]{4,3,0,1,2:T(8,128)(2,1)S(1)}, bf16[2,2,2,24,512]{4,3,0,1,2:T(8,128)(2,1)S(1)}, u32[]{:S(2)}, u32[]{:S(2)}) %collective-permute-start.4) | collective-permute-done | bytes 196640 | tf_op jit(solution)/shard_map/ppermute | solution.py:136
  123.5 4.3 %collective-permute-start.7 = (bf16[384,512]{1,0:T(8,128)(2,1)S(1)}, bf16[384,512]{1,0:T(8,128)(2,1)S(1)}, u32[]{:S(2)}, u32[]{:S(2)}) collective-permute-start(bf16[384,512]{1,0:T(8,128)(2,1)S(1)} %bitcast.59), channel_id=1, source_target_pairs={{0,24},{1,7},{2,26},{3,5},{4,28},{5,3},{6,30},{7,1},{8,16},{9,15},... | collective-permute-start | bytes 1179656 | tf_op jit(solution)/shard_map/ppermute | solution.py:136
  127.9 2.5 %collective-permute-start.6 = (bf16[384,512]{1,0:T(8,128)(2,1)S(1)}, bf16[384,512]{1,0:T(8,128)(2,1)S(1)}, u32[]{:S(2)}, u32[]{:S(2)}) collective-permute-start(bf16[384,512]{1,0:T(8,128)(2,1)S(1)} %bitcast.60), channel_id=1, source_target_pairs={{0,16},{1,5},{2,18},{3,7},{4,20},{5,1},{6,22},{7,3},{8,24},{9,13},... | collective-permute-start | bytes 1179656 | tf_op jit(solution)/shard_map/ppermute | solution.py:136
  130.3 2.2 collective-permute-start.5
  132.5 4.3 %collective-permute-done.7 = bf16[384,512]{1,0:T(8,128)(2,1)S(1)} collective-permute-done((bf16[384,512]{1,0:T(8,128)(2,1)S(1)}, bf16[384,512]{1,0:T(8,128)(2,1)S(1)}, u32[]{:S(2)}, u32[]{:S(2)}) %collective-permute-start.7) | collective-permute-done | bytes 393248 | tf_op jit(solution)/shard_map/ppermute | solution.py:136
  140.5 3.1 %collective-permute-start.8 = (bf16[4,384,512]{2,1,0:T(8,128)(2,1)S(1)}, bf16[4,384,512]{2,1,0:T(8,128)(2,1)}, u32[]{:S(2)}, u32[]{:S(2)}) collective-permute-start(bf16[4,384,512]{2,1,0:T(8,128)(2,1)S(1)} %pad_maximum_fusion.w0), channel_id=1, source_target_pairs={{0,2},{1,9},{2,0},{3,11},{4,6},{5,13},{6,4},{7,15},{8,10},{9,1},{1... | collective-permute-start | bytes 4718600 | tf_op jit(solution)/shard_map/ppermute | solution.py:136
  143.7 4.4 %collective-permute-start.9 = (bf16[4,384,512]{2,1,0:T(8,128)(2,1)S(1)}, bf16[4,384,512]{2,1,0:T(8,128)(2,1)}, u32[]{:S(2)}, u32[]{:S(2)}) collective-permute-start(bf16[4,384,512]{2,1,0:T(8,128)(2,1)S(1)} %pad_maximum_fusion.w0), channel_id=1, source_target_pairs={{0,4},{1,17},{2,6},{3,19},{4,0},{5,21},{6,2},{7,23},{8,12},{9,25},... | collective-permute-start | bytes 4718600 | tf_op jit(solution)/shard_map/ppermute | solution.py:136
  153.0 5.3 %collective-permute-start = (bf16[48,1024]{1,0:T(8,128)(2,1)}, bf16[48,1024]{1,0:T(8,128)(2,1)S(1)}, u32[]{:S(2)}, u32[]{:S(2)}) collective-permute-start(bf16[48,1024]{1,0:T(8,128)(2,1)} %get-tuple-element.14), channel_id=1, source_target_pairs={{0,1},{1,0},{2,3},{3,2},{4,5},{5,4},{6,7},{7,6},{8,9},{9,8},{10,11... | collective-permute-start | bytes 294920 | tf_op jit(solution)/shard_map/ppermute | solution.py:136
  158.4 3.7 %collective-permute-done.8.w1 = bf16[4,384,512]{2,1,0:T(8,128)(2,1)} collective-permute-done((bf16[4,384,512]{2,1,0:T(8,128)(2,1)S(1)}, bf16[4,384,512]{2,1,0:T(8,128)(2,1)}, u32[]{:S(2)}, u32[]{:S(2)}) %collective-permute-start.8) | collective-permute-done | bytes 1572896 | tf_op jit(solution)/shard_map/ppermute | solution.py:136
  162.1 19.2 %collective-permute-done.9.w2 = bf16[4,384,512]{2,1,0:T(8,128)(2,1)} collective-permute-done((bf16[4,384,512]{2,1,0:T(8,128)(2,1)S(1)}, bf16[4,384,512]{2,1,0:T(8,128)(2,1)}, u32[]{:S(2)}, u32[]{:S(2)}) %collective-permute-start.9) | collective-permute-done | bytes 1572896 | tf_op jit(solution)/shard_map/ppermute | solution.py:136
  181.2 6.5 %collective-permute-done.10.w3 = bf16[4,384,512]{2,1,0:T(8,128)(2,1)} collective-permute-done((bf16[4,384,512]{2,1,0:T(8,128)(2,1)S(1)}, bf16[4,384,512]{2,1,0:T(8,128)(2,1)}, u32[]{:S(2)}, u32[]{:S(2)}) %collective-permute-start.10) | collective-permute-done | bytes 1572896 | tf_op jit(solution)/shard_map/ppermute | solution.py:136
  188.6 4.4 %project.1 = (f32[48,3072]{1,0:T(8,128)S(1)}, bf16[48,3072]{1,0:T(8,128)(2,1)S(1)}) custom-call(s32[3]{0:T(128)S(1)} %pad_add_fusion.place_ref, bf16[48,1024]{1,0:T(8,128)(2,1)S(1)} %copy-done.4, bf16[48,1024]{1,0:T(8,128)(2,1)S(1)} %collective-permute-done.received_ref, bf16[4,384,512]{2,1,0:T(8,128)(2,1)S(1)} %pad_maximum_fusion.w0, ...), custom_call_target="tpu_custom_call" | custom-call | tf_op jit(solution)/shard_map/project/pallas_call | solution.py:191
  193.9 5.9 %collective-permute-start.11 = (bf16[48,3072]{1,0:T(8,128)(2,1)S(1)}, bf16[48,3072]{1,0:T(8,128)(2,1)S(1)}, u32[]{:S(2)}, u32[]{:S(2)}) collective-permute-start(bf16[48,3072]{1,0:T(8,128)(2,1)S(1)} %get-tuple-element.16), channel_id=1, source_target_pairs={{0,1},{1,0},{2,3},{3,2},{4,5},{5,4},{6,7},{7,6},{8,9},{9,8},{10,11... | collective-permute-start | bytes 884744 | tf_op jit(solution)/shard_map/ppermute | solution.py:136
  204.6 2.5 %normalize.1 = (bf16[48,3072]{1,0:T(8,128)(2,1)}, bf16[48,3072]{1,0:T(8,128)(2,1)}) custom-call(f32[48,3072]{1,0:T(8,128)} %copy-done.2, bf16[48,3072]{1,0:T(8,128)(2,1)} %copy-done.8, bf16[48,3072]{1,0:T(8,128)(2,1)} %copy.23.frozen_ref, bf16[48,3072]{1,0:T(8,128)(2,1)} %copy.24.upstream_ref, f32[1,3072]{1,0:T(1,128)} %reshape.45.gain_ref), custom_call_target="tpu_custom_call" | custom-call | tf_op jit(solution)/shard_map/normalize/pallas_call | solution.py:224
  209.1 2.1 copy.25
  211.2 2.2 copy.26
  215.5 3.8 %project_back.1 = bf16[96,1024]{1,0:T(8,128)(2,1)S(1)} custom-call(s32[3]{0:T(128)S(1)} %pad_add_fusion.place_ref, bf16[48,3072]{1,0:T(8,128)(2,1)S(1)} %copy-done.3, bf16[48,3072]{1,0:T(8,128)(2,1)S(1)} %collective-permute-done.12.received_ref, bf16[4,384,512]{2,1,0:T(8,128)(2,1)S(1)} %pad_maximum_fusion.w0, ...), custom_call_target="tpu_custom_call" | custom-call | tf_op jit(solution)/shard_map/project_back/pallas_call | solution.py:250
  219.3 9.2 %all-gather = bf16[384,1024]{1,0:T(8,128)(2,1)} all-gather(bf16[96,1024]{1,0:T(8,128)(2,1)S(1)} %project_back.1), channel_id=2, replica_groups=mesh['c'=8,'z'=2,'y'=4,'h'=2,'l'=2,'k'=2] {'l','k'}, dimensions={0}, use_global_device_ids=true | all-gather | bytes 983040 | tf_op jit(solution)/shard_map/all_gather | solution.py:347
  228.4 2.7 %scatter_scaled.1 = bf16[192,2048]{1,0:T(8,128)(2,1)} custom-call(f32[1]{0:T(128)} %bitcast.4.scale_ref, bf16[4,96,1024]{2,1,0:T(8,128)(2,1)} %bitcast.58), custom_call_target="tpu_custom_call" | custom-call | tf_op jit(solution)/shard_map/scatter_scaled/pallas_call | solution.py:279
  (61 shorter events, 32.9 us)
Async XLA Ops:
  0.6 30.2 %copy-start = (bf16[192,3072]{1,0:T(8,128)(2,1)S(1)}, bf16[192,3072]{1,0:T(8,128)(2,1)}, u32[]{:S(2)}) copy-start(bf16[192,3072]{1,0:T(8,128)(2,1)} %param.19) | copy-start | bytes 3538948
  7.2 60.6 %copy-start.12 = (f32[64]{0:T(128)S(1)}, f32[64]{0:T(128)}, u32[]{:S(2)}) copy-start(f32[64]{0:T(128)} %param.15) | copy-start | bytes 772
  7.2 74.9 %all-to-all-start = ((bf16[16,576,128]{2,1,0:T(8,128)(2,1)}), bf16[16,576,128]{2,1,0:T(8,128)(2,1)S(1)}, u32[]{:S(2)}, u32[]{:S(2)}) async-start(bf16[16,576,128]{2,1,0:T(8,128)(2,1)} %prepare.1), calls=%async_computation | async-start | bytes 4718592 | tf_op jit(solution)/shard_map/all_to_all | solution.py:337
  16.3 46.3 %collective-permute-start.1 = (bf16[24,512]{1,0:T(8,128)(2,1)}, bf16[24,512]{1,0:T(8,128)(2,1)}, u32[]{:S(2)}, u32[]{:S(2)}) collective-permute-start(bf16[24,512]{1,0:T(8,128)(2,1)} %bitcast.71), channel_id=1, source_target_pairs={{0,256},{1,257},{2,258},{3,259},{4,260},{5,261},{6,262},{7,263},{8... | collective-permute-start | bytes 73736 | tf_op jit(solution)/shard_map/ppermute | solution.py:136
  31.6 41.1 %copy-start.11 = (f32[3072]{0:T(1024)S(1)}, f32[3072]{0:T(1024)}, u32[]{:S(2)}) copy-start(f32[3072]{0:T(1024)} %param.18) | copy-start | bytes 36868
  63.4 0.6 copy-start.9
  63.4 1.2 copy-start.10
  64.6 16.0 %collective-permute-start.2 = (bf16[2,24,512]{2,1,0:T(8,128)(2,1)}, bf16[2,24,512]{2,1,0:T(8,128)(2,1)}, u32[]{:S(2)}, u32[]{:S(2)}) collective-permute-start(bf16[2,24,512]{2,1,0:T(8,128)(2,1)} %pad_maximum_fusion.6), channel_id=1, source_target_pairs={{0,128},{1,129},{2,130},{3,131},{4,132},{5,133},{6,134},{7,135},{8... | collective-permute-start | bytes 147464 | tf_op jit(solution)/shard_map/ppermute | solution.py:136
  93.8 0.9 copy-start.1
  94.7 8.5 %copy-start.6 = (bf16[2,1,24,512]{3,2,0,1:T(8,128)(2,1)S(1)}, bf16[2,1,24,512]{3,2,0,1:T(8,128)(2,1)}, u32[]{:S(2)}) copy-start(bf16[2,1,24,512]{3,2,0,1:T(8,128)(2,1)} %get-tuple-element.28) | copy-start | bytes 147460
  94.7 8.5 %copy-start.7 = (bf16[2,1,24,512]{3,2,0,1:T(8,128)(2,1)S(1)}, bf16[2,1,24,512]{3,2,0,1:T(8,128)(2,1)}, u32[]{:S(2)}) copy-start(bf16[2,1,24,512]{3,2,0,1:T(8,128)(2,1)} %get-tuple-element.29) | copy-start | bytes 147460
  94.7 55.5 %all-to-all-start.1 = ((bf16[64,48,128]{2,1,0:T(8,128)(2,1)}), bf16[64,48,128]{2,1,0:T(8,128)(2,1)S(1)}, u32[]{:S(2)}, u32[]{:S(2)}) async-start(bf16[64,48,128]{2,1,0:T(8,128)(2,1)} %bitcast.51), calls=%async_computation.1 | async-start | bytes 1572864 | tf_op jit(solution)/shard_map/all_to_all | solution.py:340
  103.2 10.3 %collective-permute-start.3 = (bf16[2,2,24,512]{3,2,0,1:T(8,128)(2,1)S(1)}, bf16[2,2,24,512]{3,2,0,1:T(8,128)(2,1)S(1)}, u32[]{:S(2)}, u32[]{:S(2)}) collective-permute-start(bf16[2,2,24,512]{3,2,0,1:T(8,128)(2,1)S(1)} %pad_maximum_fusion.5), channel_id=1, source_target_pairs={{0,64},{1,65},{2,66},{3,67},{4,68},{5,69},{6,70},{7,71},{8,72},{9,... | collective-permute-start | bytes 294920 | tf_op jit(solution)/shard_map/ppermute | solution.py:136
  113.6 9.8 %collective-permute-start.4 = (bf16[2,2,2,24,512]{4,3,0,1,2:T(8,128)(2,1)S(1)}, bf16[2,2,2,24,512]{4,3,0,1,2:T(8,128)(2,1)S(1)}, u32[]{:S(2)}, u32[]{:S(2)}) collective-permute-start(bf16[2,2,2,24,512]{4,3,0,1,2:T(8,128)(2,1)S(1)} %pad_maximum_fusion.2), channel_id=1, source_target_pairs={{0,32},{1,33},{2,34},{3,35},{4,36},{5,37},{6,38},{7,39},{8,40},{9,... | collective-permute-start | bytes 589832 | tf_op jit(solution)/shard_map/ppermute | solution.py:136
  123.5 13.3 %collective-permute-start.7 = (bf16[384,512]{1,0:T(8,128)(2,1)S(1)}, bf16[384,512]{1,0:T(8,128)(2,1)S(1)}, u32[]{:S(2)}, u32[]{:S(2)}) collective-permute-start(bf16[384,512]{1,0:T(8,128)(2,1)S(1)} %bitcast.59), channel_id=1, source_target_pairs={{0,24},{1,7},{2,26},{3,5},{4,28},{5,3},{6,30},{7,1},{8,16},{9,15},... | collective-permute-start | bytes 1179656 | tf_op jit(solution)/shard_map/ppermute | solution.py:136
  127.9 10.3 %collective-permute-start.6 = (bf16[384,512]{1,0:T(8,128)(2,1)S(1)}, bf16[384,512]{1,0:T(8,128)(2,1)S(1)}, u32[]{:S(2)}, u32[]{:S(2)}) collective-permute-start(bf16[384,512]{1,0:T(8,128)(2,1)S(1)} %bitcast.60), channel_id=1, source_target_pairs={{0,16},{1,5},{2,18},{3,7},{4,20},{5,1},{6,22},{7,3},{8,24},{9,13},... | collective-permute-start | bytes 1179656 | tf_op jit(solution)/shard_map/ppermute | solution.py:136
  130.3 10.0 %collective-permute-start.5 = (bf16[384,512]{1,0:T(8,128)(2,1)S(1)}, bf16[384,512]{1,0:T(8,128)(2,1)S(1)}, u32[]{:S(2)}, u32[]{:S(2)}) collective-permute-start(bf16[384,512]{1,0:T(8,128)(2,1)S(1)} %bitcast.61), channel_id=1, source_target_pairs={{0,8},{1,3},{2,10},{3,1},{4,12},{5,7},{6,14},{7,5},{8,0},{9,11},{1... | collective-permute-start | bytes 1179656 | tf_op jit(solution)/shard_map/ppermute | solution.py:136
  140.5 21.6 %collective-permute-start.8 = (bf16[4,384,512]{2,1,0:T(8,128)(2,1)S(1)}, bf16[4,384,512]{2,1,0:T(8,128)(2,1)}, u32[]{:S(2)}, u32[]{:S(2)}) collective-permute-start(bf16[4,384,512]{2,1,0:T(8,128)(2,1)S(1)} %pad_maximum_fusion.w0), channel_id=1, source_target_pairs={{0,2},{1,9},{2,0},{3,11},{4,6},{5,13},{6,4},{7,15},{8,10},{9,1},{1... | collective-permute-start | bytes 4718600 | tf_op jit(solution)/shard_map/ppermute | solution.py:136
  143.7 37.6 %collective-permute-start.9 = (bf16[4,384,512]{2,1,0:T(8,128)(2,1)S(1)}, bf16[4,384,512]{2,1,0:T(8,128)(2,1)}, u32[]{:S(2)}, u32[]{:S(2)}) collective-permute-start(bf16[4,384,512]{2,1,0:T(8,128)(2,1)S(1)} %pad_maximum_fusion.w0), channel_id=1, source_target_pairs={{0,4},{1,17},{2,6},{3,19},{4,0},{5,21},{6,2},{7,23},{8,12},{9,25},... | collective-permute-start | bytes 4718600 | tf_op jit(solution)/shard_map/ppermute | solution.py:136
  148.1 39.6 %collective-permute-start.10 = (bf16[4,384,512]{2,1,0:T(8,128)(2,1)S(1)}, bf16[4,384,512]{2,1,0:T(8,128)(2,1)}, u32[]{:S(2)}, u32[]{:S(2)}) collective-permute-start(bf16[4,384,512]{2,1,0:T(8,128)(2,1)S(1)} %pad_maximum_fusion.w0), channel_id=1, source_target_pairs={{0,6},{1,25},{2,4},{3,27},{4,2},{5,29},{6,0},{7,31},{8,14},{9,17},... | collective-permute-start | bytes 4718600 | tf_op jit(solution)/shard_map/ppermute | solution.py:136
  150.2 0.9 copy-start.5
  153.0 34.7 %collective-permute-start = (bf16[48,1024]{1,0:T(8,128)(2,1)}, bf16[48,1024]{1,0:T(8,128)(2,1)S(1)}, u32[]{:S(2)}, u32[]{:S(2)}) collective-permute-start(bf16[48,1024]{1,0:T(8,128)(2,1)} %get-tuple-element.14), channel_id=1, source_target_pairs={{0,1},{1,0},{2,3},{3,2},{4,5},{5,4},{6,7},{7,6},{8,9},{9,8},{10,11... | collective-permute-start | bytes 294920 | tf_op jit(solution)/shard_map/ppermute | solution.py:136
  187.7 0.9 copy-start.4
  193.0 0.8 copy-start.2
  193.9 10.1 %collective-permute-start.11 = (bf16[48,3072]{1,0:T(8,128)(2,1)S(1)}, bf16[48,3072]{1,0:T(8,128)(2,1)S(1)}, u32[]{:S(2)}, u32[]{:S(2)}) collective-permute-start(bf16[48,3072]{1,0:T(8,128)(2,1)S(1)} %get-tuple-element.16), channel_id=1, source_target_pairs={{0,1},{1,0},{2,3},{3,2},{4,5},{5,4},{6,7},{7,6},{8,9},{9,8},{10,11... | collective-permute-start | bytes 884744 | tf_op jit(solution)/shard_map/ppermute | solution.py:136
  203.9 0.7 copy-start.8
  207.1 8.4 %collective-permute-start.12 = (bf16[48,3072]{1,0:T(8,128)(2,1)}, bf16[48,3072]{1,0:T(8,128)(2,1)S(1)}, u32[]{:S(2)}, u32[]{:S(2)}) collective-permute-start(bf16[48,3072]{1,0:T(8,128)(2,1)} %get-tuple-element.21.grad_ref), channel_id=1, source_target_pairs={{0,1},{1,0},{2,3},{3,2},{4,5},{5,4},{6,7},{7,6},{8,9},{9,8},{10,11... | collective-permute-start | bytes 884744 | tf_op jit(solution)/shard_map/ppermute | solution.py:136
  211.2 4.3 %copy-start.3 = (bf16[48,3072]{1,0:T(8,128)(2,1)S(1)}, bf16[48,3072]{1,0:T(8,128)(2,1)}, u32[]{:S(2)}) copy-start(bf16[48,3072]{1,0:T(8,128)(2,1)} %get-tuple-element.21.grad_ref) | copy-start | bytes 884740

commit v3 on v2

--- a/solution.py
+++ b/solution.py
@@ -58,17 +58,25 @@
     )(q, k, v, cosines, sines)
 
 
-def attend(blocks, scale):
+def attend(blocks, scale, part, received=None):
     sources, three_rows, _ = blocks.shape
     rows = three_rows // 3
     length = sources * rows
-    bq, kc, kt = 512, 512, 256
-    steps = length // bq
-
-    def kernel(scale_ref, b_ref, o_ref, q_ref, k_ref, v_ref, s_ref, m_ref):
+    share = rows // 4
+    queries = length // 2
+    bq, kc, kt = 384, 512, 256
+    steps = queries // bq
+
+    def kernel(part_ref, scale_ref, b_ref, *refs):
+        refs = list(refs)
+        r_ref = refs.pop(0) if received is not None else None
+        o_ref, q_ref, k_ref, v_ref, s_ref, m_ref = refs
         for j in range(sources):
             at = slice(j * rows, (j + 1) * rows)
-            q_ref[at, :] = b_ref[j, 0:rows, :]
+            for l in range(2):
+                first = pl.multiple_of((2 * l + part_ref[0]) * share, share)
+                to = (2 * j + l) * share
+                q_ref[to : to + share, :] = b_ref[j, pl.ds(first, share), :]
             k_ref[at, :] = b_ref[j, rows : 2 * rows, :]
             v_ref[at, 0:HEAD_DIM] = b_ref[j, 2 * rows :, :]
         v_ref[:, HEAD_DIM:] = jnp.ones((length, HEAD_DIM), BF16)
@@ -82,8 +90,8 @@
                 )
                 s_ref[slot, :, j * kt : (j + 1) * kt] = s
                 for half in range(kt // 128):
-                    part = s[:, half * 128 : (half + 1) * 128]
-                    top = part if top is None else jnp.maximum(top, part)
+                    piece = s[:, half * 128 : (half + 1) * 128]
+                    top = piece if top is None else jnp.maximum(top, piece)
             m_ref[slot] = jnp.broadcast_to(jnp.max(top, axis=1, keepdims=True), (bq, 128))
 
         def mix(i, slot):
@@ -91,10 +99,13 @@
             total = None
             for j in range(length // kc):
                 p = jnp.exp2(s_ref[slot, :, j * kc : (j + 1) * kc] - top).astype(BF16)
-                part = jnp.dot(p, v_ref[j * kc : (j + 1) * kc, :], preferred_element_type=F32)
-                total = part if total is None else total + part
+                piece = jnp.dot(p, v_ref[j * kc : (j + 1) * kc, :], preferred_element_type=F32)
+                total = piece if total is None else total + piece
             out = total[:, :HEAD_DIM] * (scale_ref[0] / total[:, HEAD_DIM:])
-            o_ref[pl.ds(pl.multiple_of(i * bq, bq), bq), :] = out.astype(BF16)
+            at = pl.ds(pl.multiple_of(i * bq, bq), bq)
+            if r_ref is not None:
+                out = out + r_ref[at, :].astype(F32)
+            o_ref[at, :] = out.astype(BF16)
 
         scores(0, 0)
 
@@ -111,24 +122,47 @@
         mix(steps - 2, 0)
         mix(steps - 1, 1)
 
-    return pl.pallas_call(
-        kernel,
-        out_shape=jax.ShapeDtypeStruct((length, HEAD_DIM), BF16),
-        in_specs=[
-            pl.BlockSpec(memory_space=pltpu.SMEM),
-            pl.BlockSpec(memory_space=pltpu.VMEM),
-        ],
+    extra = () if received is None else (received,)
+    return pl.pallas_call(
+        kernel,
+        out_shape=jax.ShapeDtypeStruct((queries, HEAD_DIM), BF16),
+        in_specs=[pl.BlockSpec(memory_space=pltpu.SMEM)] * 2
+        + [pl.BlockSpec(memory_space=pltpu.VMEM)] * (1 + len(extra)),
         out_specs=pl.BlockSpec(memory_space=pltpu.VMEM),
         scratch_shapes=[
-            pltpu.VMEM((length, HEAD_DIM), BF16),
+            pltpu.VMEM((queries, HEAD_DIM), BF16),
             pltpu.VMEM((length, HEAD_DIM), BF16),
             pltpu.VMEM((length, 2 * HEAD_DIM), BF16),
             pltpu.VMEM((2, bq, length), F32),
             pltpu.VMEM((2, bq, 128), F32),
         ],
-        compiler_params=pltpu.CompilerParams(vmem_limit_bytes=48 << 20),
-        name="attend",
-    )(scale, blocks)
+        compiler_params=pltpu.CompilerParams(vmem_limit_bytes=40 << 20),
+        cost_estimate=pl.CostEstimate(
+            flops=4 * queries * length * HEAD_DIM,
+            bytes_accessed=2 * blocks.size,
+            transcendentals=queries * length,
+        ),
+        name="attend_last" if extra else "attend_first",
+    )(part, scale, blocks, *extra)
+
+
+def order_along_z(w, z):
+    def kernel(z_ref, w_ref, o_ref):
+        for other in range(16):
+            d = z_ref[0] ^ other
+            at = (d & 1) * 8 + ((d >> 1) & 1) * 4 + ((d >> 2) & 1) * 2 + ((d >> 3) & 1)
+            o_ref[other] = w_ref[at]
+
+    return pl.pallas_call(
+        kernel,
+        out_shape=jax.ShapeDtypeStruct(w.shape, BF16),
+        in_specs=[
+            pl.BlockSpec(memory_space=pltpu.SMEM),
+            pl.BlockSpec(memory_space=pltpu.VMEM),
+        ],
+        out_specs=pl.BlockSpec(memory_space=pltpu.VMEM),
+        name="order_along_z",
+    )(z, w)
 
 
 def exchange(x, partner):
@@ -144,7 +178,7 @@
             for block in range(2):
                 for r in range(4):
                     head = (2 * block + part) * 4 + r
-                    total = jnp.sum(p_ref[pl.ds(head * 4, 4)].astype(F32), axis=0)
+                    total = p_ref[2 * head].astype(F32) + p_ref[2 * head + 1].astype(F32)
                     at = (block * 4 + r) * HEAD_DIM
                     out[:, at : at + HEAD_DIM] = total.astype(BF16)
 
@@ -206,19 +240,38 @@
     )(place, keep, received, *weights)
 
 
-def normalize(own, received, frozen, upstream, gain):
+def widen(frozen, upstream, gain):
+    def kernel(frozen_ref, upstream_ref, gain_ref, f_ref, u_ref):
+        f_ref[...] = frozen_ref[...].astype(F32)
+        u_ref[...] = upstream_ref[...].astype(F32) * gain_ref[...]
+
+    shape = jax.ShapeDtypeStruct(frozen.shape, F32)
+    return pl.pallas_call(
+        kernel,
+        out_shape=(shape, shape),
+        in_specs=[pl.BlockSpec(memory_space=pltpu.VMEM)] * 3,
+        out_specs=(pl.BlockSpec(memory_space=pltpu.VMEM),) * 2,
+        name="widen",
+    )(frozen, upstream, gain)
+
+
+def normalize(own, received, frozen, upstream, gain, block):
     share, width = own.shape
 
-    def kernel(own_ref, received_ref, frozen_ref, upstream_ref, gain_ref, normed_ref, grad_ref):
-        hidden = own_ref[...] + received_ref[...].astype(F32) + frozen_ref[...].astype(F32)
-        gain = gain_ref[...]
-        up = upstream_ref[...].astype(F32) * gain
+    def kernel(own_ref, received_ref, frozen_ref, up_ref, gain_ref, normed_ref, grad_ref, n_ref):
+        hidden = own_ref[...] + received_ref[...].astype(F32) + frozen_ref[...]
+        up = up_ref[...]
         inverse = lax.rsqrt(jnp.mean(hidden * hidden, axis=-1, keepdims=True) + EPS)
         inner = jnp.mean(up * hidden, axis=-1, keepdims=True)
-        normed_ref[...] = (hidden * inverse * gain).astype(BF16)
         grad_ref[...] = (
             inverse * up - hidden * (inverse * inverse * inverse) * inner
         ).astype(BF16)
+        normed = hidden * inverse * gain_ref[...]
+        for z in range(16):
+            for group in range(8):
+                to, at = (z * 8 + group) * block, (group * 16 + z) * block
+                n_ref[:, to : to + block] = normed[:, at : at + block]
+        normed_ref[...] = n_ref[...].astype(BF16)
 
     shape = jax.ShapeDtypeStruct((share, width), BF16)
     return pl.pallas_call(
@@ -226,6 +279,7 @@
         out_shape=(shape, shape),
         in_specs=[pl.BlockSpec(memory_space=pltpu.VMEM)] * 5,
         out_specs=(pl.BlockSpec(memory_space=pltpu.VMEM),) * 2,
+        scratch_shapes=[pltpu.VMEM((share, width), F32)],
         name="normalize",
     )(own, received, frozen, upstream, gain)
 
@@ -303,15 +357,10 @@
     def to_partner(v):
         return exchange(v, lambda i: i ^ 1)
 
-    w = out_weight.T
+    w = out_weight.T[None]
     for stage in range(4):
-        bit = 3 - stage
-        other = exchange(w, lambda i: i ^ (32 << bit))
-        mine_high = (z >> bit) & 1 == 1
-        w = jnp.stack(
-            [jnp.where(mine_high, other, w), jnp.where(mine_high, w, other)], axis=stage
-        )
-    w = w.reshape(16 * own, features)
+        w = jnp.concatenate([w, exchange(w, lambda i: i ^ (256 >> stage))])
+    w = order_along_z(w, z.astype(jnp.int32).reshape(1)).reshape(16 * own, features)
     w = jnp.stack(
         [w]
         + [exchange(w, lambda i: i ^ (r << (3 if i % 2 == 0 else 1))) for r in range(1, 4)]
@@ -324,29 +373,27 @@
         v = v.reshape(v.shape[0], 16, 8, own)
         return jnp.transpose(v, (0, 2, 1, 3)).reshape(v.shape[0], -1)
 
-    def columns_back(v):
-        v = v.reshape(v.shape[0], 8, 16, own)
-        return jnp.transpose(v, (0, 2, 1, 3)).reshape(v.shape[0], -1)
-
-    frozen = columns_first(frozen)
     gain = columns_first(norm_gain[None])
     upstream = columns_first(lax.dynamic_slice_in_dim(cotangent, branch * share, share, 0))
+    frozen, upstream = widen(columns_first(frozen), upstream, gain)
 
     cosines, sines = rope_tables(positions)
     blocks = prepare(q_ctl[0], k_ctl[0], v_ctl[0], cosines, sines)
     blocks = lax.all_to_all(blocks, CLIP, 0, 0, tiled=True)
-    blocks, frozen, gain, upstream = lax.optimization_barrier((blocks, frozen, gain, upstream))
-    attended = attend(blocks, scale)
+    blocks, frozen, upstream, gain = lax.optimization_barrier((blocks, frozen, upstream, gain))
+    core = core.astype(jnp.int32).reshape(1)
+    received = to_partner(attend(blocks, scale, 1 - core))
+    attended = attend(blocks, scale, core, received)
     pieces = lax.all_to_all(
-        attended.reshape(HEADS * 4, share, HEAD_DIM), CLIP + BRANCH, 0, 0, tiled=True
+        attended.reshape(HEADS * 2, share, HEAD_DIM), CLIP + ("l",), 0, 0, tiled=True
     )
-    keep, send = sum_pieces(pieces, core.reshape(1))
+    keep, send = sum_pieces(pieces, core)
     own_part, send = project(place, keep, to_partner(send), weights)
-    normed, grad = normalize(own_part, to_partner(send), frozen, upstream, gain)
+    normed, grad = normalize(own_part, to_partner(send), frozen, upstream, gain, own)
     cot = project_back(place, grad, to_partner(grad), weights)
     parts = lax.all_gather(cot, BRANCH, axis=0, tiled=False)
     grad_attn = scatter_scaled(parts, scale)
-    return columns_back(normed), grad_attn[None]
+    return normed, grad_attn[None]
 
 
 def solution(mesh):

time: 233 us -> 211 us (0.906)
  waiting for transfers between devices: 78.7 us -> 52.9 us
  Pallas kernels: 31.5 us -> 39.1 us
  starting transfers between devices: 75.9 us -> 71.9 us
    ppermute x13 -> x14, waiting for transfers between devices: 78.7 us -> 52.9 us  [exchange(): lax.ppermute(x, SEQ + BRANCH, [(i, partner(i)) for i in range(count)])]
    pallas_call x1 -> x4, Pallas kernels: 11.7 us -> 18.3 us  [the longest x2 14.4 us: attend(): pl.pallas_call(kernel, out_shape=jax.ShapeDtypeStruct((queries, HEAD_DIM)...]
    optimization_barrier x2 -> x0, local copies, waits for them, and re-layouts: 4.2 us -> none  [on_device(): lax.optimization_barrier((blocks, frozen, gain, upstream))]
    reshape x1 -> x3, local copies, waits for them, and re-layouts: 1.55 us -> 5.74 us  [columns_first(): return jnp.transpose(v, (0, 2, 1, 3)).reshape(v.shape[0], -1)]
    concatenate x0 -> x3, other arithmetic: none -> 3.02 us  [on_device(): w = jnp.concatenate([w, exchange(w, lambda i: i ^ 256 >> stage)])]
    all_to_all x1, starting transfers between devices: 8.46 us -> 5.5 us  [on_device(): lax.all_to_all(attended.reshape(HEADS * 2, share, HEAD_DIM), CLIP + ('l',...]
    another operation x8 -> x0, other arithmetic: 2.96 us -> none  [on_device(): jnp.stack([jnp.where(mine_high, other, w), jnp.where(mine_high, w, other)...]
    unnamed x29 -> x28, local copies, waits for them, and re-layouts: 11.1 us -> 13.1 us
  transfers between devices with their start and end apart: 15 -> 16, of which waited for: 9 -> 8; matrix products, arithmetic and copies ran while one was open for 12% -> 13% of each run, Pallas kernels for 1% -> 10%
where the time goes in v3:
time: 211 us; the launch traced here: 209 us
  starting transfers between devices  71.9 us (34%)
  waiting for transfers between devices  52.9 us (25%)
  Pallas kernels  39.1 us (19%)
  local copies, waits for them, and re-layouts  27.5 us (13%)
  blocking collectives  9.16 us (4%)
  other arithmetic  7.31 us (3%)
    ppermute x14, starting transfers between devices, exchange(): lax.ppermute(x, SEQ + BRANCH, [(i, partner(i)) for i in range(count)])  57.3 us
    ppermute x14, waiting for transfers between devices, exchange(): lax.ppermute(x, SEQ + BRANCH, [(i, partner(i)) for i in range(count)])  52.9 us
    pallas_call x2, Pallas kernels, attend(): pl.pallas_call(kernel, out_shape=jax.ShapeDtypeStruct((queries, HEAD_DIM)...  14.4 us
    unnamed x28, local copies, waits for them, and re-layouts  13.1 us
    all_gather x1, blocking collectives, on_device(): parts = lax.all_gather(cot, BRANCH, axis=0, tiled=False)  9.16 us
    all_to_all x1, starting transfers between devices, on_device(): blocks = lax.all_to_all(blocks, CLIP, 0, 0, tiled=True)  9.06 us
    reshape x3, local copies, waits for them, and re-layouts, columns_first(): return jnp.transpose(v, (0, 2, 1, 3)).reshape(v.shape[0], -1)  5.74 us
    transpose x3, local copies, waits for them, and re-layouts, columns_first(): return jnp.transpose(v, (0, 2, 1, 3)).reshape(v.shape[0], -1)  5.68 us
  transfers between devices with their start and end apart: 16, of which 8 were waited for; matrix products, arithmetic and copies ran while one was open for 13% of the time, Pallas kernels for 10%

profile of v3, /device:TPU:1, one launch (start us, length us, event | category | flops | bytes accessed | tf_op | source)
XLA Modules:
  0.0 209.5 jit_solution(4226006678884965794)
XLA Ops:
  2.7 4.6 %prepare.1 = bf16[16,576,128]{2,1,0:T(8,128)(2,1)} custom-call(bf16[192,2048]{1,0:T(8,128)(2,1)} %bitcast.43, bf16[192,2048]{1,0:T(8,128)(2,1)} %bitcast.44, bf16[192,2048]{1,0:T(8,128)(2,1)} %bitcast.45, f32[192,128]{1,0:T(8,128)} %get-tuple-element.29.c_ref, f32[192,128]{1,0:T(8,128)} %get-tuple-element.30.s_ref), custom_call_target="tpu_custom_call" | custom-call | tf_op jit(solution)/shard_map/prepare/pallas_call | solution.py:51
  7.3 9.1 %all-to-all-start = ((bf16[16,576,128]{2,1,0:T(8,128)(2,1)}), bf16[16,576,128]{2,1,0:T(8,128)(2,1)S(1)}, u32[]{:S(2)}, u32[]{:S(2)}) async-start(bf16[16,576,128]{2,1,0:T(8,128)(2,1)} %prepare.1), calls=%async_computation | async-start | bytes 4718592 | tf_op jit(solution)/shard_map/all_to_all | solution.py:382
  16.3 14.5 %collective-permute-start.2 = (bf16[1,24,512]{2,1,0:T(8,128)(2,1)}, bf16[1,24,512]{2,1,0:T(8,128)(2,1)}, u32[]{:S(2)}, u32[]{:S(2)}) collective-permute-start(bf16[1,24,512]{2,1,0:T(8,128)(2,1)} %bitcast.47), channel_id=1, source_target_pairs={{0,256},{1,257},{2,258},{3,259},{4,260},{5,261},{6,262},{7,263},{8... | collective-permute-start | bytes 73736 | tf_op jit(solution)/shard_map/ppermute | solution.py:170
  34.3 2.1 %copy.13 = bf16[48,3072]{0,1:T(8,128)(2,1)} copy(bf16[48,3072]{1,0:T(8,128)(2,1)} %param.17) | data formatting | bytes 589824 | tf_op args[7]
  40.6 2.1 %copy.20 = bf16[48,3072]{0,1:T(8,128)(2,1)} copy(bf16[48,3072]{1,0:T(8,128)(2,1)} %constant_dynamic-slice_fusion) | data formatting | bytes 589824
  42.7 2.1 %copy.16 = bf16[48,8,16,24]{0,3,2,1:T(8,128)(2,1)} copy(bf16[48,8,16,24]{0,3,1,2:T(8,128)(2,1)} %bitcast.35) | data formatting | bytes 589824 | tf_op jit(solution)/shard_map/transpose | solution.py:374
  50.6 2.1 %widen.1 = (f32[48,3072]{1,0:T(8,128)}, f32[48,3072]{1,0:T(8,128)}) custom-call(bf16[48,3072]{1,0:T(8,128)(2,1)} %copy.18.frozen_ref, bf16[48,3072]{1,0:T(8,128)(2,1)} %copy.19.upstream_ref, f32[1,3072]{1,0:T(1,128)} %reshape.44.gain_ref), custom_call_target="tpu_custom_call" | custom-call | tf_op jit(solution)/shard_map/widen/pallas_call | solution.py:249
  52.8 9.9 %collective-permute-done.2 = bf16[1,24,512]{2,1,0:T(8,128)(2,1)} collective-permute-done((bf16[1,24,512]{2,1,0:T(8,128)(2,1)}, bf16[1,24,512]{2,1,0:T(8,128)(2,1)}, u32[]{:S(2)}, u32[]{:S(2)}) %collective-permute-start.2) | collective-permute-done | bytes 24608 | tf_op jit(solution)/shard_map/ppermute | solution.py:170
  63.4 3.2 %collective-permute-start.3 = (bf16[2,24,512]{2,1,0:T(8,128)(2,1)S(1)}, bf16[2,24,512]{2,1,0:T(8,128)(2,1)S(1)}, u32[]{:S(2)}, u32[]{:S(2)}) collective-permute-start(bf16[2,24,512]{2,1,0:T(8,128)(2,1)S(1)} %pad_maximum_fusion.5), channel_id=1, source_target_pairs={{0,128},{1,129},{2,130},{3,131},{4,132},{5,133},{6,134},{7,135},{8... | collective-permute-start | bytes 147464 | tf_op jit(solution)/shard_map/ppermute | solution.py:170
  68.0 5.7 %collective-permute-done.3 = bf16[2,24,512]{2,1,0:T(8,128)(2,1)S(1)} collective-permute-done((bf16[2,24,512]{2,1,0:T(8,128)(2,1)S(1)}, bf16[2,24,512]{2,1,0:T(8,128)(2,1)S(1)}, u32[]{:S(2)}, u32[]{:S(2)}) %collective-permute-start.3) | collective-permute-done | bytes 49184 | tf_op jit(solution)/shard_map/ppermute | solution.py:170
  77.0 3.7 %collective-permute-done.4 = bf16[4,24,512]{2,1,0:T(8,128)(2,1)S(1)} collective-permute-done((bf16[4,24,512]{2,1,0:T(8,128)(2,1)S(1)}, bf16[4,24,512]{2,1,0:T(8,128)(2,1)S(1)}, u32[]{:S(2)}, u32[]{:S(2)}) %collective-permute-start.4) | collective-permute-done | bytes 98336 | tf_op jit(solution)/shard_map/ppermute | solution.py:170
  84.1 7.1 %attend_first.1 = bf16[1536,128]{1,0:T(8,128)(2,1)} custom-call(s32[1]{0:T(128)S(6)} %sub.3.part_ref, f32[1]{0:T(128)} %bitcast.4.scale_ref, bf16[16,576,128]{2,1,0:T(8,128)(2,1)S(1)} %all-to-all-done.b_ref), custom_call_target="tpu_custom_call" | custom-call | flops 2415919104 | bytes 2359296 | tf_op jit(solution)/shard_map/attend_first/pallas_call | solution.py:126
  91.2 6.0 %collective-permute-start = (bf16[1536,128]{1,0:T(8,128)(2,1)}, bf16[1536,128]{1,0:T(8,128)(2,1)}, u32[]{:S(2)}, u32[]{:S(2)}) collective-permute-start(bf16[1536,128]{1,0:T(8,128)(2,1)} %attend_first.1), channel_id=1, source_target_pairs={{0,1},{1,0},{2,3},{3,2},{4,5},{5,4},{6,7},{7,6},{8,9},{9,8},{10,11... | collective-permute-start | bytes 1179656 | tf_op jit(solution)/shard_map/ppermute | solution.py:170
  101.4 3.7 %collective-permute-start.8 = (bf16[384,512]{1,0:T(8,128)(2,1)}, bf16[384,512]{1,0:T(8,128)(2,1)}, u32[]{:S(2)}, u32[]{:S(2)}) collective-permute-start(bf16[384,512]{1,0:T(8,128)(2,1)} %bitcast.39), channel_id=1, source_target_pairs={{0,24},{1,7},{2,26},{3,5},{4,28},{5,3},{6,30},{7,1},{8,16},{9,15},... | collective-permute-start | bytes 1179656 | tf_op jit(solution)/shard_map/ppermute | solution.py:170
  105.1 2.5 %collective-permute-start.7 = (bf16[384,512]{1,0:T(8,128)(2,1)}, bf16[384,512]{1,0:T(8,128)(2,1)}, u32[]{:S(2)}, u32[]{:S(2)}) collective-permute-start(bf16[384,512]{1,0:T(8,128)(2,1)} %bitcast.40), channel_id=1, source_target_pairs={{0,16},{1,5},{2,18},{3,7},{4,20},{5,1},{6,22},{7,3},{8,24},{9,13},... | collective-permute-start | bytes 1179656 | tf_op jit(solution)/shard_map/ppermute | solution.py:170
  107.6 3.0 %collective-permute-start.6 = (bf16[384,512]{1,0:T(8,128)(2,1)}, bf16[384,512]{1,0:T(8,128)(2,1)}, u32[]{:S(2)}, u32[]{:S(2)}) collective-permute-start(bf16[384,512]{1,0:T(8,128)(2,1)} %bitcast.41), channel_id=1, source_target_pairs={{0,8},{1,3},{2,10},{3,1},{4,12},{5,7},{6,14},{7,5},{8,0},{9,11},{1... | collective-permute-start | bytes 1179656 | tf_op jit(solution)/shard_map/ppermute | solution.py:170
  110.6 7.3 %attend_last.1 = bf16[1536,128]{1,0:T(8,128)(2,1)S(1)} custom-call(s32[1]{0:T(128)} %bitcast.part_ref.core_ref, f32[1]{0:T(128)} %bitcast.4.scale_ref, bf16[16,576,128]{2,1,0:T(8,128)(2,1)S(1)} %all-to-all-done.b_ref, bf16[1536,128]{1,0:T(8,128)(2,1)} %collective-permute-done.refs_0_), custom_call_target="tpu_custom_call" | custom-call | flops 2415919104 | bytes 2359296 | tf_op jit(solution)/shard_map/attend_last/pallas_call | solution.py:126
  118.6 5.5 %all-to-all-start.1 = ((bf16[32,48,128]{2,1,0:T(8,128)(2,1)}), bf16[32,48,128]{2,1,0:T(8,128)(2,1)S(1)}, u32[]{:S(2)}, u32[]{:S(2)}) async-start(bf16[32,48,128]{2,1,0:T(8,128)(2,1)} %bitcast.33), calls=%async_computation.1 | async-start | bytes 786432 | tf_op jit(solution)/shard_map/all_to_all | solution.py:387
  125.7 3.1 %collective-permute-start.9 = (bf16[4,384,512]{2,1,0:T(8,128)(2,1)S(1)}, bf16[4,384,512]{2,1,0:T(8,128)(2,1)}, u32[]{:S(2)}, u32[]{:S(2)}) collective-permute-start(bf16[4,384,512]{2,1,0:T(8,128)(2,1)S(1)} %pad_maximum_fusion.w0), channel_id=1, source_target_pairs={{0,2},{1,9},{2,0},{3,11},{4,6},{5,13},{6,4},{7,15},{8,10},{9,1},{1... | collective-permute-start | bytes 4718600 | tf_op jit(solution)/shard_map/ppermute | solution.py:170
  128.9 4.3 %collective-permute-start.10 = (bf16[4,384,512]{2,1,0:T(8,128)(2,1)S(1)}, bf16[4,384,512]{2,1,0:T(8,128)(2,1)}, u32[]{:S(2)}, u32[]{:S(2)}) collective-permute-start(bf16[4,384,512]{2,1,0:T(8,128)(2,1)S(1)} %pad_maximum_fusion.w0), channel_id=1, source_target_pairs={{0,4},{1,17},{2,6},{3,19},{4,0},{5,21},{6,2},{7,23},{8,12},{9,25},... | collective-permute-start | bytes 4718600 | tf_op jit(solution)/shard_map/ppermute | solution.py:170
  133.2 2.1 %collective-permute-start.11 = (bf16[4,384,512]{2,1,0:T(8,128)(2,1)S(1)}, bf16[4,384,512]{2,1,0:T(8,128)(2,1)}, u32[]{:S(2)}, u32[]{:S(2)}) collective-permute-start(bf16[4,384,512]{2,1,0:T(8,128)(2,1)S(1)} %pad_maximum_fusion.w0), channel_id=1, source_target_pairs={{0,6},{1,25},{2,4},{3,27},{4,2},{5,29},{6,0},{7,31},{8,14},{9,17},... | collective-permute-start | bytes 4718600 | tf_op jit(solution)/shard_map/ppermute | solution.py:170
  137.8 3.9 %collective-permute-start.1 = (bf16[48,1024]{1,0:T(8,128)(2,1)}, bf16[48,1024]{1,0:T(8,128)(2,1)S(1)}, u32[]{:S(2)}, u32[]{:S(2)}) collective-permute-start(bf16[48,1024]{1,0:T(8,128)(2,1)} %get-tuple-element.18), channel_id=1, source_target_pairs={{0,1},{1,0},{2,3},{3,2},{4,5},{5,4},{6,7},{7,6},{8,9},{9,8},{10,11... | collective-permute-start | bytes 294920 | tf_op jit(solution)/shard_map/ppermute | solution.py:170
  141.8 7.3 %collective-permute-done.9.w1 = bf16[4,384,512]{2,1,0:T(8,128)(2,1)} collective-permute-done((bf16[4,384,512]{2,1,0:T(8,128)(2,1)S(1)}, bf16[4,384,512]{2,1,0:T(8,128)(2,1)}, u32[]{:S(2)}, u32[]{:S(2)}) %collective-permute-start.9) | collective-permute-done | bytes 1572896 | tf_op jit(solution)/shard_map/ppermute | solution.py:170
  149.1 18.9 %collective-permute-done.10.w2 = bf16[4,384,512]{2,1,0:T(8,128)(2,1)} collective-permute-done((bf16[4,384,512]{2,1,0:T(8,128)(2,1)S(1)}, bf16[4,384,512]{2,1,0:T(8,128)(2,1)}, u32[]{:S(2)}, u32[]{:S(2)}) %collective-permute-start.10) | collective-permute-done | bytes 1572896 | tf_op jit(solution)/shard_map/ppermute | solution.py:170
  168.0 4.8 %collective-permute-done.11.w3 = bf16[4,384,512]{2,1,0:T(8,128)(2,1)} collective-permute-done((bf16[4,384,512]{2,1,0:T(8,128)(2,1)S(1)}, bf16[4,384,512]{2,1,0:T(8,128)(2,1)}, u32[]{:S(2)}, u32[]{:S(2)}) %collective-permute-start.11) | collective-permute-done | bytes 1572896 | tf_op jit(solution)/shard_map/ppermute | solution.py:170
  173.7 4.4 %project.1 = (f32[48,3072]{1,0:T(8,128)S(1)}, bf16[48,3072]{1,0:T(8,128)(2,1)S(1)}) custom-call(s32[3]{0:T(128)S(1)} %pad_add_fusion.place_ref, bf16[48,1024]{1,0:T(8,128)(2,1)S(1)} %copy-done.4, bf16[48,1024]{1,0:T(8,128)(2,1)S(1)} %collective-permute-done.1.received_ref, bf16[4,384,512]{2,1,0:T(8,128)(2,1)S(1)} %pad_maximum_fusion.w0, ...), custom_call_target="tpu_custom_call" | custom-call | tf_op jit(solution)/shard_map/project/pallas_call | solution.py:225
  179.0 4.8 %collective-permute-start.12 = (bf16[48,3072]{1,0:T(8,128)(2,1)S(1)}, bf16[48,3072]{1,0:T(8,128)(2,1)S(1)}, u32[]{:S(2)}, u32[]{:S(2)}) collective-permute-start(bf16[48,3072]{1,0:T(8,128)(2,1)S(1)} %get-tuple-element.20), channel_id=1, source_target_pairs={{0,1},{1,0},{2,3},{3,2},{4,5},{5,4},{6,7},{7,6},{8,9},{9,8},{10,11... | collective-permute-start | bytes 884744 | tf_op jit(solution)/shard_map/ppermute | solution.py:170
  185.6 3.5 %normalize.1 = (bf16[48,3072]{1,0:T(8,128)(2,1)}, bf16[48,3072]{1,0:T(8,128)(2,1)}) custom-call(f32[48,3072]{1,0:T(8,128)} %copy-done.1, bf16[48,3072]{1,0:T(8,128)(2,1)} %copy-done.8, f32[48,3072]{1,0:T(8,128)} %get-tuple-element.21.frozen_ref, f32[48,3072]{1,0:T(8,128)} %get-tuple-element.22.up_ref, f32[1,3072]{1,0:T(1,128)} %reshape.44.gain_ref), custom_call_target="tpu_custom_call" | custom-call | tf_op jit(solution)/shard_map/normalize/pallas_call | solution.py:277
  189.1 2.3 %collective-permute-start.13 = (bf16[48,3072]{1,0:T(8,128)(2,1)}, bf16[48,3072]{1,0:T(8,128)(2,1)S(1)}, u32[]{:S(2)}, u32[]{:S(2)}) collective-permute-start(bf16[48,3072]{1,0:T(8,128)(2,1)} %get-tuple-element.25.grad_ref), channel_id=1, source_target_pairs={{0,1},{1,0},{2,3},{3,2},{4,5},{5,4},{6,7},{7,6},{8,9},{9,8},{10,11... | collective-permute-start | bytes 884744 | tf_op jit(solution)/shard_map/ppermute | solution.py:170
  193.8 3.8 %project_back.1 = bf16[96,1024]{1,0:T(8,128)(2,1)S(1)} custom-call(s32[3]{0:T(128)S(1)} %pad_add_fusion.place_ref, bf16[48,3072]{1,0:T(8,128)(2,1)S(1)} %copy-done.3, bf16[48,3072]{1,0:T(8,128)(2,1)S(1)} %collective-permute-done.13.received_ref, bf16[4,384,512]{2,1,0:T(8,128)(2,1)S(1)} %pad_maximum_fusion.w0, ...), custom_call_target="tpu_custom_call" | custom-call | tf_op jit(solution)/shard_map/project_back/pallas_call | solution.py:304
  197.5 9.2 %all-gather = bf16[384,1024]{1,0:T(8,128)(2,1)} all-gather(bf16[96,1024]{1,0:T(8,128)(2,1)S(1)} %project_back.1), channel_id=2, replica_groups=mesh['c'=8,'z'=2,'y'=4,'h'=2,'l'=2,'k'=2] {'l','k'}, dimensions={0}, use_global_device_ids=true | all-gather | bytes 983040 | tf_op jit(solution)/shard_map/all_gather | solution.py:394
  206.7 2.8 %scatter_scaled.1 = bf16[192,2048]{1,0:T(8,128)(2,1)} custom-call(f32[1]{0:T(128)} %bitcast.4.scale_ref, bf16[4,96,1024]{2,1,0:T(8,128)(2,1)} %bitcast.38), custom_call_target="tpu_custom_call" | custom-call | tf_op jit(solution)/shard_map/scatter_scaled/pallas_call | solution.py:333
  (58 shorter events, 38.4 us)
Async XLA Ops:
  0.6 32.3 %copy-start = (bf16[192,3072]{1,0:T(8,128)(2,1)S(1)}, bf16[192,3072]{1,0:T(8,128)(2,1)}, u32[]{:S(2)}) copy-start(bf16[192,3072]{1,0:T(8,128)(2,1)} %param.19) | copy-start | bytes 3538948
  7.3 26.4 %copy-start.10 = (f32[64]{0:T(128)S(1)}, f32[64]{0:T(128)}, u32[]{:S(2)}) copy-start(f32[64]{0:T(128)} %param.15) | copy-start | bytes 772
  7.3 76.9 %all-to-all-start = ((bf16[16,576,128]{2,1,0:T(8,128)(2,1)}), bf16[16,576,128]{2,1,0:T(8,128)(2,1)S(1)}, u32[]{:S(2)}, u32[]{:S(2)}) async-start(bf16[16,576,128]{2,1,0:T(8,128)(2,1)} %prepare.1), calls=%async_computation | async-start | bytes 4718592 | tf_op jit(solution)/shard_map/all_to_all | solution.py:382
  16.3 46.3 %collective-permute-start.2 = (bf16[1,24,512]{2,1,0:T(8,128)(2,1)}, bf16[1,24,512]{2,1,0:T(8,128)(2,1)}, u32[]{:S(2)}, u32[]{:S(2)}) collective-permute-start(bf16[1,24,512]{2,1,0:T(8,128)(2,1)} %bitcast.47), channel_id=1, source_target_pairs={{0,256},{1,257},{2,258},{3,259},{4,260},{5,261},{6,262},{7,263},{8... | collective-permute-start | bytes 73736 | tf_op jit(solution)/shard_map/ppermute | solution.py:170
  42.7 4.2 %copy-start.9 = (f32[3072]{0:T(1024)S(1)}, f32[3072]{0:T(1024)}, u32[]{:S(2)}) copy-start(f32[3072]{0:T(1024)} %param.18) | copy-start | bytes 36868
  63.4 10.2 %collective-permute-start.3 = (bf16[2,24,512]{2,1,0:T(8,128)(2,1)S(1)}, bf16[2,24,512]{2,1,0:T(8,128)(2,1)S(1)}, u32[]{:S(2)}, u32[]{:S(2)}) collective-permute-start(bf16[2,24,512]{2,1,0:T(8,128)(2,1)S(1)} %pad_maximum_fusion.5), channel_id=1, source_target_pairs={{0,128},{1,129},{2,130},{3,131},{4,132},{5,133},{6,134},{7,135},{8... | collective-permute-start | bytes 147464 | tf_op jit(solution)/shard_map/ppermute | solution.py:170
  74.4 6.3 %collective-permute-start.4 = (bf16[4,24,512]{2,1,0:T(8,128)(2,1)S(1)}, bf16[4,24,512]{2,1,0:T(8,128)(2,1)S(1)}, u32[]{:S(2)}, u32[]{:S(2)}) collective-permute-start(bf16[4,24,512]{2,1,0:T(8,128)(2,1)S(1)} %pad_maximum_fusion.4), channel_id=1, source_target_pairs={{0,64},{1,65},{2,66},{3,67},{4,68},{5,69},{6,70},{7,71},{8,72},{9,... | collective-permute-start | bytes 294920 | tf_op jit(solution)/shard_map/ppermute | solution.py:170
  80.7 1.5 copy-start.6
  82.2 15.7 %collective-permute-start.5 = (bf16[8,24,512]{2,1,0:T(8,128)(2,1)}, bf16[8,24,512]{2,1,0:T(8,128)(2,1)}, u32[]{:S(2)}, u32[]{:S(2)}) collective-permute-start(bf16[8,24,512]{2,1,0:T(8,128)(2,1)} %pad_maximum_fusion.1), channel_id=1, source_target_pairs={{0,32},{1,33},{2,34},{3,35},{4,36},{5,37},{6,38},{7,39},{8,40},{9,... | collective-permute-start | bytes 589832 | tf_op jit(solution)/shard_map/ppermute | solution.py:170
  84.1 13.1 %copy-start.7 = (bf16[4,24,512]{2,1,0:T(8,128)(2,1)S(1)}, bf16[4,24,512]{2,1,0:T(8,128)(2,1)}, u32[]{:S(2)}) copy-start(bf16[4,24,512]{2,1,0:T(8,128)(2,1)} %copy-done.6) | copy-start | bytes 294916
  91.2 19.3 %collective-permute-start = (bf16[1536,128]{1,0:T(8,128)(2,1)}, bf16[1536,128]{1,0:T(8,128)(2,1)}, u32[]{:S(2)}, u32[]{:S(2)}) collective-permute-start(bf16[1536,128]{1,0:T(8,128)(2,1)} %attend_first.1), channel_id=1, source_target_pairs={{0,1},{1,0},{2,3},{3,2},{4,5},{5,4},{6,7},{7,6},{8,9},{9,8},{10,11... | collective-permute-start | bytes 1179656 | tf_op jit(solution)/shard_map/ppermute | solution.py:170
  101.4 22.8 %collective-permute-start.8 = (bf16[384,512]{1,0:T(8,128)(2,1)}, bf16[384,512]{1,0:T(8,128)(2,1)}, u32[]{:S(2)}, u32[]{:S(2)}) collective-permute-start(bf16[384,512]{1,0:T(8,128)(2,1)} %bitcast.39), channel_id=1, source_target_pairs={{0,24},{1,7},{2,26},{3,5},{4,28},{5,3},{6,30},{7,1},{8,16},{9,15},... | collective-permute-start | bytes 1179656 | tf_op jit(solution)/shard_map/ppermute | solution.py:170
  105.1 19.0 %collective-permute-start.7 = (bf16[384,512]{1,0:T(8,128)(2,1)}, bf16[384,512]{1,0:T(8,128)(2,1)}, u32[]{:S(2)}, u32[]{:S(2)}) collective-permute-start(bf16[384,512]{1,0:T(8,128)(2,1)} %bitcast.40), channel_id=1, source_target_pairs={{0,16},{1,5},{2,18},{3,7},{4,20},{5,1},{6,22},{7,3},{8,24},{9,13},... | collective-permute-start | bytes 1179656 | tf_op jit(solution)/shard_map/ppermute | solution.py:170
  107.6 16.6 %collective-permute-start.6 = (bf16[384,512]{1,0:T(8,128)(2,1)}, bf16[384,512]{1,0:T(8,128)(2,1)}, u32[]{:S(2)}, u32[]{:S(2)}) collective-permute-start(bf16[384,512]{1,0:T(8,128)(2,1)} %bitcast.41), channel_id=1, source_target_pairs={{0,8},{1,3},{2,10},{3,1},{4,12},{5,7},{6,14},{7,5},{8,0},{9,11},{1... | collective-permute-start | bytes 1179656 | tf_op jit(solution)/shard_map/ppermute | solution.py:170
  117.9 0.7 copy-start.2
  118.6 16.7 %all-to-all-start.1 = ((bf16[32,48,128]{2,1,0:T(8,128)(2,1)}), bf16[32,48,128]{2,1,0:T(8,128)(2,1)S(1)}, u32[]{:S(2)}, u32[]{:S(2)}) async-start(bf16[32,48,128]{2,1,0:T(8,128)(2,1)} %bitcast.33), calls=%async_computation.1 | async-start | bytes 786432 | tf_op jit(solution)/shard_map/all_to_all | solution.py:387
  125.7 23.4 %collective-permute-start.9 = (bf16[4,384,512]{2,1,0:T(8,128)(2,1)S(1)}, bf16[4,384,512]{2,1,0:T(8,128)(2,1)}, u32[]{:S(2)}, u32[]{:S(2)}) collective-permute-start(bf16[4,384,512]{2,1,0:T(8,128)(2,1)S(1)} %pad_maximum_fusion.w0), channel_id=1, source_target_pairs={{0,2},{1,9},{2,0},{3,11},{4,6},{5,13},{6,4},{7,15},{8,10},{9,1},{1... | collective-permute-start | bytes 4718600 | tf_op jit(solution)/shard_map/ppermute | solution.py:170
  128.9 39.2 %collective-permute-start.10 = (bf16[4,384,512]{2,1,0:T(8,128)(2,1)S(1)}, bf16[4,384,512]{2,1,0:T(8,128)(2,1)}, u32[]{:S(2)}, u32[]{:S(2)}) collective-permute-start(bf16[4,384,512]{2,1,0:T(8,128)(2,1)S(1)} %pad_maximum_fusion.w0), channel_id=1, source_target_pairs={{0,4},{1,17},{2,6},{3,19},{4,0},{5,21},{6,2},{7,23},{8,12},{9,25},... | collective-permute-start | bytes 4718600 | tf_op jit(solution)/shard_map/ppermute | solution.py:170
  133.2 39.6 %collective-permute-start.11 = (bf16[4,384,512]{2,1,0:T(8,128)(2,1)S(1)}, bf16[4,384,512]{2,1,0:T(8,128)(2,1)}, u32[]{:S(2)}, u32[]{:S(2)}) collective-permute-start(bf16[4,384,512]{2,1,0:T(8,128)(2,1)S(1)} %pad_maximum_fusion.w0), channel_id=1, source_target_pairs={{0,6},{1,25},{2,4},{3,27},{4,2},{5,29},{6,0},{7,31},{8,14},{9,17},... | collective-permute-start | bytes 4718600 | tf_op jit(solution)/shard_map/ppermute | solution.py:170
  135.3 0.7 copy-start.5
  137.8 35.0 %collective-permute-start.1 = (bf16[48,1024]{1,0:T(8,128)(2,1)}, bf16[48,1024]{1,0:T(8,128)(2,1)S(1)}, u32[]{:S(2)}, u32[]{:S(2)}) collective-permute-start(bf16[48,1024]{1,0:T(8,128)(2,1)} %get-tuple-element.18), channel_id=1, source_target_pairs={{0,1},{1,0},{2,3},{3,2},{4,5},{5,4},{6,7},{7,6},{8,9},{9,8},{10,11... | collective-permute-start | bytes 294920 | tf_op jit(solution)/shard_map/ppermute | solution.py:170
  172.8 0.9 copy-start.4
  178.1 0.8 copy-start.1
  179.0 6.0 %collective-permute-start.12 = (bf16[48,3072]{1,0:T(8,128)(2,1)S(1)}, bf16[48,3072]{1,0:T(8,128)(2,1)S(1)}, u32[]{:S(2)}, u32[]{:S(2)}) collective-permute-start(bf16[48,3072]{1,0:T(8,128)(2,1)S(1)} %get-tuple-element.20), channel_id=1, source_target_pairs={{0,1},{1,0},{2,3},{3,2},{4,5},{5,4},{6,7},{7,6},{8,9},{9,8},{10,11... | collective-permute-start | bytes 884744 | tf_op jit(solution)/shard_map/ppermute | solution.py:170
  184.9 0.7 copy-start.8
  189.1 3.7 %collective-permute-start.13 = (bf16[48,3072]{1,0:T(8,128)(2,1)}, bf16[48,3072]{1,0:T(8,128)(2,1)S(1)}, u32[]{:S(2)}, u32[]{:S(2)}) collective-permute-start(bf16[48,3072]{1,0:T(8,128)(2,1)} %get-tuple-element.25.grad_ref), channel_id=1, source_target_pairs={{0,1},{1,0},{2,3},{3,2},{4,5},{5,4},{6,7},{7,6},{8,9},{9,8},{10,11... | collective-permute-start | bytes 884744 | tf_op jit(solution)/shard_map/ppermute | solution.py:170
  192.8 1.0 copy-start.3

commit v4 on v3

--- a/solution.py
+++ b/solution.py
@@ -146,12 +146,13 @@
     )(part, scale, blocks, *extra)
 
 
-def order_along_z(w, z):
-    def kernel(z_ref, w_ref, o_ref):
-        for other in range(16):
-            d = z_ref[0] ^ other
-            at = (d & 1) * 8 + ((d >> 1) & 1) * 4 + ((d >> 2) & 1) * 2 + ((d >> 3) & 1)
-            o_ref[other] = w_ref[at]
+def order_along_z(w, place):
+    def kernel(place_ref, w_ref, o_ref):
+        c, z = place_ref[0], place_ref[1]
+        for there in range(16):
+            d = (there // 2 - c) * (1 - 2 * z) & 7
+            at = (d & 1) * 8 + ((d >> 1) & 1) * 4 + ((d >> 2) & 1) * 2 + ((there & 1) ^ z)
+            o_ref[there] = w_ref[at]
 
     return pl.pallas_call(
         kernel,
@@ -162,7 +163,7 @@
         ],
         out_specs=pl.BlockSpec(memory_space=pltpu.VMEM),
         name="order_along_z",
-    )(z, w)
+    )(place, w)
 
 
 def exchange(x, partner):
@@ -185,12 +186,13 @@
     shape = jax.ShapeDtypeStruct((share, HEADS // 2 * HEAD_DIM), BF16)
     return pl.pallas_call(
         kernel,
+        grid=(1,),
         out_shape=(shape, shape),
         in_specs=[
             pl.BlockSpec(memory_space=pltpu.SMEM),
-            pl.BlockSpec(memory_space=pltpu.VMEM),
-        ],
-        out_specs=(pl.BlockSpec(memory_space=pltpu.VMEM),) * 2,
+            whole(pieces),
+        ],
+        out_specs=(whole(shape),) * 2,
         name="sum_pieces",
     )(core, pieces)
 
@@ -203,39 +205,48 @@
     return x_there % 2, y_there * 2 + x_there // 2
 
 
+def whole(x):
+    return pl.BlockSpec(x.shape, lambda *_: (0,) * len(x.shape))
+
+
 def project(place, keep, received, weights):
     share, rows = keep.shape
-    _, columns, features = weights[0].shape
+    pieces, columns, features = weights[0].shape
+    own = jax.ShapeDtypeStruct((share, 8 * columns), F32)
+    send = jax.ShapeDtypeStruct((share, 8 * columns), BF16)
 
     def kernel(place_ref, keep_ref, received_ref, w0, w1, w2, w3, own_ref, send_ref, m_ref, a_ref):
-        m_ref[0:share, :] = keep_ref[...]
-        m_ref[share:, :] = received_ref[...]
-        a_ref[...] = jnp.zeros_like(a_ref)
+        inner = pl.program_id(0)
+
+        @pl.when(inner == 0)
+        def _():
+            m_ref[0:share, :] = keep_ref[...]
+            m_ref[share:, :] = received_ref[...]
+            a_ref[...] = jnp.zeros_like(a_ref)
+
         for outer, w_ref in enumerate((w0, w1, w2, w3)):
-            for inner in range(4):
-                row, column = weight_block(place_ref, outer, inner)
-                m = m_ref[:, pl.ds(pl.multiple_of(row * features, features), features)]
-                at = pl.ds(pl.multiple_of(column * columns, columns), columns)
-                a_ref[:, at] += lax.dot_general(
-                    m, w_ref[inner], NT, preferred_element_type=F32
-                )
-        own_ref[...] = a_ref[0:share, :]
-        send_ref[...] = a_ref[share:, :].astype(BF16)
-
-    return pl.pallas_call(
-        kernel,
-        out_shape=(
-            jax.ShapeDtypeStruct((share, 8 * columns), F32),
-            jax.ShapeDtypeStruct((share, 8 * columns), BF16),
-        ),
-        in_specs=[pl.BlockSpec(memory_space=pltpu.SMEM)]
-        + [pl.BlockSpec(memory_space=pltpu.VMEM)] * 6,
-        out_specs=(pl.BlockSpec(memory_space=pltpu.VMEM),) * 2,
+            row, column = weight_block(place_ref, outer, inner)
+            m = m_ref[:, pl.ds(pl.multiple_of(row * features, features), features)]
+            at = pl.ds(pl.multiple_of(column * columns, columns), columns)
+            a_ref[:, at] += lax.dot_general(m, w_ref[0], NT, preferred_element_type=F32)
+
+        @pl.when(inner == pieces - 1)
+        def _():
+            own_ref[...] = a_ref[0:share, :]
+            send_ref[...] = a_ref[share:, :].astype(BF16)
+
+    piece = pl.BlockSpec((1, columns, features), lambda i: (i, 0, 0))
+    return pl.pallas_call(
+        kernel,
+        out_shape=(own, send),
+        grid=(pieces,),
+        in_specs=[pl.BlockSpec(memory_space=pltpu.SMEM), whole(keep), whole(received)]
+        + [piece] * 4,
+        out_specs=(whole(own), whole(send)),
         scratch_shapes=[
             pltpu.VMEM((2 * share, rows), BF16),
             pltpu.VMEM((2 * share, 8 * columns), F32),
         ],
-        compiler_params=pltpu.CompilerParams(vmem_limit_bytes=32 << 20),
         name="project",
     )(place, keep, received, *weights)
 
@@ -277,8 +288,9 @@
     return pl.pallas_call(
         kernel,
         out_shape=(shape, shape),
-        in_specs=[pl.BlockSpec(memory_space=pltpu.VMEM)] * 5,
-        out_specs=(pl.BlockSpec(memory_space=pltpu.VMEM),) * 2,
+        grid=(1,),
+        in_specs=[whole(v) for v in (own, received, frozen, upstream, gain)],
+        out_specs=(whole(shape),) * 2,
         scratch_shapes=[pltpu.VMEM((share, width), F32)],
         name="normalize",
     )(own, received, frozen, upstream, gain)
@@ -286,32 +298,40 @@
 
 def project_back(place, grad, received, weights):
     share, width = grad.shape
-    _, columns, features = weights[0].shape
+    pieces, columns, features = weights[0].shape
+    out = jax.ShapeDtypeStruct((2 * share, 2 * features), BF16)
 
     def kernel(place_ref, grad_ref, received_ref, w0, w1, w2, w3, o_ref, g_ref, a_ref):
-        core = place_ref[0]
-        g_ref[pl.ds(pl.multiple_of(core * share, share), share), :] = grad_ref[...]
-        g_ref[pl.ds(pl.multiple_of((1 - core) * share, share), share), :] = received_ref[...]
-        a_ref[...] = jnp.zeros_like(a_ref)
+        inner, core = pl.program_id(0), place_ref[0]
+
+        @pl.when(inner == 0)
+        def _():
+            g_ref[pl.ds(pl.multiple_of(core * share, share), share), :] = grad_ref[...]
+            g_ref[pl.ds(pl.multiple_of((1 - core) * share, share), share), :] = received_ref[...]
+            a_ref[...] = jnp.zeros_like(a_ref)
+
         for outer, w_ref in enumerate((w0, w1, w2, w3)):
-            for inner in range(4):
-                row, column = weight_block(place_ref, outer, inner)
-                g = g_ref[:, pl.ds(pl.multiple_of(column * columns, columns), columns)]
-                a_ref[row] += jnp.dot(g, w_ref[inner], preferred_element_type=F32)
-        for row in range(2):
-            o_ref[:, row * features : (row + 1) * features] = a_ref[row].astype(BF16)
-
-    return pl.pallas_call(
-        kernel,
-        out_shape=jax.ShapeDtypeStruct((2 * share, 2 * features), BF16),
-        in_specs=[pl.BlockSpec(memory_space=pltpu.SMEM)]
-        + [pl.BlockSpec(memory_space=pltpu.VMEM)] * 6,
-        out_specs=pl.BlockSpec(memory_space=pltpu.VMEM),
+            row, column = weight_block(place_ref, outer, inner)
+            g = g_ref[:, pl.ds(pl.multiple_of(column * columns, columns), columns)]
+            a_ref[row] += jnp.dot(g, w_ref[0], preferred_element_type=F32)
+
+        @pl.when(inner == pieces - 1)
+        def _():
+            for row in range(2):
+                o_ref[:, row * features : (row + 1) * features] = a_ref[row].astype(BF16)
+
+    piece = pl.BlockSpec((1, columns, features), lambda i: (i, 0, 0))
+    return pl.pallas_call(
+        kernel,
+        out_shape=out,
+        grid=(pieces,),
+        in_specs=[pl.BlockSpec(memory_space=pltpu.SMEM), whole(grad), whole(received)]
+        + [piece] * 4,
+        out_specs=whole(out),
         scratch_shapes=[
             pltpu.VMEM((2 * share, width), BF16),
             pltpu.VMEM((2, 2 * share, features), F32),
         ],
-        compiler_params=pltpu.CompilerParams(vmem_limit_bytes=32 << 20),
         name="project_back",
     )(place, grad, received, *weights)
 
@@ -321,23 +341,21 @@
     features = rows // 2
 
     def kernel(scale_ref, p_ref, o_ref):
-        for l in range(2):
-            for k in range(2):
-                for row in range(2):
-                    at = (2 * row + k) * features
-                    part = p_ref[2 * l + k, :, row * features : (row + 1) * features]
-                    o_ref[l * tokens : (l + 1) * tokens, at : at + features] = (
-                        scale_ref[0] * part.astype(F32)
-                    ).astype(BF16)
+        for k in range(2):
+            for row in range(2):
+                at = (2 * row + k) * features
+                part = p_ref[k, :, row * features : (row + 1) * features]
+                o_ref[:, at : at + features] = (scale_ref[0] * part.astype(F32)).astype(BF16)
 
     return pl.pallas_call(
         kernel,
         out_shape=jax.ShapeDtypeStruct((2 * tokens, 2 * rows), BF16),
+        grid=(2,),
         in_specs=[
             pl.BlockSpec(memory_space=pltpu.SMEM),
-            pl.BlockSpec(memory_space=pltpu.VMEM),
-        ],
-        out_specs=pl.BlockSpec(memory_space=pltpu.VMEM),
+            pl.BlockSpec((2, tokens, rows), lambda l: (l, 0, 0)),
+        ],
+        out_specs=pl.BlockSpec((tokens, 2 * rows), lambda l: (l, 0)),
         name="scatter_scaled",
     )(scale, parts)
 
@@ -346,7 +364,8 @@
     q_ctl, k_ctl, v_ctl, positions, branch_ids, cond_scale, out_weight, frozen, norm_gain, cotangent
 ):
     branch, core = lax.axis_index(BRANCH), lax.axis_index("k")
-    z, y, x = lax.axis_index(("c", "z")), lax.axis_index("y"), lax.axis_index(("h", "l"))
+    clip, z = lax.axis_index("c"), lax.axis_index("z")
+    y, x = lax.axis_index("y"), lax.axis_index(("h", "l"))
     share, _ = frozen.shape
     features, own = out_weight.shape
     place = jnp.stack([core, x, y]).astype(jnp.int32)
@@ -358,13 +377,20 @@
         return exchange(v, lambda i: i ^ 1)
 
     w = out_weight.T[None]
-    for stage in range(4):
-        w = jnp.concatenate([w, exchange(w, lambda i: i ^ (256 >> stage))])
-    w = order_along_z(w, z.astype(jnp.int32).reshape(1)).reshape(16 * own, features)
-    w = jnp.stack(
-        [w]
-        + [exchange(w, lambda i: i ^ (r << (3 if i % 2 == 0 else 1))) for r in range(1, 4)]
-    )
+    w = jnp.concatenate([w, exchange(w, lambda i: i ^ 32)])
+
+    def away(step):
+        return lambda i: (i + (step if i & 32 else -step) * 64) % 512
+
+    cosines, sines = rope_tables(positions)
+    blocks = prepare(q_ctl[0], k_ctl[0], v_ctl[0], cosines, sines)
+    w, blocks = lax.optimization_barrier((w, blocks))
+    blocks = lax.all_to_all(blocks, CLIP, 0, 0, tiled=True)
+    for step in (4, 2, 1):
+        w = jnp.concatenate([w, exchange(w, away(step))])
+    w = order_along_z(w, jnp.stack([clip, z]).astype(jnp.int32)).reshape(16 * own, features)
+    arrived = [exchange(w, lambda i: i ^ (r << (3 if i % 2 == 0 else 1))) for r in range(1, 4)]
+    w = jnp.stack([w] + arrived)
     weights = [w] + [
         exchange(w, lambda i: i ^ (r << (1 if i % 2 == 0 else 3))) for r in range(1, 4)
     ]
@@ -377,9 +403,6 @@
     upstream = columns_first(lax.dynamic_slice_in_dim(cotangent, branch * share, share, 0))
     frozen, upstream = widen(columns_first(frozen), upstream, gain)
 
-    cosines, sines = rope_tables(positions)
-    blocks = prepare(q_ctl[0], k_ctl[0], v_ctl[0], cosines, sines)
-    blocks = lax.all_to_all(blocks, CLIP, 0, 0, tiled=True)
     blocks, frozen, upstream, gain = lax.optimization_barrier((blocks, frozen, upstream, gain))
     core = core.astype(jnp.int32).reshape(1)
     received = to_partner(attend(blocks, scale, 1 - core))

time: 211 us -> 206 us (0.976)
  local copies, waits for them, and re-layouts: 27.5 us -> 20.7 us
  waiting for transfers between devices: 52.9 us -> 49 us
  Pallas kernels: 39.1 us -> 41.9 us
  other arithmetic: 7.31 us -> 10.1 us
  starting transfers between devices: 71.9 us -> 69.6 us
    unnamed x28, local copies, waits for them, and re-layouts: 13.1 us -> 7.83 us
    ppermute x14, waiting for transfers between devices: 52.9 us -> 49 us  [exchange(): lax.ppermute(x, SEQ + BRANCH, [(i, partner(i)) for i in range(count)])]
    pallas_call x4, Pallas kernels: 13.4 us -> 16.4 us  [the longest x1 5.95 us: project(): pl.pallas_call(kernel, out_shape=(own, send), grid=(pieces,), in_specs=[p...]
    all_to_all x1, starting transfers between devices: 9.06 us -> 6.89 us  [on_device(): blocks = lax.all_to_all(blocks, CLIP, 0, 0, tiled=True)]
    concatenate x3 -> x4, other arithmetic: 3.02 us -> 4.77 us  [the longest x3 4.14 us: on_device(): w = jnp.concatenate([w, exchange(w, away(step))])]
  transfers between devices with their start and end apart: 16 -> 16, of which waited for: 8 -> 6; matrix products, arithmetic and copies ran while one was open for 13% -> 13% of each run, Pallas kernels for 10% -> 12%
where the time goes in v4:
time: 206 us; the launch traced here: 204 us
  starting transfers between devices  69.6 us (34%)
  waiting for transfers between devices  49 us (24%)
  Pallas kernels  41.9 us (20%)
  local copies, waits for them, and re-layouts  20.7 us (10%)
  blocking collectives  11 us (5%)
  other arithmetic  10.1 us (5%)
    ppermute x14, starting transfers between devices, exchange(): lax.ppermute(x, SEQ + BRANCH, [(i, partner(i)) for i in range(count)])  58.8 us
    ppermute x14, waiting for transfers between devices, exchange(): lax.ppermute(x, SEQ + BRANCH, [(i, partner(i)) for i in range(count)])  49 us
    pallas_call x2, Pallas kernels, attend(): pl.pallas_call(kernel, out_shape=jax.ShapeDtypeStruct((queries, HEAD_DIM)...  14.4 us
    all_gather x1, blocking collectives, on_device(): parts = lax.all_gather(cot, BRANCH, axis=0, tiled=False)  11 us
    unnamed x28, local copies, waits for them, and re-layouts  7.83 us
    all_to_all x1, starting transfers between devices, on_device(): blocks = lax.all_to_all(blocks, CLIP, 0, 0, tiled=True)  6.89 us
    pallas_call x1, Pallas kernels, project(): pl.pallas_call(kernel, out_shape=(own, send), grid=(pieces,), in_specs=[p...  5.95 us
    reshape x3, local copies, waits for them, and re-layouts, columns_first(): return jnp.transpose(v, (0, 2, 1, 3)).reshape(v.shape[0], -1)  5.74 us
  transfers between devices with their start and end apart: 16, of which 6 were waited for; matrix products, arithmetic and copies ran while one was open for 13% of the time, Pallas kernels for 12%

profile of v4, /device:TPU:1, one launch (start us, length us, event | category | flops | bytes accessed | tf_op | source)
XLA Modules:
  0.0 203.9 jit_solution(5359040812460078234)
XLA Ops:
  0.6 4.5 %collective-permute-start = (bf16[1,24,512]{2,1,0:T(8,128)(2,1)}, bf16[1,24,512]{2,1,0:T(8,128)(2,1)S(1)}, u32[]{:S(2)}, u32[]{:S(2)}) collective-permute-start(bf16[1,24,512]{2,1,0:T(8,128)(2,1)} %bitcast.48), channel_id=1, source_target_pairs={{0,32},{1,33},{2,34},{3,35},{4,36},{5,37},{6,38},{7,39},{8,40},{9,... | collective-permute-start | bytes 73736 | tf_op jit(solution)/shard_map/ppermute | solution.py:171
  7.1 4.6 %prepare.1 = bf16[16,576,128]{2,1,0:T(8,128)(2,1)} custom-call(bf16[192,2048]{1,0:T(8,128)(2,1)} %bitcast.43, bf16[192,2048]{1,0:T(8,128)(2,1)} %bitcast.44, bf16[192,2048]{1,0:T(8,128)(2,1)} %bitcast.45, f32[192,128]{1,0:T(8,128)} %get-tuple-element.33.c_ref, f32[192,128]{1,0:T(8,128)} %get-tuple-element.34.s_ref), custom_call_target="tpu_custom_call" | custom-call | tf_op jit(solution)/shard_map/prepare/pallas_call | solution.py:51
  12.3 6.9 %all-to-all-start = ((bf16[16,576,128]{2,1,0:T(8,128)(2,1)}), bf16[16,576,128]{2,1,0:T(8,128)(2,1)S(1)}, u32[]{:S(2)}, u32[]{:S(2)}) async-start(bf16[16,576,128]{2,1,0:T(8,128)(2,1)} %prepare.1), calls=%async_computation | async-start | bytes 4718592 | tf_op jit(solution)/shard_map/all_to_all | solution.py:388
  19.2 15.0 %collective-permute-start.3 = (bf16[2,24,512]{2,1,0:T(8,128)(2,1)}, bf16[2,24,512]{2,1,0:T(8,128)(2,1)}, u32[]{:S(2)}, u32[]{:S(2)}) collective-permute-start(bf16[2,24,512]{2,1,0:T(8,128)(2,1)} %pad_maximum_fusion.6), channel_id=1, source_target_pairs={{0,256},{1,257},{2,258},{3,259},{4,260},{5,261},{6,262},{7,263},{8... | collective-permute-start | bytes 147464 | tf_op jit(solution)/shard_map/ppermute | solution.py:171
  39.4 2.1 %copy.20 = bf16[48,3072]{0,1:T(8,128)(2,1)} copy(bf16[48,3072]{1,0:T(8,128)(2,1)} %constant_dynamic-slice_fusion) | data formatting | bytes 589824
  41.5 2.1 %copy.16 = bf16[48,8,16,24]{0,3,2,1:T(8,128)(2,1)} copy(bf16[48,8,16,24]{0,3,1,2:T(8,128)(2,1)} %bitcast.34) | data formatting | bytes 589824 | tf_op jit(solution)/shard_map/transpose | solution.py:400
  45.7 2.1 %copy.13 = bf16[48,3072]{0,1:T(8,128)(2,1)} copy(bf16[48,3072]{1,0:T(8,128)(2,1)} %param.17) | data formatting | bytes 589824 | tf_op args[7]
  47.8 2.1 %copy.14 = bf16[48,8,16,24]{0,3,2,1:T(8,128)(2,1)} copy(bf16[48,8,16,24]{0,3,1,2:T(8,128)(2,1)} %bitcast.37) | data formatting | bytes 589824 | tf_op jit(solution)/shard_map/transpose | solution.py:400
  49.9 2.1 %copy.18.frozen_ref = bf16[48,3072]{1,0:T(8,128)(2,1)} copy(bf16[48,3072]{0,1:T(8,128)(2,1)} %bitcast.36) | data formatting | bytes 589824 | tf_op jit(solution)/shard_map/reshape | solution.py:400
  52.0 2.1 %widen.1 = (f32[48,3072]{1,0:T(8,128)}, f32[48,3072]{1,0:T(8,128)}) custom-call(bf16[48,3072]{1,0:T(8,128)(2,1)} %copy.18.frozen_ref, bf16[48,3072]{1,0:T(8,128)(2,1)} %copy.19.upstream_ref, f32[1,3072]{1,0:T(1,128)} %reshape.41.gain_ref), custom_call_target="tpu_custom_call" | custom-call | tf_op jit(solution)/shard_map/widen/pallas_call | solution.py:260
  54.1 13.2 %collective-permute-done.3 = bf16[2,24,512]{2,1,0:T(8,128)(2,1)} collective-permute-done((bf16[2,24,512]{2,1,0:T(8,128)(2,1)}, bf16[2,24,512]{2,1,0:T(8,128)(2,1)}, u32[]{:S(2)}, u32[]{:S(2)}) %collective-permute-start.3) | collective-permute-done | bytes 49184 | tf_op jit(solution)/shard_map/ppermute | solution.py:171
  70.7 6.8 %collective-permute-done.4 = bf16[4,24,512]{2,1,0:T(8,128)(2,1)S(1)} collective-permute-done((bf16[4,24,512]{2,1,0:T(8,128)(2,1)S(1)}, bf16[4,24,512]{2,1,0:T(8,128)(2,1)S(1)}, u32[]{:S(2)}, u32[]{:S(2)}) %collective-permute-start.4) | collective-permute-done | bytes 98336 | tf_op jit(solution)/shard_map/ppermute | solution.py:171
  79.1 2.3 %collective-permute-start.5 = (bf16[8,24,512]{2,1,0:T(8,128)(2,1)}, bf16[8,24,512]{2,1,0:T(8,128)(2,1)}, u32[]{:S(2)}, u32[]{:S(2)}) collective-permute-start(bf16[8,24,512]{2,1,0:T(8,128)(2,1)} %pad_maximum_fusion.2), channel_id=1, source_target_pairs={{0,448},{1,449},{2,450},{3,451},{4,452},{5,453},{6,454},{7,455},{8... | collective-permute-start | bytes 589832 | tf_op jit(solution)/shard_map/ppermute | solution.py:171
  81.4 7.1 %attend_first.1 = bf16[1536,128]{1,0:T(8,128)(2,1)} custom-call(s32[1]{0:T(128)S(6)} %sub.3.part_ref, f32[1]{0:T(128)} %bitcast.4.scale_ref, bf16[16,576,128]{2,1,0:T(8,128)(2,1)S(1)} %all-to-all-done.b_ref), custom_call_target="tpu_custom_call" | custom-call | flops 2415919104 | bytes 2359296 | tf_op jit(solution)/shard_map/attend_first/pallas_call | solution.py:126
  88.5 6.6 %collective-permute-start.1 = (bf16[1536,128]{1,0:T(8,128)(2,1)}, bf16[1536,128]{1,0:T(8,128)(2,1)}, u32[]{:S(2)}, u32[]{:S(2)}) collective-permute-start(bf16[1536,128]{1,0:T(8,128)(2,1)} %attend_first.1), channel_id=1, source_target_pairs={{0,1},{1,0},{2,3},{3,2},{4,5},{5,4},{6,7},{7,6},{8,9},{9,8},{10,11... | collective-permute-start | bytes 1179656 | tf_op jit(solution)/shard_map/ppermute | solution.py:171
  99.3 3.4 %collective-permute-start.8 = (bf16[384,512]{1,0:T(8,128)(2,1)}, bf16[384,512]{1,0:T(8,128)(2,1)}, u32[]{:S(2)}, u32[]{:S(2)}) collective-permute-start(bf16[384,512]{1,0:T(8,128)(2,1)} %bitcast.39), channel_id=1, source_target_pairs={{0,24},{1,7},{2,26},{3,5},{4,28},{5,3},{6,30},{7,1},{8,16},{9,15},... | collective-permute-start | bytes 1179656 | tf_op jit(solution)/shard_map/ppermute | solution.py:171
  102.7 2.5 %collective-permute-start.7 = (bf16[384,512]{1,0:T(8,128)(2,1)}, bf16[384,512]{1,0:T(8,128)(2,1)}, u32[]{:S(2)}, u32[]{:S(2)}) collective-permute-start(bf16[384,512]{1,0:T(8,128)(2,1)} %bitcast.40), channel_id=1, source_target_pairs={{0,16},{1,5},{2,18},{3,7},{4,20},{5,1},{6,22},{7,3},{8,24},{9,13},... | collective-permute-start | bytes 1179656 | tf_op jit(solution)/shard_map/ppermute | solution.py:171
  105.2 3.2 %collective-permute-start.6 = (bf16[384,512]{1,0:T(8,128)(2,1)}, bf16[384,512]{1,0:T(8,128)(2,1)}, u32[]{:S(2)}, u32[]{:S(2)}) collective-permute-start(bf16[384,512]{1,0:T(8,128)(2,1)} %bitcast.41), channel_id=1, source_target_pairs={{0,8},{1,3},{2,10},{3,1},{4,12},{5,7},{6,14},{7,5},{8,0},{9,11},{1... | collective-permute-start | bytes 1179656 | tf_op jit(solution)/shard_map/ppermute | solution.py:171
  108.5 7.3 %attend_last.1 = bf16[1536,128]{1,0:T(8,128)(2,1)S(1)} custom-call(s32[1]{0:T(128)} %bitcast.part_ref.core_ref, f32[1]{0:T(128)} %bitcast.4.scale_ref, bf16[16,576,128]{2,1,0:T(8,128)(2,1)S(1)} %all-to-all-done.b_ref, bf16[1536,128]{1,0:T(8,128)(2,1)} %collective-permute-done.1.refs_0_), custom_call_target="tpu_custom_call" | custom-call | flops 2415919104 | bytes 2359296 | tf_op jit(solution)/shard_map/attend_last/pallas_call | solution.py:126
  116.5 4.0 %all-to-all-start.1 = ((bf16[32,48,128]{2,1,0:T(8,128)(2,1)}), bf16[32,48,128]{2,1,0:T(8,128)(2,1)S(1)}, u32[]{:S(2)}, u32[]{:S(2)}) async-start(bf16[32,48,128]{2,1,0:T(8,128)(2,1)} %bitcast.33), calls=%async_computation.1 | async-start | bytes 786432 | tf_op jit(solution)/shard_map/all_to_all | solution.py:410
  122.1 4.4 %collective-permute-start.11 = (bf16[4,384,512]{2,1,0:T(8,128)(2,1)S(1)}, bf16[4,384,512]{2,1,0:T(8,128)(2,1)}, u32[]{:S(2)}, u32[]{:S(2)}) collective-permute-start(bf16[4,384,512]{2,1,0:T(8,128)(2,1)S(1)} %pad_maximum_fusion.w0), channel_id=1, source_target_pairs={{0,6},{1,25},{2,4},{3,27},{4,2},{5,29},{6,0},{7,31},{8,14},{9,17},... | collective-permute-start | bytes 4718600 | tf_op jit(solution)/shard_map/ppermute | solution.py:171
  126.5 2.5 %collective-permute-start.10 = (bf16[4,384,512]{2,1,0:T(8,128)(2,1)S(1)}, bf16[4,384,512]{2,1,0:T(8,128)(2,1)}, u32[]{:S(2)}, u32[]{:S(2)}) collective-permute-start(bf16[4,384,512]{2,1,0:T(8,128)(2,1)S(1)} %pad_maximum_fusion.w0), channel_id=1, source_target_pairs={{0,4},{1,17},{2,6},{3,19},{4,0},{5,21},{6,2},{7,23},{8,12},{9,25},... | collective-permute-start | bytes 4718600 | tf_op jit(solution)/shard_map/ppermute | solution.py:171
  129.0 2.1 %collective-permute-start.9 = (bf16[4,384,512]{2,1,0:T(8,128)(2,1)S(1)}, bf16[4,384,512]{2,1,0:T(8,128)(2,1)}, u32[]{:S(2)}, u32[]{:S(2)}) collective-permute-start(bf16[4,384,512]{2,1,0:T(8,128)(2,1)S(1)} %pad_maximum_fusion.w0), channel_id=1, source_target_pairs={{0,2},{1,9},{2,0},{3,11},{4,6},{5,13},{6,4},{7,15},{8,10},{9,1},{1... | collective-permute-start | bytes 4718600 | tf_op jit(solution)/shard_map/ppermute | solution.py:171
  133.6 3.9 %collective-permute-start.2 = (bf16[48,1024]{1,0:T(8,128)(2,1)}, bf16[48,1024]{1,0:T(8,128)(2,1)S(1)}, u32[]{:S(2)}, u32[]{:S(2)}) collective-permute-start(bf16[48,1024]{1,0:T(8,128)(2,1)} %get-tuple-element.21), channel_id=1, source_target_pairs={{0,1},{1,0},{2,3},{3,2},{4,5},{5,4},{6,7},{7,6},{8,9},{9,8},{10,11... | collective-permute-start | bytes 294920 | tf_op jit(solution)/shard_map/ppermute | solution.py:171
  138.1 25.6 %collective-permute-done.11.w3 = bf16[4,384,512]{2,1,0:T(8,128)(2,1)} collective-permute-done((bf16[4,384,512]{2,1,0:T(8,128)(2,1)S(1)}, bf16[4,384,512]{2,1,0:T(8,128)(2,1)}, u32[]{:S(2)}, u32[]{:S(2)}) %collective-permute-start.11) | collective-permute-done | bytes 1572896 | tf_op jit(solution)/shard_map/ppermute | solution.py:171
  164.9 6.0 %project.1 = (f32[48,3072]{1,0:T(8,128)}, bf16[48,3072]{1,0:T(8,128)(2,1)}) custom-call(s32[3]{0:T(128)} %pad_add_fusion.place_ref, bf16[48,1024]{1,0:T(8,128)(2,1)} %get-tuple-element.20.keep_ref, bf16[48,1024]{1,0:T(8,128)(2,1)} %copy-done.9, bf16[4,384,512]{2,1,0:T(8,128)(2,1)} %copy-done.2, bf16[4,384,512]{2,1,0:T(8,128)(2,1)} %collective-permute-done.9.w1, ...), custom_call_target="tpu_custom_call" | custom-call | tf_op jit(solution)/shard_map/project/pallas_call | solution.py:239
  170.8 4.2 %collective-permute-start.12 = (bf16[48,3072]{1,0:T(8,128)(2,1)}, bf16[48,3072]{1,0:T(8,128)(2,1)S(1)}, u32[]{:S(2)}, u32[]{:S(2)}) collective-permute-start(bf16[48,3072]{1,0:T(8,128)(2,1)} %get-tuple-element.24), channel_id=1, source_target_pairs={{0,1},{1,0},{2,3},{3,2},{4,5},{5,4},{6,7},{7,6},{8,9},{9,8},{10,11... | collective-permute-start | bytes 884744 | tf_op jit(solution)/shard_map/ppermute | solution.py:171
  177.2 3.5 %normalize.1 = (bf16[48,3072]{1,0:T(8,128)(2,1)}, bf16[48,3072]{1,0:T(8,128)(2,1)}) custom-call(f32[48,3072]{1,0:T(8,128)} %get-tuple-element.23.own_ref, bf16[48,3072]{1,0:T(8,128)(2,1)} %copy-done.8, f32[48,3072]{1,0:T(8,128)} %get-tuple-element.25.frozen_ref, f32[48,3072]{1,0:T(8,128)} %get-tuple-element.26.up_ref, f32[1,3072]{1,0:T(1,128)} %reshape.41.gain_ref), custom_call_target="tpu_custom_call" | custom-call | tf_op jit(solution)/shard_map/normalize/pallas_call | solution.py:288
  180.7 2.3 %collective-permute-start.13 = (bf16[48,3072]{1,0:T(8,128)(2,1)}, bf16[48,3072]{1,0:T(8,128)(2,1)S(1)}, u32[]{:S(2)}, u32[]{:S(2)}) collective-permute-start(bf16[48,3072]{1,0:T(8,128)(2,1)} %get-tuple-element.29.grad_ref), channel_id=1, source_target_pairs={{0,1},{1,0},{2,3},{3,2},{4,5},{5,4},{6,7},{7,6},{8,9},{9,8},{10,11... | collective-permute-start | bytes 884744 | tf_op jit(solution)/shard_map/ppermute | solution.py:171
  185.1 5.3 %project_back.1 = bf16[96,1024]{1,0:T(8,128)(2,1)} custom-call(s32[3]{0:T(128)} %pad_add_fusion.place_ref, bf16[48,3072]{1,0:T(8,128)(2,1)} %get-tuple-element.29.grad_ref, bf16[48,3072]{1,0:T(8,128)(2,1)} %copy-done.7, bf16[4,384,512]{2,1,0:T(8,128)(2,1)} %copy-done.2, bf16[4,384,512]{2,1,0:T(8,128)(2,1)} %collective-permute-done.9.w1, ...), custom_call_target="tpu_custom_call" | custom-call | tf_op jit(solution)/shard_map/project_back/pallas_call | solution.py:324
  190.4 11.0 %all-gather = bf16[384,1024]{1,0:T(8,128)(2,1)} all-gather(bf16[96,1024]{1,0:T(8,128)(2,1)} %project_back.1), channel_id=2, replica_groups=mesh['c'=8,'z'=2,'y'=4,'h'=2,'l'=2,'k'=2] {'l','k'}, dimensions={0}, use_global_device_ids=true | all-gather | bytes 983040 | tf_op jit(solution)/shard_map/all_gather | solution.py:417
  201.4 2.6 %scatter_scaled.1 = bf16[192,2048]{1,0:T(8,128)(2,1)} custom-call(f32[1]{0:T(128)} %bitcast.4.scale_ref, bf16[4,96,1024]{2,1,0:T(8,128)(2,1)} %bitcast.38), custom_call_target="tpu_custom_call" | custom-call | tf_op jit(solution)/shard_map/scatter_scaled/pallas_call | solution.py:350
  (59 shorter events, 29.1 us)
Async XLA Ops:
  0.6 33.6 %copy-start = (bf16[192,3072]{1,0:T(8,128)(2,1)S(1)}, bf16[192,3072]{1,0:T(8,128)(2,1)}, u32[]{:S(2)}) copy-start(bf16[192,3072]{1,0:T(8,128)(2,1)} %param.19) | copy-start | bytes 3538948
  0.6 11.0 %collective-permute-start = (bf16[1,24,512]{2,1,0:T(8,128)(2,1)}, bf16[1,24,512]{2,1,0:T(8,128)(2,1)S(1)}, u32[]{:S(2)}, u32[]{:S(2)}) collective-permute-start(bf16[1,24,512]{2,1,0:T(8,128)(2,1)} %bitcast.48), channel_id=1, source_target_pairs={{0,32},{1,33},{2,34},{3,35},{4,36},{5,37},{6,38},{7,39},{8,40},{9,... | collective-permute-start | bytes 73736 | tf_op jit(solution)/shard_map/ppermute | solution.py:171
  7.1 4.6 %copy-start.10 = (bf16[512,24]{0,1:T(8,128)(2,1)S(1)}, bf16[512,24]{0,1:T(8,128)(2,1)}, u32[]{:S(2)}) copy-start(bf16[512,24]{0,1:T(8,128)(2,1)} %param.16) | copy-start | bytes 73732
  12.3 23.3 %copy-start.11 = (f32[3072]{0:T(1024)S(1)}, f32[3072]{0:T(1024)}, u32[]{:S(2)}) copy-start(f32[3072]{0:T(1024)} %param.18) | copy-start | bytes 36868
  12.3 69.1 %all-to-all-start = ((bf16[16,576,128]{2,1,0:T(8,128)(2,1)}), bf16[16,576,128]{2,1,0:T(8,128)(2,1)S(1)}, u32[]{:S(2)}, u32[]{:S(2)}) async-start(bf16[16,576,128]{2,1,0:T(8,128)(2,1)} %prepare.1), calls=%async_computation | async-start | bytes 4718592 | tf_op jit(solution)/shard_map/all_to_all | solution.py:388
  19.2 48.1 %collective-permute-start.3 = (bf16[2,24,512]{2,1,0:T(8,128)(2,1)}, bf16[2,24,512]{2,1,0:T(8,128)(2,1)}, u32[]{:S(2)}, u32[]{:S(2)}) collective-permute-start(bf16[2,24,512]{2,1,0:T(8,128)(2,1)} %pad_maximum_fusion.6), channel_id=1, source_target_pairs={{0,256},{1,257},{2,258},{3,259},{4,260},{5,261},{6,262},{7,263},{8... | collective-permute-start | bytes 147464 | tf_op jit(solution)/shard_map/ppermute | solution.py:171
  47.8 22.3 %copy-start.12 = (f32[64]{0:T(128)S(1)}, f32[64]{0:T(128)}, u32[]{:S(2)}) copy-start(f32[64]{0:T(128)} %param.15) | copy-start | bytes 772
  68.2 9.4 %collective-permute-start.4 = (bf16[4,24,512]{2,1,0:T(8,128)(2,1)S(1)}, bf16[4,24,512]{2,1,0:T(8,128)(2,1)S(1)}, u32[]{:S(2)}, u32[]{:S(2)}) collective-permute-start(bf16[4,24,512]{2,1,0:T(8,128)(2,1)S(1)} %pad_maximum_fusion.5), channel_id=1, source_target_pairs={{0,384},{1,385},{2,386},{3,387},{4,388},{5,389},{6,390},{7,391},{8... | collective-permute-start | bytes 294920 | tf_op jit(solution)/shard_map/ppermute | solution.py:171
  77.5 1.6 copy-start.5
  79.1 16.6 %collective-permute-start.5 = (bf16[8,24,512]{2,1,0:T(8,128)(2,1)}, bf16[8,24,512]{2,1,0:T(8,128)(2,1)}, u32[]{:S(2)}, u32[]{:S(2)}) collective-permute-start(bf16[8,24,512]{2,1,0:T(8,128)(2,1)} %pad_maximum_fusion.2), channel_id=1, source_target_pairs={{0,448},{1,449},{2,450},{3,451},{4,452},{5,453},{6,454},{7,455},{8... | collective-permute-start | bytes 589832 | tf_op jit(solution)/shard_map/ppermute | solution.py:171
  81.4 14.3 %copy-start.4 = (bf16[2,24,512]{2,1,0:T(8,128)(2,1)S(1)}, bf16[2,24,512]{2,1,0:T(8,128)(2,1)}, u32[]{:S(2)}) copy-start(bf16[2,24,512]{2,1,0:T(8,128)(2,1)} %pad_maximum_fusion.6) | copy-start | bytes 147460
  81.4 14.3 %copy-start.6 = (bf16[4,24,512]{2,1,0:T(8,128)(2,1)S(1)}, bf16[4,24,512]{2,1,0:T(8,128)(2,1)}, u32[]{:S(2)}) copy-start(bf16[4,24,512]{2,1,0:T(8,128)(2,1)} %copy-done.5) | copy-start | bytes 294916
  88.5 20.0 %collective-permute-start.1 = (bf16[1536,128]{1,0:T(8,128)(2,1)}, bf16[1536,128]{1,0:T(8,128)(2,1)}, u32[]{:S(2)}, u32[]{:S(2)}) collective-permute-start(bf16[1536,128]{1,0:T(8,128)(2,1)} %attend_first.1), channel_id=1, source_target_pairs={{0,1},{1,0},{2,3},{3,2},{4,5},{5,4},{6,7},{7,6},{8,9},{9,8},{10,11... | collective-permute-start | bytes 1179656 | tf_op jit(solution)/shard_map/ppermute | solution.py:171
  99.3 21.2 %collective-permute-start.8 = (bf16[384,512]{1,0:T(8,128)(2,1)}, bf16[384,512]{1,0:T(8,128)(2,1)}, u32[]{:S(2)}, u32[]{:S(2)}) collective-permute-start(bf16[384,512]{1,0:T(8,128)(2,1)} %bitcast.39), channel_id=1, source_target_pairs={{0,24},{1,7},{2,26},{3,5},{4,28},{5,3},{6,30},{7,1},{8,16},{9,15},... | collective-permute-start | bytes 1179656 | tf_op jit(solution)/shard_map/ppermute | solution.py:171
  102.7 17.8 %collective-permute-start.7 = (bf16[384,512]{1,0:T(8,128)(2,1)}, bf16[384,512]{1,0:T(8,128)(2,1)}, u32[]{:S(2)}, u32[]{:S(2)}) collective-permute-start(bf16[384,512]{1,0:T(8,128)(2,1)} %bitcast.40), channel_id=1, source_target_pairs={{0,16},{1,5},{2,18},{3,7},{4,20},{5,1},{6,22},{7,3},{8,24},{9,13},... | collective-permute-start | bytes 1179656 | tf_op jit(solution)/shard_map/ppermute | solution.py:171
  105.2 15.3 %collective-permute-start.6 = (bf16[384,512]{1,0:T(8,128)(2,1)}, bf16[384,512]{1,0:T(8,128)(2,1)}, u32[]{:S(2)}, u32[]{:S(2)}) collective-permute-start(bf16[384,512]{1,0:T(8,128)(2,1)} %bitcast.41), channel_id=1, source_target_pairs={{0,8},{1,3},{2,10},{3,1},{4,12},{5,7},{6,14},{7,5},{8,0},{9,11},{1... | collective-permute-start | bytes 1179656 | tf_op jit(solution)/shard_map/ppermute | solution.py:171
  115.8 0.7 copy-start.1
  116.5 14.6 %all-to-all-start.1 = ((bf16[32,48,128]{2,1,0:T(8,128)(2,1)}), bf16[32,48,128]{2,1,0:T(8,128)(2,1)S(1)}, u32[]{:S(2)}, u32[]{:S(2)}) async-start(bf16[32,48,128]{2,1,0:T(8,128)(2,1)} %bitcast.33), calls=%async_computation.1 | async-start | bytes 786432 | tf_op jit(solution)/shard_map/all_to_all | solution.py:410
  122.1 42.1 %copy-start.2 = (bf16[4,384,512]{2,1,0:T(8,128)(2,1)}, bf16[4,384,512]{2,1,0:T(8,128)(2,1)S(1)}, u32[]{:S(2)}) copy-start(bf16[4,384,512]{2,1,0:T(8,128)(2,1)S(1)} %pad_maximum_fusion.w0) | copy-start | bytes 4718596
  122.1 41.6 %collective-permute-start.11 = (bf16[4,384,512]{2,1,0:T(8,128)(2,1)S(1)}, bf16[4,384,512]{2,1,0:T(8,128)(2,1)}, u32[]{:S(2)}, u32[]{:S(2)}) collective-permute-start(bf16[4,384,512]{2,1,0:T(8,128)(2,1)S(1)} %pad_maximum_fusion.w0), channel_id=1, source_target_pairs={{0,6},{1,25},{2,4},{3,27},{4,2},{5,29},{6,0},{7,31},{8,14},{9,17},... | collective-permute-start | bytes 4718600 | tf_op jit(solution)/shard_map/ppermute | solution.py:171
  126.5 37.2 %collective-permute-start.10 = (bf16[4,384,512]{2,1,0:T(8,128)(2,1)S(1)}, bf16[4,384,512]{2,1,0:T(8,128)(2,1)}, u32[]{:S(2)}, u32[]{:S(2)}) collective-permute-start(bf16[4,384,512]{2,1,0:T(8,128)(2,1)S(1)} %pad_maximum_fusion.w0), channel_id=1, source_target_pairs={{0,4},{1,17},{2,6},{3,19},{4,0},{5,21},{6,2},{7,23},{8,12},{9,25},... | collective-permute-start | bytes 4718600 | tf_op jit(solution)/shard_map/ppermute | solution.py:171
  129.0 35.3 %collective-permute-start.9 = (bf16[4,384,512]{2,1,0:T(8,128)(2,1)S(1)}, bf16[4,384,512]{2,1,0:T(8,128)(2,1)}, u32[]{:S(2)}, u32[]{:S(2)}) collective-permute-start(bf16[4,384,512]{2,1,0:T(8,128)(2,1)S(1)} %pad_maximum_fusion.w0), channel_id=1, source_target_pairs={{0,2},{1,9},{2,0},{3,11},{4,6},{5,13},{6,4},{7,15},{8,10},{9,1},{1... | collective-permute-start | bytes 4718600 | tf_op jit(solution)/shard_map/ppermute | solution.py:171
  131.1 0.7 copy-start.3
  133.6 30.7 %collective-permute-start.2 = (bf16[48,1024]{1,0:T(8,128)(2,1)}, bf16[48,1024]{1,0:T(8,128)(2,1)S(1)}, u32[]{:S(2)}, u32[]{:S(2)}) collective-permute-start(bf16[48,1024]{1,0:T(8,128)(2,1)} %get-tuple-element.21), channel_id=1, source_target_pairs={{0,1},{1,0},{2,3},{3,2},{4,5},{5,4},{6,7},{7,6},{8,9},{9,8},{10,11... | collective-permute-start | bytes 294920 | tf_op jit(solution)/shard_map/ppermute | solution.py:171
  164.2 0.6 copy-start.9
  170.8 5.7 %collective-permute-start.12 = (bf16[48,3072]{1,0:T(8,128)(2,1)}, bf16[48,3072]{1,0:T(8,128)(2,1)S(1)}, u32[]{:S(2)}, u32[]{:S(2)}) collective-permute-start(bf16[48,3072]{1,0:T(8,128)(2,1)} %get-tuple-element.24), channel_id=1, source_target_pairs={{0,1},{1,0},{2,3},{3,2},{4,5},{5,4},{6,7},{7,6},{8,9},{9,8},{10,11... | collective-permute-start | bytes 884744 | tf_op jit(solution)/shard_map/ppermute | solution.py:171
  176.5 0.7 copy-start.8
  180.7 3.7 %collective-permute-start.13 = (bf16[48,3072]{1,0:T(8,128)(2,1)}, bf16[48,3072]{1,0:T(8,128)(2,1)S(1)}, u32[]{:S(2)}, u32[]{:S(2)}) collective-permute-start(bf16[48,3072]{1,0:T(8,128)(2,1)} %get-tuple-element.29.grad_ref), channel_id=1, source_target_pairs={{0,1},{1,0},{2,3},{3,2},{4,5},{5,4},{6,7},{7,6},{8,9},{9,8},{10,11... | collective-permute-start | bytes 884744 | tf_op jit(solution)/shard_map/ppermute | solution.py:171
  184.4 0.7 copy-start.7

commit v5 on v3

--- a/solution.py
+++ b/solution.py
@@ -54,6 +54,7 @@
         grid=(HEADS // group,),
         in_specs=[column, column, column, whole, whole],
         out_specs=pl.BlockSpec((group, 3 * rows, HEAD_DIM), lambda i: (i, 0, 0)),
+        compiler_params=pltpu.CompilerParams(vmem_limit_bytes=10 << 20),
         name="prepare",
     )(q, k, v, cosines, sines)
 
@@ -136,7 +137,7 @@
             pltpu.VMEM((2, bq, length), F32),
             pltpu.VMEM((2, bq, 128), F32),
         ],
-        compiler_params=pltpu.CompilerParams(vmem_limit_bytes=40 << 20),
+        compiler_params=pltpu.CompilerParams(vmem_limit_bytes=20 << 20),
         cost_estimate=pl.CostEstimate(
             flops=4 * queries * length * HEAD_DIM,
             bytes_accessed=2 * blocks.size,
@@ -144,25 +145,6 @@
         ),
         name="attend_last" if extra else "attend_first",
     )(part, scale, blocks, *extra)
-
-
-def order_along_z(w, z):
-    def kernel(z_ref, w_ref, o_ref):
-        for other in range(16):
-            d = z_ref[0] ^ other
-            at = (d & 1) * 8 + ((d >> 1) & 1) * 4 + ((d >> 2) & 1) * 2 + ((d >> 3) & 1)
-            o_ref[other] = w_ref[at]
-
-    return pl.pallas_call(
-        kernel,
-        out_shape=jax.ShapeDtypeStruct(w.shape, BF16),
-        in_specs=[
-            pl.BlockSpec(memory_space=pltpu.SMEM),
-            pl.BlockSpec(memory_space=pltpu.VMEM),
-        ],
-        out_specs=pl.BlockSpec(memory_space=pltpu.VMEM),
-        name="order_along_z",
-    )(z, w)
 
 
 def exchange(x, partner):
@@ -191,6 +173,7 @@
             pl.BlockSpec(memory_space=pltpu.VMEM),
         ],
         out_specs=(pl.BlockSpec(memory_space=pltpu.VMEM),) * 2,
+        compiler_params=pltpu.CompilerParams(vmem_limit_bytes=4 << 20),
         name="sum_pieces",
     )(core, pieces)
 
@@ -235,7 +218,7 @@
             pltpu.VMEM((2 * share, rows), BF16),
             pltpu.VMEM((2 * share, 8 * columns), F32),
         ],
-        compiler_params=pltpu.CompilerParams(vmem_limit_bytes=32 << 20),
+        compiler_params=pltpu.CompilerParams(vmem_limit_bytes=16 << 20),
         name="project",
     )(place, keep, received, *weights)
 
@@ -251,6 +234,7 @@
         out_shape=(shape, shape),
         in_specs=[pl.BlockSpec(memory_space=pltpu.VMEM)] * 3,
         out_specs=(pl.BlockSpec(memory_space=pltpu.VMEM),) * 2,
+        compiler_params=pltpu.CompilerParams(vmem_limit_bytes=6 << 20),
         name="widen",
     )(frozen, upstream, gain)
 
@@ -280,6 +264,7 @@
         in_specs=[pl.BlockSpec(memory_space=pltpu.VMEM)] * 5,
         out_specs=(pl.BlockSpec(memory_space=pltpu.VMEM),) * 2,
         scratch_shapes=[pltpu.VMEM((share, width), F32)],
+        compiler_params=pltpu.CompilerParams(vmem_limit_bytes=8 << 20),
         name="normalize",
     )(own, received, frozen, upstream, gain)
 
@@ -311,7 +296,7 @@
             pltpu.VMEM((2 * share, width), BF16),
             pltpu.VMEM((2, 2 * share, features), F32),
         ],
-        compiler_params=pltpu.CompilerParams(vmem_limit_bytes=32 << 20),
+        compiler_params=pltpu.CompilerParams(vmem_limit_bytes=16 << 20),
         name="project_back",
     )(place, grad, received, *weights)
 
@@ -321,23 +306,22 @@
     features = rows // 2
 
     def kernel(scale_ref, p_ref, o_ref):
-        for l in range(2):
-            for k in range(2):
-                for row in range(2):
-                    at = (2 * row + k) * features
-                    part = p_ref[2 * l + k, :, row * features : (row + 1) * features]
-                    o_ref[l * tokens : (l + 1) * tokens, at : at + features] = (
-                        scale_ref[0] * part.astype(F32)
-                    ).astype(BF16)
+        for k in range(2):
+            for row in range(2):
+                at = (2 * row + k) * features
+                part = p_ref[k, :, row * features : (row + 1) * features]
+                o_ref[:, at : at + features] = (scale_ref[0] * part.astype(F32)).astype(BF16)
 
     return pl.pallas_call(
         kernel,
         out_shape=jax.ShapeDtypeStruct((2 * tokens, 2 * rows), BF16),
+        grid=(2,),
         in_specs=[
             pl.BlockSpec(memory_space=pltpu.SMEM),
-            pl.BlockSpec(memory_space=pltpu.VMEM),
+            pl.BlockSpec((2, tokens, rows), lambda l: (l, 0, 0)),
         ],
-        out_specs=pl.BlockSpec(memory_space=pltpu.VMEM),
+        out_specs=pl.BlockSpec((tokens, 2 * rows), lambda l: (l, 0)),
+        compiler_params=pltpu.CompilerParams(vmem_limit_bytes=6 << 20),
         name="scatter_scaled",
     )(scale, parts)
 
@@ -346,7 +330,7 @@
     q_ctl, k_ctl, v_ctl, positions, branch_ids, cond_scale, out_weight, frozen, norm_gain, cotangent
 ):
     branch, core = lax.axis_index(BRANCH), lax.axis_index("k")
-    z, y, x = lax.axis_index(("c", "z")), lax.axis_index("y"), lax.axis_index(("h", "l"))
+    y, x = lax.axis_index("y"), lax.axis_index(("h", "l"))
     share, _ = frozen.shape
     features, own = out_weight.shape
     place = jnp.stack([core, x, y]).astype(jnp.int32)
@@ -357,14 +341,14 @@
     def to_partner(v):
         return exchange(v, lambda i: i ^ 1)
 
-    w = out_weight.T[None]
-    for stage in range(4):
-        w = jnp.concatenate([w, exchange(w, lambda i: i ^ (256 >> stage))])
-    w = order_along_z(w, z.astype(jnp.int32).reshape(1)).reshape(16 * own, features)
-    w = jnp.stack(
-        [w]
-        + [exchange(w, lambda i: i ^ (r << (3 if i % 2 == 0 else 1))) for r in range(1, 4)]
-    )
+    w = jnp.broadcast_to(out_weight.T[None], (16, own, features))
+    w = lax.all_to_all(w, ("c", "z"), 0, 0, tiled=True).reshape(16 * own, features)
+    cosines, sines = rope_tables(positions)
+    blocks = prepare(q_ctl[0], k_ctl[0], v_ctl[0], cosines, sines)
+    w, blocks = lax.optimization_barrier((w, blocks))
+    blocks = lax.all_to_all(blocks, CLIP, 0, 0, tiled=True)
+    arrived = [exchange(w, lambda i: i ^ (r << (3 if i % 2 == 0 else 1))) for r in range(1, 4)]
+    w = jnp.stack([w] + arrived)
     weights = [w] + [
         exchange(w, lambda i: i ^ (r << (1 if i % 2 == 0 else 3))) for r in range(1, 4)
     ]
@@ -377,9 +361,6 @@
     upstream = columns_first(lax.dynamic_slice_in_dim(cotangent, branch * share, share, 0))
     frozen, upstream = widen(columns_first(frozen), upstream, gain)
 
-    cosines, sines = rope_tables(positions)
-    blocks = prepare(q_ctl[0], k_ctl[0], v_ctl[0], cosines, sines)
-    blocks = lax.all_to_all(blocks, CLIP, 0, 0, tiled=True)
     blocks, frozen, upstream, gain = lax.optimization_barrier((blocks, frozen, upstream, gain))
     core = core.astype(jnp.int32).reshape(1)
     received = to_partner(attend(blocks, scale, 1 - core))

time: 211 us -> 185 us (0.88)
  Pallas kernels: 39.1 us -> 27.5 us
  starting transfers between devices: 71.9 us -> 67.6 us
  other arithmetic: 7.31 us -> 3.49 us
  local copies, waits for them, and re-layouts: 27.5 us -> 23.7 us
  waiting for transfers between devices: 52.9 us -> 50.5 us
    ppermute x14 -> x10, starting transfers between devices: 57.3 us -> 35 us  [exchange(): lax.ppermute(x, SEQ + BRANCH, [(i, partner(i)) for i in range(count)])]
    ppermute x14 -> x10, waiting for transfers between devices: 52.9 us -> 31.5 us  [exchange(): lax.ppermute(x, SEQ + BRANCH, [(i, partner(i)) for i in range(count)])]
    all_to_all x0 -> x1, starting transfers between devices: none -> 15.8 us  [on_device(): lax.all_to_all(w, ('c', 'z'), 0, 0, tiled=True).reshape(16 * own, features)]
    all_to_all x0 -> x1, waiting for transfers between devices: none -> 13.1 us  [on_device(): lax.all_to_all(w, ('c', 'z'), 0, 0, tiled=True).reshape(16 * own, features)]
    all_to_all x1, waiting for transfers between devices: 0.01 us -> 5.84 us  [on_device(): blocks = lax.all_to_all(blocks, CLIP, 0, 0, tiled=True)]
    unnamed x28, local copies, waits for them, and re-layouts: 13.1 us -> 9.71 us
    concatenate x3 -> x0, other arithmetic: 3.02 us -> none  [on_device(): w = jnp.concatenate([w, exchange(w, lambda i: i ^ 256 >> stage)])]
  transfers between devices with their start and end apart: 16 -> 13, of which waited for: 8 -> 6; matrix products, arithmetic and copies ran while one was open for 13% -> 11% of each run, Pallas kernels for 10% -> 5%
where the time goes in v5:
time: 185 us; the launch traced here: 183 us
  starting transfers between devices  67.6 us (37%)
  waiting for transfers between devices  50.5 us (27%)
  Pallas kernels  27.5 us (15%)
  local copies, waits for them, and re-layouts  23.7 us (13%)
  blocking collectives  9.13 us (5%)
  other arithmetic  3.49 us (2%)
    ppermute x10, starting transfers between devices, exchange(): lax.ppermute(x, SEQ + BRANCH, [(i, partner(i)) for i in range(count)])  35 us
    ppermute x10, waiting for transfers between devices, exchange(): lax.ppermute(x, SEQ + BRANCH, [(i, partner(i)) for i in range(count)])  31.5 us
    all_to_all x1, starting transfers between devices, on_device(): lax.all_to_all(w, ('c', 'z'), 0, 0, tiled=True).reshape(16 * own, features)  15.8 us
    all_to_all x1, waiting for transfers between devices, on_device(): lax.all_to_all(w, ('c', 'z'), 0, 0, tiled=True).reshape(16 * own, features)  13.1 us
    pallas_call x2, Pallas kernels, attend(): pl.pallas_call(kernel, out_shape=jax.ShapeDtypeStruct((queries, HEAD_DIM)...  12.7 us
    all_to_all x1, starting transfers between devices, on_device(): blocks = lax.all_to_all(blocks, CLIP, 0, 0, tiled=True)  10.9 us
    unnamed x28, local copies, waits for them, and re-layouts  9.71 us
    all_gather x1, blocking collectives, on_device(): parts = lax.all_gather(cot, BRANCH, axis=0, tiled=False)  9.13 us
  transfers between devices with their start and end apart: 13, of which 6 were waited for; matrix products, arithmetic and copies ran while one was open for 11% of the time, Pallas kernels for 5%

profile of v5, /device:TPU:1, one launch (start us, length us, event | category | flops | bytes accessed | tf_op | source)
XLA Modules:
  0.0 183.4 jit_solution(1863156421512938766)
XLA Ops:
  0.7 1.7 broadcast_in_dim.16
  2.3 15.8 %all-to-all-start = ((bf16[16,24,512]{2,1,0:T(8,128)(2,1)}), bf16[16,24,512]{2,1,0:T(8,128)(2,1)}, u32[]{:S(2)}, u32[]{:S(2)}) async-start(bf16[16,24,512]{2,1,0:T(8,128)(2,1)} %broadcast_in_dim.16), calls=%async_computation | async-start | bytes 786432 | tf_op jit(solution)/shard_map/all_to_all | solution.py:345
  20.5 2.6 %prepare.1 = bf16[16,576,128]{2,1,0:T(8,128)(2,1)} custom-call(bf16[192,2048]{1,0:T(8,128)(2,1)S(1)} %bitcast.30, bf16[192,2048]{1,0:T(8,128)(2,1)S(1)} %bitcast.31, bf16[192,2048]{1,0:T(8,128)(2,1)S(1)} %bitcast.32, f32[192,128]{1,0:T(8,128)S(1)} %get-tuple-element.33.c_ref, f32[192,128]{1,0:T(8,128)S(1)} %get-tuple-element.34.s_ref), custom_call_target="tpu_custom_call" | custom-call | tf_op jit(solution)/shard_map/prepare/pallas_call | solution.py:51
  23.2 13.1 %all-to-all-done = bf16[16,24,512]{2,1,0:T(8,128)(2,1)} async-done(((bf16[16,24,512]{2,1,0:T(8,128)(2,1)}), bf16[16,24,512]{2,1,0:T(8,128)(2,1)}, u32[]{:S(2)}, u32[]{:S(2)}) %all-to-all-start) | async-done | bytes 393248 | tf_op jit(solution)/shard_map/all_to_all | solution.py:345
  36.3 10.9 %all-to-all-start.1 = ((bf16[16,576,128]{2,1,0:T(8,128)(2,1)}), bf16[16,576,128]{2,1,0:T(8,128)(2,1)S(1)}, u32[]{:S(2)}, u32[]{:S(2)}) async-start(bf16[16,576,128]{2,1,0:T(8,128)(2,1)} %prepare.1), calls=%async_computation.1 | async-start | bytes 4718592 | tf_op jit(solution)/shard_map/all_to_all | solution.py:349
  51.7 2.1 %copy.20 = bf16[48,3072]{0,1:T(8,128)(2,1)} copy(bf16[48,3072]{1,0:T(8,128)(2,1)} %constant_dynamic-slice_fusion) | data formatting | bytes 589824
  53.9 2.1 %copy.16 = bf16[48,8,16,24]{0,3,2,1:T(8,128)(2,1)} copy(bf16[48,8,16,24]{0,3,1,2:T(8,128)(2,1)} %bitcast.34) | data formatting | bytes 589824 | tf_op jit(solution)/shard_map/transpose | solution.py:358
  56.0 2.1 %copy.19.upstream_ref = bf16[48,3072]{1,0:T(8,128)(2,1)} copy(bf16[48,3072]{0,1:T(8,128)(2,1)} %bitcast.35) | data formatting | bytes 589824 | tf_op jit(solution)/shard_map/reshape | solution.py:358
  58.0 2.1 %copy.13 = bf16[48,3072]{0,1:T(8,128)(2,1)} copy(bf16[48,3072]{1,0:T(8,128)(2,1)} %param.17) | data formatting | bytes 589824 | tf_op args[7]
  60.2 2.1 %copy.14 = bf16[48,8,16,24]{0,3,2,1:T(8,128)(2,1)} copy(bf16[48,8,16,24]{0,3,1,2:T(8,128)(2,1)} %bitcast.37) | data formatting | bytes 589824 | tf_op jit(solution)/shard_map/transpose | solution.py:358
  62.3 2.1 %copy.18.frozen_ref = bf16[48,3072]{1,0:T(8,128)(2,1)} copy(bf16[48,3072]{0,1:T(8,128)(2,1)} %bitcast.36) | data formatting | bytes 589824 | tf_op jit(solution)/shard_map/reshape | solution.py:358
  68.7 5.8 %all-to-all-done.1.b_ref = bf16[16,576,128]{2,1,0:T(8,128)(2,1)S(1)} async-done(((bf16[16,576,128]{2,1,0:T(8,128)(2,1)}), bf16[16,576,128]{2,1,0:T(8,128)(2,1)S(1)}, u32[]{:S(2)}, u32[]{:S(2)}) %all-to-all-start.1) | async-done | bytes 2359328 | tf_op jit(solution)/shard_map/all_to_all | solution.py:349
  74.5 6.4 %attend_first.1 = bf16[1536,128]{1,0:T(8,128)(2,1)S(1)} custom-call(s32[1]{0:T(128)S(6)} %sub.3.part_ref, f32[1]{0:T(128)} %bitcast.4.scale_ref, bf16[16,576,128]{2,1,0:T(8,128)(2,1)S(1)} %all-to-all-done.1.b_ref), custom_call_target="tpu_custom_call" | custom-call | flops 2415919104 | bytes 2359296 | tf_op jit(solution)/shard_map/attend_first/pallas_call | solution.py:127
  80.9 5.4 %collective-permute-start = (bf16[1536,128]{1,0:T(8,128)(2,1)S(1)}, bf16[1536,128]{1,0:T(8,128)(2,1)S(1)}, u32[]{:S(2)}, u32[]{:S(2)}) collective-permute-start(bf16[1536,128]{1,0:T(8,128)(2,1)S(1)} %attend_first.1), channel_id=1, source_target_pairs={{0,1},{1,0},{2,3},{3,2},{4,5},{5,4},{6,7},{7,6},{8,9},{9,8},{10,11... | collective-permute-start | bytes 1179656 | tf_op jit(solution)/shard_map/ppermute | solution.py:152
  86.3 4.7 %collective-permute-start.4 = (bf16[384,512]{1,0:T(8,128)(2,1)}, bf16[384,512]{1,0:T(8,128)(2,1)}, u32[]{:S(2)}, u32[]{:S(2)}) collective-permute-start(bf16[384,512]{1,0:T(8,128)(2,1)} %bitcast.6), channel_id=1, source_target_pairs={{0,24},{1,7},{2,26},{3,5},{4,28},{5,3},{6,30},{7,1},{8,16},{9,15},... | collective-permute-start | bytes 1179656 | tf_op jit(solution)/shard_map/ppermute | solution.py:152
  91.0 3.7 %collective-permute-start.3 = (bf16[384,512]{1,0:T(8,128)(2,1)}, bf16[384,512]{1,0:T(8,128)(2,1)}, u32[]{:S(2)}, u32[]{:S(2)}) collective-permute-start(bf16[384,512]{1,0:T(8,128)(2,1)} %bitcast.6), channel_id=1, source_target_pairs={{0,16},{1,5},{2,18},{3,7},{4,20},{5,1},{6,22},{7,3},{8,24},{9,13},... | collective-permute-start | bytes 1179656 | tf_op jit(solution)/shard_map/ppermute | solution.py:152
  94.6 2.1 %collective-permute-start.2 = (bf16[384,512]{1,0:T(8,128)(2,1)}, bf16[384,512]{1,0:T(8,128)(2,1)}, u32[]{:S(2)}, u32[]{:S(2)}) collective-permute-start(bf16[384,512]{1,0:T(8,128)(2,1)} %bitcast.6), channel_id=1, source_target_pairs={{0,8},{1,3},{2,10},{3,1},{4,12},{5,7},{6,14},{7,5},{8,0},{9,11},{1... | collective-permute-start | bytes 1179656 | tf_op jit(solution)/shard_map/ppermute | solution.py:152
  96.8 6.4 %attend_last.1 = bf16[1536,128]{1,0:T(8,128)(2,1)S(1)} custom-call(s32[1]{0:T(128)} %bitcast.part_ref.core_ref, f32[1]{0:T(128)} %bitcast.4.scale_ref, bf16[16,576,128]{2,1,0:T(8,128)(2,1)S(1)} %all-to-all-done.1.b_ref, bf16[1536,128]{1,0:T(8,128)(2,1)S(1)} %collective-permute-done.refs_0_), custom_call_target="tpu_custom_call" | custom-call | flops 2415919104 | bytes 2359296 | tf_op jit(solution)/shard_map/attend_last/pallas_call | solution.py:127
  103.9 5.9 %all-to-all-start.2 = ((bf16[32,48,128]{2,1,0:T(8,128)(2,1)}), bf16[32,48,128]{2,1,0:T(8,128)(2,1)S(1)}, u32[]{:S(2)}, u32[]{:S(2)}) async-start(bf16[32,48,128]{2,1,0:T(8,128)(2,1)} %bitcast.33), calls=%async_computation.2 | async-start | bytes 786432 | tf_op jit(solution)/shard_map/all_to_all | solution.py:368
  109.9 1.6 pad_maximum_fusion.w0
  111.4 4.4 %collective-permute-start.7 = (bf16[4,384,512]{2,1,0:T(8,128)(2,1)S(1)}, bf16[4,384,512]{2,1,0:T(8,128)(2,1)}, u32[]{:S(2)}, u32[]{:S(2)}) collective-permute-start(bf16[4,384,512]{2,1,0:T(8,128)(2,1)S(1)} %pad_maximum_fusion.w0), channel_id=1, source_target_pairs={{0,6},{1,25},{2,4},{3,27},{4,2},{5,29},{6,0},{7,31},{8,14},{9,17},... | collective-permute-start | bytes 4718600 | tf_op jit(solution)/shard_map/ppermute | solution.py:152
  115.8 2.5 %collective-permute-start.6 = (bf16[4,384,512]{2,1,0:T(8,128)(2,1)S(1)}, bf16[4,384,512]{2,1,0:T(8,128)(2,1)}, u32[]{:S(2)}, u32[]{:S(2)}) collective-permute-start(bf16[4,384,512]{2,1,0:T(8,128)(2,1)S(1)} %pad_maximum_fusion.w0), channel_id=1, source_target_pairs={{0,4},{1,17},{2,6},{3,19},{4,0},{5,21},{6,2},{7,23},{8,12},{9,25},... | collective-permute-start | bytes 4718600 | tf_op jit(solution)/shard_map/ppermute | solution.py:152
  118.3 2.1 %collective-permute-start.5 = (bf16[4,384,512]{2,1,0:T(8,128)(2,1)S(1)}, bf16[4,384,512]{2,1,0:T(8,128)(2,1)}, u32[]{:S(2)}, u32[]{:S(2)}) collective-permute-start(bf16[4,384,512]{2,1,0:T(8,128)(2,1)S(1)} %pad_maximum_fusion.w0), channel_id=1, source_target_pairs={{0,2},{1,9},{2,0},{3,11},{4,6},{5,13},{6,4},{7,15},{8,10},{9,1},{1... | collective-permute-start | bytes 4718600 | tf_op jit(solution)/shard_map/ppermute | solution.py:152
  120.5 3.8 %collective-permute-start.1 = (bf16[48,1024]{1,0:T(8,128)(2,1)S(1)}, bf16[48,1024]{1,0:T(8,128)(2,1)S(1)}, u32[]{:S(2)}, u32[]{:S(2)}) collective-permute-start(bf16[48,1024]{1,0:T(8,128)(2,1)S(1)} %get-tuple-element.21), channel_id=1, source_target_pairs={{0,1},{1,0},{2,3},{3,2},{4,5},{5,4},{6,7},{7,6},{8,9},{9,8},{10,11... | collective-permute-start | bytes 294920 | tf_op jit(solution)/shard_map/ppermute | solution.py:152
  124.4 28.6 %collective-permute-done.7.w3 = bf16[4,384,512]{2,1,0:T(8,128)(2,1)} collective-permute-done((bf16[4,384,512]{2,1,0:T(8,128)(2,1)S(1)}, bf16[4,384,512]{2,1,0:T(8,128)(2,1)}, u32[]{:S(2)}, u32[]{:S(2)}) %collective-permute-start.7) | collective-permute-done | bytes 1572896 | tf_op jit(solution)/shard_map/ppermute | solution.py:152
  153.5 4.6 %project.1 = (f32[48,3072]{1,0:T(8,128)S(1)}, bf16[48,3072]{1,0:T(8,128)(2,1)S(1)}) custom-call(s32[3]{0:T(128)S(1)} %pad_add_fusion.place_ref, bf16[48,1024]{1,0:T(8,128)(2,1)S(1)} %get-tuple-element.20.keep_ref, bf16[48,1024]{1,0:T(8,128)(2,1)S(1)} %collective-permute-done.1.received_ref, bf16[4,384,512]{2,1,0:T(8,128)(2,1)S(1)} %pad_maximum_fusion.w0, ...), custom_call_target="tpu_custom_call" | custom-call | tf_op jit(solution)/shard_map/project/pallas_call | solution.py:208
  158.1 4.1 %collective-permute-start.8 = (bf16[48,3072]{1,0:T(8,128)(2,1)S(1)}, bf16[48,3072]{1,0:T(8,128)(2,1)S(1)}, u32[]{:S(2)}, u32[]{:S(2)}) collective-permute-start(bf16[48,3072]{1,0:T(8,128)(2,1)S(1)} %get-tuple-element.24), channel_id=1, source_target_pairs={{0,1},{1,0},{2,3},{3,2},{4,5},{5,4},{6,7},{7,6},{8,9},{9,8},{10,11... | collective-permute-start | bytes 884744 | tf_op jit(solution)/shard_map/ppermute | solution.py:152
  163.5 2.0 %normalize.1 = (bf16[48,3072]{1,0:T(8,128)(2,1)}, bf16[48,3072]{1,0:T(8,128)(2,1)S(1)}) custom-call(f32[48,3072]{1,0:T(8,128)S(1)} %get-tuple-element.23.own_ref, bf16[48,3072]{1,0:T(8,128)(2,1)S(1)} %collective-permute-done.8.received_ref, f32[48,3072]{1,0:T(8,128)S(1)} %copy-done.7, f32[48,3072]{1,0:T(8,128)S(1)} %copy-done.9, f32[1,3072]{1,0:T(1,128)S(1)} %reshape.43.gain_ref), custom_call_target="tpu_custom_call" | custom-call | tf_op jit(solution)/shard_map/normalize/pallas_call | solution.py:261
  165.5 2.3 %collective-permute-start.9 = (bf16[48,3072]{1,0:T(8,128)(2,1)S(1)}, bf16[48,3072]{1,0:T(8,128)(2,1)S(1)}, u32[]{:S(2)}, u32[]{:S(2)}) collective-permute-start(bf16[48,3072]{1,0:T(8,128)(2,1)S(1)} %get-tuple-element.29.grad_ref), channel_id=1, source_target_pairs={{0,1},{1,0},{2,3},{3,2},{4,5},{5,4},{6,7},{7,6},{8,9},{9,8},{10,11... | collective-permute-start | bytes 884744 | tf_op jit(solution)/shard_map/ppermute | solution.py:152
  169.0 3.8 %project_back.1 = bf16[96,1024]{1,0:T(8,128)(2,1)S(1)} custom-call(s32[3]{0:T(128)S(1)} %pad_add_fusion.place_ref, bf16[48,3072]{1,0:T(8,128)(2,1)S(1)} %get-tuple-element.29.grad_ref, bf16[48,3072]{1,0:T(8,128)(2,1)S(1)} %collective-permute-done.9.received_ref, bf16[4,384,512]{2,1,0:T(8,128)(2,1)S(1)} %pad_maximum_fusion.w0, ...), custom_call_target="tpu_custom_call" | custom-call | tf_op jit(solution)/shard_map/project_back/pallas_call | solution.py:289
  172.7 9.1 %all-gather = bf16[384,1024]{1,0:T(8,128)(2,1)S(1)} all-gather(bf16[96,1024]{1,0:T(8,128)(2,1)S(1)} %project_back.1), channel_id=2, replica_groups=mesh['c'=8,'z'=2,'y'=4,'h'=2,'l'=2,'k'=2] {'l','k'}, dimensions={0}, use_global_device_ids=true | all-gather | bytes 983040 | tf_op jit(solution)/shard_map/all_gather | solution.py:375
  181.8 1.6 scatter_scaled.1
  (48 shorter events, 14.4 us)
Async XLA Ops:
  0.6 50.4 %copy-start = (bf16[192,3072]{1,0:T(8,128)(2,1)S(1)}, bf16[192,3072]{1,0:T(8,128)(2,1)}, u32[]{:S(2)}) copy-start(bf16[192,3072]{1,0:T(8,128)(2,1)} %param.19) | copy-start | bytes 3538948
  0.6 18.7 %copy-start.4 = (bf16[1,192,2048]{2,1,0:T(8,128)(2,1)S(1)}, bf16[1,192,2048]{2,1,0:T(8,128)(2,1)}, u32[]{:S(2)}) copy-start(bf16[1,192,2048]{2,1,0:T(8,128)(2,1)} %param.11) | copy-start | bytes 2359300
  0.7 18.7 %copy-start.3 = (bf16[1,192,2048]{2,1,0:T(8,128)(2,1)S(1)}, bf16[1,192,2048]{2,1,0:T(8,128)(2,1)}, u32[]{:S(2)}) copy-start(bf16[1,192,2048]{2,1,0:T(8,128)(2,1)} %param.10) | copy-start | bytes 2359300
  2.3 34.0 %all-to-all-start = ((bf16[16,24,512]{2,1,0:T(8,128)(2,1)}), bf16[16,24,512]{2,1,0:T(8,128)(2,1)}, u32[]{:S(2)}, u32[]{:S(2)}) async-start(bf16[16,24,512]{2,1,0:T(8,128)(2,1)} %broadcast_in_dim.16), calls=%async_computation | async-start | bytes 786432 | tf_op jit(solution)/shard_map/all_to_all | solution.py:345
  19.4 1.1 copy-start.5
  36.3 11.5 %copy-start.11 = (f32[3072]{0:T(1024)S(1)}, f32[3072]{0:T(1024)}, u32[]{:S(2)}) copy-start(f32[3072]{0:T(1024)} %param.18) | copy-start | bytes 36868
  36.3 38.2 %all-to-all-start.1 = ((bf16[16,576,128]{2,1,0:T(8,128)(2,1)}), bf16[16,576,128]{2,1,0:T(8,128)(2,1)S(1)}, u32[]{:S(2)}, u32[]{:S(2)}) async-start(bf16[16,576,128]{2,1,0:T(8,128)(2,1)} %prepare.1), calls=%async_computation.1 | async-start | bytes 4718592 | tf_op jit(solution)/shard_map/all_to_all | solution.py:349
  60.2 7.9 %copy-start.12 = (f32[64]{0:T(128)S(1)}, f32[64]{0:T(128)}, u32[]{:S(2)}) copy-start(f32[64]{0:T(128)} %param.15) | copy-start | bytes 772
  64.4 1.0 copy-start.1
  65.3 1.0 copy-start.2
  66.4 0.8 copy-start.6
  67.2 0.8 copy-start.8
  80.9 15.9 %collective-permute-start = (bf16[1536,128]{1,0:T(8,128)(2,1)S(1)}, bf16[1536,128]{1,0:T(8,128)(2,1)S(1)}, u32[]{:S(2)}, u32[]{:S(2)}) collective-permute-start(bf16[1536,128]{1,0:T(8,128)(2,1)S(1)} %attend_first.1), channel_id=1, source_target_pairs={{0,1},{1,0},{2,3},{3,2},{4,5},{5,4},{6,7},{7,6},{8,9},{9,8},{10,11... | collective-permute-start | bytes 1179656 | tf_op jit(solution)/shard_map/ppermute | solution.py:152
  86.3 23.6 %collective-permute-start.4 = (bf16[384,512]{1,0:T(8,128)(2,1)}, bf16[384,512]{1,0:T(8,128)(2,1)}, u32[]{:S(2)}, u32[]{:S(2)}) collective-permute-start(bf16[384,512]{1,0:T(8,128)(2,1)} %bitcast.6), channel_id=1, source_target_pairs={{0,24},{1,7},{2,26},{3,5},{4,28},{5,3},{6,30},{7,1},{8,16},{9,15},... | collective-permute-start | bytes 1179656 | tf_op jit(solution)/shard_map/ppermute | solution.py:152
  91.0 18.9 %collective-permute-start.3 = (bf16[384,512]{1,0:T(8,128)(2,1)}, bf16[384,512]{1,0:T(8,128)(2,1)}, u32[]{:S(2)}, u32[]{:S(2)}) collective-permute-start(bf16[384,512]{1,0:T(8,128)(2,1)} %bitcast.6), channel_id=1, source_target_pairs={{0,16},{1,5},{2,18},{3,7},{4,20},{5,1},{6,22},{7,3},{8,24},{9,13},... | collective-permute-start | bytes 1179656 | tf_op jit(solution)/shard_map/ppermute | solution.py:152
  94.6 15.2 %collective-permute-start.2 = (bf16[384,512]{1,0:T(8,128)(2,1)}, bf16[384,512]{1,0:T(8,128)(2,1)}, u32[]{:S(2)}, u32[]{:S(2)}) collective-permute-start(bf16[384,512]{1,0:T(8,128)(2,1)} %bitcast.6), channel_id=1, source_target_pairs={{0,8},{1,3},{2,10},{3,1},{4,12},{5,7},{6,14},{7,5},{8,0},{9,11},{1... | collective-permute-start | bytes 1179656 | tf_op jit(solution)/shard_map/ppermute | solution.py:152
  103.2 0.8 copy-start.10
  103.9 16.5 %all-to-all-start.2 = ((bf16[32,48,128]{2,1,0:T(8,128)(2,1)}), bf16[32,48,128]{2,1,0:T(8,128)(2,1)S(1)}, u32[]{:S(2)}, u32[]{:S(2)}) async-start(bf16[32,48,128]{2,1,0:T(8,128)(2,1)} %bitcast.33), calls=%async_computation.2 | async-start | bytes 786432 | tf_op jit(solution)/shard_map/all_to_all | solution.py:368
  111.4 41.6 %collective-permute-start.7 = (bf16[4,384,512]{2,1,0:T(8,128)(2,1)S(1)}, bf16[4,384,512]{2,1,0:T(8,128)(2,1)}, u32[]{:S(2)}, u32[]{:S(2)}) collective-permute-start(bf16[4,384,512]{2,1,0:T(8,128)(2,1)S(1)} %pad_maximum_fusion.w0), channel_id=1, source_target_pairs={{0,6},{1,25},{2,4},{3,27},{4,2},{5,29},{6,0},{7,31},{8,14},{9,17},... | collective-permute-start | bytes 4718600 | tf_op jit(solution)/shard_map/ppermute | solution.py:152
  115.8 37.2 %collective-permute-start.6 = (bf16[4,384,512]{2,1,0:T(8,128)(2,1)S(1)}, bf16[4,384,512]{2,1,0:T(8,128)(2,1)}, u32[]{:S(2)}, u32[]{:S(2)}) collective-permute-start(bf16[4,384,512]{2,1,0:T(8,128)(2,1)S(1)} %pad_maximum_fusion.w0), channel_id=1, source_target_pairs={{0,4},{1,17},{2,6},{3,19},{4,0},{5,21},{6,2},{7,23},{8,12},{9,25},... | collective-permute-start | bytes 4718600 | tf_op jit(solution)/shard_map/ppermute | solution.py:152
  118.3 35.3 %collective-permute-start.5 = (bf16[4,384,512]{2,1,0:T(8,128)(2,1)S(1)}, bf16[4,384,512]{2,1,0:T(8,128)(2,1)}, u32[]{:S(2)}, u32[]{:S(2)}) collective-permute-start(bf16[4,384,512]{2,1,0:T(8,128)(2,1)S(1)} %pad_maximum_fusion.w0), channel_id=1, source_target_pairs={{0,2},{1,9},{2,0},{3,11},{4,6},{5,13},{6,4},{7,15},{8,10},{9,1},{1... | collective-permute-start | bytes 4718600 | tf_op jit(solution)/shard_map/ppermute | solution.py:152
  120.5 33.0 %collective-permute-start.1 = (bf16[48,1024]{1,0:T(8,128)(2,1)S(1)}, bf16[48,1024]{1,0:T(8,128)(2,1)S(1)}, u32[]{:S(2)}, u32[]{:S(2)}) collective-permute-start(bf16[48,1024]{1,0:T(8,128)(2,1)S(1)} %get-tuple-element.21), channel_id=1, source_target_pairs={{0,1},{1,0},{2,3},{3,2},{4,5},{5,4},{6,7},{7,6},{8,9},{9,8},{10,11... | collective-permute-start | bytes 294920 | tf_op jit(solution)/shard_map/ppermute | solution.py:152
  153.5 9.9 %copy-start.7 = (f32[48,3072]{1,0:T(8,128)S(1)}, f32[48,3072]{1,0:T(8,128)}, u32[]{:S(2)}) copy-start(f32[48,3072]{1,0:T(8,128)} %copy-done.6) | copy-start | bytes 1769476
  153.5 9.9 %copy-start.9 = (f32[48,3072]{1,0:T(8,128)S(1)}, f32[48,3072]{1,0:T(8,128)}, u32[]{:S(2)}) copy-start(f32[48,3072]{1,0:T(8,128)} %copy-done.8) | copy-start | bytes 1769476
  158.1 5.3 %collective-permute-start.8 = (bf16[48,3072]{1,0:T(8,128)(2,1)S(1)}, bf16[48,3072]{1,0:T(8,128)(2,1)S(1)}, u32[]{:S(2)}, u32[]{:S(2)}) collective-permute-start(bf16[48,3072]{1,0:T(8,128)(2,1)S(1)} %get-tuple-element.24), channel_id=1, source_target_pairs={{0,1},{1,0},{2,3},{3,2},{4,5},{5,4},{6,7},{7,6},{8,9},{9,8},{10,11... | collective-permute-start | bytes 884744 | tf_op jit(solution)/shard_map/ppermute | solution.py:152
  165.5 3.5 %collective-permute-start.9 = (bf16[48,3072]{1,0:T(8,128)(2,1)S(1)}, bf16[48,3072]{1,0:T(8,128)(2,1)S(1)}, u32[]{:S(2)}, u32[]{:S(2)}) collective-permute-start(bf16[48,3072]{1,0:T(8,128)(2,1)S(1)} %get-tuple-element.29.grad_ref), channel_id=1, source_target_pairs={{0,1},{1,0},{2,3},{3,2},{4,5},{5,4},{6,7},{7,6},{8,9},{9,8},{10,11... | collective-permute-start | bytes 884744 | tf_op jit(solution)/shard_map/ppermute | solution.py:152

commit v6 on v5

--- a/solution.py
+++ b/solution.py
@@ -178,25 +178,28 @@
     )(core, pieces)
 
 
-def weight_block(place_ref, outer, inner):
+def weight_block(place_ref, offset, inner):
     core, x, y = place_ref[0], place_ref[1], place_ref[2]
     first = core == 0
-    x_there = x ^ jnp.where(first, outer, inner)
-    y_there = y ^ jnp.where(first, inner, outer)
-    return x_there % 2, y_there * 2 + x_there // 2
+    x_there = jnp.where(first, (x + offset) & 3, x ^ inner)
+    y_there = jnp.where(first, y ^ inner, (y + offset) & 3)
+    return x_there & 1, y_there * 2 + (x_there >> 1)
+
+
+BUFFERS = ((0, 0, 4), (1, 0, 4), (3, 0, 4), (2, 0, 2), (2, 2, 2))
 
 
 def project(place, keep, received, weights):
     share, rows = keep.shape
     _, columns, features = weights[0].shape
 
-    def kernel(place_ref, keep_ref, received_ref, w0, w1, w2, w3, own_ref, send_ref, m_ref, a_ref):
+    def kernel(place_ref, keep_ref, received_ref, w0, w1, w2, w3, w4, own_ref, send_ref, m_ref, a_ref):
         m_ref[0:share, :] = keep_ref[...]
         m_ref[share:, :] = received_ref[...]
         a_ref[...] = jnp.zeros_like(a_ref)
-        for outer, w_ref in enumerate((w0, w1, w2, w3)):
-            for inner in range(4):
-                row, column = weight_block(place_ref, outer, inner)
+        for w_ref, (offset, begin, count) in zip((w0, w1, w2, w3, w4), BUFFERS):
+            for inner in range(count):
+                row, column = weight_block(place_ref, offset, begin + inner)
                 m = m_ref[:, pl.ds(pl.multiple_of(row * features, features), features)]
                 at = pl.ds(pl.multiple_of(column * columns, columns), columns)
                 a_ref[:, at] += lax.dot_general(
@@ -212,7 +215,7 @@
             jax.ShapeDtypeStruct((share, 8 * columns), BF16),
         ),
         in_specs=[pl.BlockSpec(memory_space=pltpu.SMEM)]
-        + [pl.BlockSpec(memory_space=pltpu.VMEM)] * 6,
+        + [pl.BlockSpec(memory_space=pltpu.VMEM)] * 7,
         out_specs=(pl.BlockSpec(memory_space=pltpu.VMEM),) * 2,
         scratch_shapes=[
             pltpu.VMEM((2 * share, rows), BF16),
@@ -273,14 +276,14 @@
     share, width = grad.shape
     _, columns, features = weights[0].shape
 
-    def kernel(place_ref, grad_ref, received_ref, w0, w1, w2, w3, o_ref, g_ref, a_ref):
+    def kernel(place_ref, grad_ref, received_ref, w0, w1, w2, w3, w4, o_ref, g_ref, a_ref):
         core = place_ref[0]
         g_ref[pl.ds(pl.multiple_of(core * share, share), share), :] = grad_ref[...]
         g_ref[pl.ds(pl.multiple_of((1 - core) * share, share), share), :] = received_ref[...]
         a_ref[...] = jnp.zeros_like(a_ref)
-        for outer, w_ref in enumerate((w0, w1, w2, w3)):
-            for inner in range(4):
-                row, column = weight_block(place_ref, outer, inner)
+        for w_ref, (offset, begin, count) in zip((w0, w1, w2, w3, w4), BUFFERS):
+            for inner in range(count):
+                row, column = weight_block(place_ref, offset, begin + inner)
                 g = g_ref[:, pl.ds(pl.multiple_of(column * columns, columns), columns)]
                 a_ref[row] += jnp.dot(g, w_ref[inner], preferred_element_type=F32)
         for row in range(2):
@@ -290,7 +293,7 @@
         kernel,
         out_shape=jax.ShapeDtypeStruct((2 * share, 2 * features), BF16),
         in_specs=[pl.BlockSpec(memory_space=pltpu.SMEM)]
-        + [pl.BlockSpec(memory_space=pltpu.VMEM)] * 6,
+        + [pl.BlockSpec(memory_space=pltpu.VMEM)] * 7,
         out_specs=pl.BlockSpec(memory_space=pltpu.VMEM),
         scratch_shapes=[
             pltpu.VMEM((2 * share, width), BF16),
@@ -349,9 +352,16 @@
     blocks = lax.all_to_all(blocks, CLIP, 0, 0, tiled=True)
     arrived = [exchange(w, lambda i: i ^ (r << (3 if i % 2 == 0 else 1))) for r in range(1, 4)]
     w = jnp.stack([w] + arrived)
-    weights = [w] + [
-        exchange(w, lambda i: i ^ (r << (1 if i % 2 == 0 else 3))) for r in range(1, 4)
-    ]
+
+    def along(step):
+        def partner(i):
+            low = 3 if i % 2 else 1
+            return i + ((((i >> low) + step) & 3) - ((i >> low) & 3) << low)
+
+        return partner
+
+    up, down = exchange(w, along(-1)), exchange(w, along(1))
+    weights = [w, up, down, exchange(up[:2], along(-1)), exchange(down[2:], along(1))]
 
     def columns_first(v):
         v = v.reshape(v.shape[0], 16, 8, own)

time: 185 us -> 172 us (0.930)
  local copies, waits for them, and re-layouts: 23.7 us -> 11.4 us
  waiting for transfers between devices: 50.5 us -> 45.6 us
  Pallas kernels: 27.5 us -> 32.2 us
    all_to_all x1, waiting for transfers between devices: 5.84 us -> 0.01 us  [on_device(): blocks = lax.all_to_all(blocks, CLIP, 0, 0, tiled=True)]
    transpose x3, local copies, waits for them, and re-layouts: 5.7 us -> 0.19 us  [columns_first(): return jnp.transpose(v, (0, 2, 1, 3)).reshape(v.shape[0], -1)]
    unnamed x28 -> x22, local copies, waits for them, and re-layouts: 9.71 us -> 4.61 us
    reshape x3, local copies, waits for them, and re-layouts: 5.12 us -> 0.64 us  [columns_first(): return jnp.transpose(v, (0, 2, 1, 3)).reshape(v.shape[0], -1)]
    slice x0 -> x2, local copies, waits for them, and re-layouts: none -> 4.19 us  [the longest x1 2.13 us: on_device(): down[2:]]
    pallas_call x2, Pallas kernels: 12.7 us -> 16.9 us  [attend(): pl.pallas_call(kernel, out_shape=jax.ShapeDtypeStruct((queries, HEAD_DIM)...]
    ppermute x10 -> x11, waiting for transfers between devices: 31.5 us -> 32.5 us  [exchange(): lax.ppermute(x, SEQ + BRANCH, [(i, partner(i)) for i in range(count)])]
    ppermute x10 -> x11, starting transfers between devices: 35 us -> 35.9 us  [exchange(): lax.ppermute(x, SEQ + BRANCH, [(i, partner(i)) for i in range(count)])]
  transfers between devices with their start and end apart: 13 -> 14, of which waited for: 6 -> 7; matrix products, arithmetic and copies ran while one was open for 11% -> 6% of each run, Pallas kernels for 5% -> 12%
where the time goes in v6:
time: 172 us; the launch traced here: 171 us
  starting transfers between devices  67.4 us (39%)
  waiting for transfers between devices  45.6 us (27%)
  Pallas kernels  32.2 us (19%)
  local copies, waits for them, and re-layouts  11.4 us (7%)
  blocking collectives  8.76 us (5%)
  other arithmetic  3.54 us (2%)
    ppermute x11, starting transfers between devices, exchange(): lax.ppermute(x, SEQ + BRANCH, [(i, partner(i)) for i in range(count)])  35.9 us
    ppermute x11, waiting for transfers between devices, exchange(): lax.ppermute(x, SEQ + BRANCH, [(i, partner(i)) for i in range(count)])  32.5 us
    pallas_call x2, Pallas kernels, attend(): pl.pallas_call(kernel, out_shape=jax.ShapeDtypeStruct((queries, HEAD_DIM)...  16.9 us
    all_to_all x1, starting transfers between devices, on_device(): lax.all_to_all(w, ('c', 'z'), 0, 0, tiled=True).reshape(16 * own, features)  15.8 us
    all_to_all x1, waiting for transfers between devices, on_device(): lax.all_to_all(w, ('c', 'z'), 0, 0, tiled=True).reshape(16 * own, features)  13.1 us
    all_to_all x1, starting transfers between devices, on_device(): blocks = lax.all_to_all(blocks, CLIP, 0, 0, tiled=True)  10.9 us
    all_gather x1, blocking collectives, on_device(): parts = lax.all_gather(cot, BRANCH, axis=0, tiled=False)  8.76 us
    all_to_all x1, starting transfers between devices, on_device(): lax.all_to_all(attended.reshape(HEADS * 2, share, HEAD_DIM), CLIP + ('l',...  4.81 us
  transfers between devices with their start and end apart: 14, of which 7 were waited for; matrix products, arithmetic and copies ran while one was open for 6% of the time, Pallas kernels for 12%

profile of v6, /device:TPU:1, one launch (start us, length us, event | category | flops | bytes accessed | tf_op | source)
XLA Modules:
  0.0 170.5 jit_solution(15358483531626353002)
XLA Ops:
  0.7 1.7 broadcast_in_dim.16
  2.3 15.8 %all-to-all-start = ((bf16[16,24,512]{2,1,0:T(8,128)(2,1)}), bf16[16,24,512]{2,1,0:T(8,128)(2,1)}, u32[]{:S(2)}, u32[]{:S(2)}) async-start(bf16[16,24,512]{2,1,0:T(8,128)(2,1)} %broadcast_in_dim.16), calls=%async_computation | async-start | bytes 786432 | tf_op jit(solution)/shard_map/all_to_all | solution.py:348
  20.5 2.7 %prepare.1 = bf16[16,576,128]{2,1,0:T(8,128)(2,1)} custom-call(bf16[192,2048]{1,0:T(8,128)(2,1)S(1)} %bitcast.30, bf16[192,2048]{1,0:T(8,128)(2,1)S(1)} %bitcast.31, bf16[192,2048]{1,0:T(8,128)(2,1)S(1)} %bitcast.32, f32[192,128]{1,0:T(8,128)S(1)} %get-tuple-element.33.c_ref, f32[192,128]{1,0:T(8,128)S(1)} %get-tuple-element.34.s_ref), custom_call_target="tpu_custom_call" | custom-call | tf_op jit(solution)/shard_map/prepare/pallas_call | solution.py:51
  23.2 13.1 %all-to-all-done = bf16[16,24,512]{2,1,0:T(8,128)(2,1)} async-done(((bf16[16,24,512]{2,1,0:T(8,128)(2,1)}), bf16[16,24,512]{2,1,0:T(8,128)(2,1)}, u32[]{:S(2)}, u32[]{:S(2)}) %all-to-all-start) | async-done | bytes 393248 | tf_op jit(solution)/shard_map/all_to_all | solution.py:348
  36.3 10.9 %all-to-all-start.1 = ((bf16[16,576,128]{2,1,0:T(8,128)(2,1)}), bf16[16,576,128]{2,1,0:T(8,128)(2,1)}, u32[]{:S(2)}, u32[]{:S(2)}) async-start(bf16[16,576,128]{2,1,0:T(8,128)(2,1)} %prepare.1), calls=%async_computation.1 | async-start | bytes 4718592 | tf_op jit(solution)/shard_map/all_to_all | solution.py:352
  48.1 4.5 %collective-permute-start.4 = (bf16[384,512]{1,0:T(8,128)(2,1)}, bf16[384,512]{1,0:T(8,128)(2,1)}, u32[]{:S(2)}, u32[]{:S(2)}) collective-permute-start(bf16[384,512]{1,0:T(8,128)(2,1)} %bitcast.6), channel_id=1, source_target_pairs={{0,24},{1,7},{2,26},{3,5},{4,28},{5,3},{6,30},{7,1},{8,16},{9,15},... | collective-permute-start | bytes 1179656 | tf_op jit(solution)/shard_map/ppermute | solution.py:152
  52.6 2.2 %collective-permute-start.3 = (bf16[384,512]{1,0:T(8,128)(2,1)}, bf16[384,512]{1,0:T(8,128)(2,1)}, u32[]{:S(2)}, u32[]{:S(2)}) collective-permute-start(bf16[384,512]{1,0:T(8,128)(2,1)} %bitcast.6), channel_id=1, source_target_pairs={{0,16},{1,5},{2,18},{3,7},{4,20},{5,1},{6,22},{7,3},{8,24},{9,13},... | collective-permute-start | bytes 1179656 | tf_op jit(solution)/shard_map/ppermute | solution.py:152
  54.8 2.3 %collective-permute-start.2 = (bf16[384,512]{1,0:T(8,128)(2,1)}, bf16[384,512]{1,0:T(8,128)(2,1)}, u32[]{:S(2)}, u32[]{:S(2)}) collective-permute-start(bf16[384,512]{1,0:T(8,128)(2,1)} %bitcast.6), channel_id=1, source_target_pairs={{0,8},{1,3},{2,10},{3,1},{4,12},{5,7},{6,14},{7,5},{8,0},{9,11},{1... | collective-permute-start | bytes 1179656 | tf_op jit(solution)/shard_map/ppermute | solution.py:152
  57.9 1.3 copy.13
  62.1 23.1 %collective-permute-done.4 = bf16[384,512]{1,0:T(8,128)(2,1)} collective-permute-done((bf16[384,512]{1,0:T(8,128)(2,1)}, bf16[384,512]{1,0:T(8,128)(2,1)}, u32[]{:S(2)}, u32[]{:S(2)}) %collective-permute-start.4) | collective-permute-done | bytes 393248 | tf_op jit(solution)/shard_map/ppermute | solution.py:152
  85.2 1.5 pad_maximum_fusion.w0
  86.8 2.9 %collective-permute-start.6 = (bf16[4,384,512]{2,1,0:T(8,128)(2,1)S(1)}, bf16[4,384,512]{2,1,0:T(8,128)(2,1)}, u32[]{:S(2)}, u32[]{:S(2)}) collective-permute-start(bf16[4,384,512]{2,1,0:T(8,128)(2,1)S(1)} %pad_maximum_fusion.w0), channel_id=1, source_target_pairs={{0,2},{1,9},{2,4},{3,11},{4,6},{5,13},{6,0},{7,15},{8,10},{9,17},{... | collective-permute-start | bytes 4718600 | tf_op jit(solution)/shard_map/ppermute | solution.py:152
  89.7 3.6 %collective-permute-start.5 = (bf16[4,384,512]{2,1,0:T(8,128)(2,1)S(1)}, bf16[4,384,512]{2,1,0:T(8,128)(2,1)}, u32[]{:S(2)}, u32[]{:S(2)}) collective-permute-start(bf16[4,384,512]{2,1,0:T(8,128)(2,1)S(1)} %pad_maximum_fusion.w0), channel_id=1, source_target_pairs={{0,6},{1,25},{2,0},{3,27},{4,2},{5,29},{6,4},{7,31},{8,14},{9,1},{... | collective-permute-start | bytes 4718600 | tf_op jit(solution)/shard_map/ppermute | solution.py:152
  93.3 8.0 %attend_first.1 = bf16[1536,128]{1,0:T(8,128)(2,1)S(1)} custom-call(s32[1]{0:T(128)S(6)} %sub.3.part_ref, f32[1]{0:T(128)} %bitcast.4.scale_ref, bf16[16,576,128]{2,1,0:T(8,128)(2,1)} %all-to-all-done.1.b_ref), custom_call_target="tpu_custom_call" | custom-call | flops 2415919104 | bytes 2359296 | tf_op jit(solution)/shard_map/attend_first/pallas_call | solution.py:127
  101.4 5.1 %collective-permute-start = (bf16[1536,128]{1,0:T(8,128)(2,1)S(1)}, bf16[1536,128]{1,0:T(8,128)(2,1)S(1)}, u32[]{:S(2)}, u32[]{:S(2)}) collective-permute-start(bf16[1536,128]{1,0:T(8,128)(2,1)S(1)} %attend_first.1), channel_id=1, source_target_pairs={{0,1},{1,0},{2,3},{3,2},{4,5},{5,4},{6,7},{7,6},{8,9},{9,8},{10,11... | collective-permute-start | bytes 1179656 | tf_op jit(solution)/shard_map/ppermute | solution.py:152
  107.6 8.8 %attend_last.1 = bf16[1536,128]{1,0:T(8,128)(2,1)} custom-call(s32[1]{0:T(128)} %bitcast.part_ref.core_ref, f32[1]{0:T(128)} %bitcast.4.scale_ref, bf16[16,576,128]{2,1,0:T(8,128)(2,1)} %all-to-all-done.1.b_ref, bf16[1536,128]{1,0:T(8,128)(2,1)S(1)} %collective-permute-done.refs_0_), custom_call_target="tpu_custom_call" | custom-call | flops 2415919104 | bytes 2359296 | tf_op jit(solution)/shard_map/attend_last/pallas_call | solution.py:127
  116.4 4.8 %all-to-all-start.2 = ((bf16[32,48,128]{2,1,0:T(8,128)(2,1)}), bf16[32,48,128]{2,1,0:T(8,128)(2,1)}, u32[]{:S(2)}, u32[]{:S(2)}) async-start(bf16[32,48,128]{2,1,0:T(8,128)(2,1)} %bitcast.17), calls=%async_computation.2 | async-start | bytes 786432 | tf_op jit(solution)/shard_map/all_to_all | solution.py:378
  121.3 2.1 %slice.9 = bf16[2,384,512]{2,1,0:T(8,128)(2,1)} slice(bf16[4,384,512]{2,1,0:T(8,128)(2,1)} %collective-permute-done.6.w2), slice={[2:4], [0:384], [0:512]} | slice | bytes 1572864 | tf_op jit(solution)/shard_map/slice | solution.py:364
  123.4 3.1 %collective-permute-start.8 = (bf16[2,384,512]{2,1,0:T(8,128)(2,1)}, bf16[2,384,512]{2,1,0:T(8,128)(2,1)S(1)}, u32[]{:S(2)}, u32[]{:S(2)}) collective-permute-start(bf16[2,384,512]{2,1,0:T(8,128)(2,1)} %slice.9), channel_id=1, source_target_pairs={{0,2},{1,9},{2,4},{3,11},{4,6},{5,13},{6,0},{7,15},{8,10},{9,17},{... | collective-permute-start | bytes 2359304 | tf_op jit(solution)/shard_map/ppermute | solution.py:152
  126.5 2.1 %slice.8 = bf16[2,384,512]{2,1,0:T(8,128)(2,1)} slice(bf16[4,384,512]{2,1,0:T(8,128)(2,1)} %collective-permute-done.5.w1), slice={[0:2], [0:384], [0:512]} | slice | bytes 1572864 | tf_op jit(solution)/shard_map/slice | solution.py:364
  128.5 3.4 %collective-permute-start.7 = (bf16[2,384,512]{2,1,0:T(8,128)(2,1)}, bf16[2,384,512]{2,1,0:T(8,128)(2,1)}, u32[]{:S(2)}, u32[]{:S(2)}) collective-permute-start(bf16[2,384,512]{2,1,0:T(8,128)(2,1)} %slice.8), channel_id=1, source_target_pairs={{0,6},{1,25},{2,0},{3,27},{4,2},{5,29},{6,4},{7,31},{8,14},{9,1},{... | collective-permute-start | bytes 2359304 | tf_op jit(solution)/shard_map/ppermute | solution.py:152
  133.0 2.9 %collective-permute-start.1 = (bf16[48,1024]{1,0:T(8,128)(2,1)S(1)}, bf16[48,1024]{1,0:T(8,128)(2,1)S(1)}, u32[]{:S(2)}, u32[]{:S(2)}) collective-permute-start(bf16[48,1024]{1,0:T(8,128)(2,1)S(1)} %get-tuple-element.21), channel_id=1, source_target_pairs={{0,1},{1,0},{2,3},{3,2},{4,5},{5,4},{6,7},{7,6},{8,9},{9,8},{10,11... | collective-permute-start | bytes 294920 | tf_op jit(solution)/shard_map/ppermute | solution.py:152
  136.0 3.3 %collective-permute-done.8.w4 = bf16[2,384,512]{2,1,0:T(8,128)(2,1)S(1)} collective-permute-done((bf16[2,384,512]{2,1,0:T(8,128)(2,1)}, bf16[2,384,512]{2,1,0:T(8,128)(2,1)S(1)}, u32[]{:S(2)}, u32[]{:S(2)}) %collective-permute-start.8) | collective-permute-done | bytes 786464 | tf_op jit(solution)/shard_map/ppermute | solution.py:152
  139.3 2.6 %collective-permute-done.7.w3 = bf16[2,384,512]{2,1,0:T(8,128)(2,1)} collective-permute-done((bf16[2,384,512]{2,1,0:T(8,128)(2,1)}, bf16[2,384,512]{2,1,0:T(8,128)(2,1)}, u32[]{:S(2)}, u32[]{:S(2)}) %collective-permute-start.7) | collective-permute-done | bytes 786464 | tf_op jit(solution)/shard_map/ppermute | solution.py:152
  141.9 4.3 %project.1 = (f32[48,3072]{1,0:T(8,128)S(1)}, bf16[48,3072]{1,0:T(8,128)(2,1)S(1)}) custom-call(s32[3]{0:T(128)S(1)} %pad_add_fusion.place_ref, bf16[48,1024]{1,0:T(8,128)(2,1)S(1)} %get-tuple-element.20.keep_ref, bf16[48,1024]{1,0:T(8,128)(2,1)S(1)} %collective-permute-done.1.received_ref, bf16[4,384,512]{2,1,0:T(8,128)(2,1)S(1)} %pad_maximum_fusion.w0, ...), custom_call_target="tpu_custom_call" | custom-call | tf_op jit(solution)/shard_map/project/pallas_call | solution.py:211
  146.2 3.7 %collective-permute-start.9 = (bf16[48,3072]{1,0:T(8,128)(2,1)S(1)}, bf16[48,3072]{1,0:T(8,128)(2,1)S(1)}, u32[]{:S(2)}, u32[]{:S(2)}) collective-permute-start(bf16[48,3072]{1,0:T(8,128)(2,1)S(1)} %get-tuple-element.24), channel_id=1, source_target_pairs={{0,1},{1,0},{2,3},{3,2},{4,5},{5,4},{6,7},{7,6},{8,9},{9,8},{10,11... | collective-permute-start | bytes 884744 | tf_op jit(solution)/shard_map/ppermute | solution.py:152
  149.9 1.2 collective-permute-done.9.received_ref
  151.1 2.0 %normalize.1 = (bf16[48,3072]{1,0:T(8,128)(2,1)}, bf16[48,3072]{1,0:T(8,128)(2,1)S(1)}) custom-call(f32[48,3072]{1,0:T(8,128)S(1)} %get-tuple-element.23.own_ref, bf16[48,3072]{1,0:T(8,128)(2,1)S(1)} %collective-permute-done.9.received_ref, f32[48,3072]{1,0:T(8,128)S(1)} %copy-done.5, f32[48,3072]{1,0:T(8,128)S(1)} %copy-done.7, f32[1,3072]{1,0:T(1,128)S(1)} %reshape.43.gain_ref), custom_call_target="tpu_custom_call" | custom-call | tf_op jit(solution)/shard_map/normalize/pallas_call | solution.py:264
  153.1 2.3 %collective-permute-start.10 = (bf16[48,3072]{1,0:T(8,128)(2,1)S(1)}, bf16[48,3072]{1,0:T(8,128)(2,1)S(1)}, u32[]{:S(2)}, u32[]{:S(2)}) collective-permute-start(bf16[48,3072]{1,0:T(8,128)(2,1)S(1)} %get-tuple-element.29.grad_ref), channel_id=1, source_target_pairs={{0,1},{1,0},{2,3},{3,2},{4,5},{5,4},{6,7},{7,6},{8,9},{9,8},{10,11... | collective-permute-start | bytes 884744 | tf_op jit(solution)/shard_map/ppermute | solution.py:152
  156.6 3.5 %project_back.1 = bf16[96,1024]{1,0:T(8,128)(2,1)S(1)} custom-call(s32[3]{0:T(128)S(1)} %pad_add_fusion.place_ref, bf16[48,3072]{1,0:T(8,128)(2,1)S(1)} %get-tuple-element.29.grad_ref, bf16[48,3072]{1,0:T(8,128)(2,1)S(1)} %collective-permute-done.10.received_ref, bf16[4,384,512]{2,1,0:T(8,128)(2,1)S(1)} %pad_maximum_fusion.w0, ...), custom_call_target="tpu_custom_call" | custom-call | tf_op jit(solution)/shard_map/project_back/pallas_call | solution.py:292
  160.1 8.8 %all-gather = bf16[384,1024]{1,0:T(8,128)(2,1)S(1)} all-gather(bf16[96,1024]{1,0:T(8,128)(2,1)S(1)} %project_back.1), channel_id=2, replica_groups=mesh['c'=8,'z'=2,'y'=4,'h'=2,'l'=2,'k'=2] {'l','k'}, dimensions={0}, use_global_device_ids=true | all-gather | bytes 983040 | tf_op jit(solution)/shard_map/all_gather | solution.py:385
  168.9 1.7 scatter_scaled.1
  (46 shorter events, 9.7 us)
Async XLA Ops:
  0.6 56.5 %copy-start = (bf16[192,3072]{1,0:T(8,128)(2,1)S(1)}, bf16[192,3072]{1,0:T(8,128)(2,1)}, u32[]{:S(2)}) copy-start(bf16[192,3072]{1,0:T(8,128)(2,1)} %param.19) | copy-start | bytes 3538948
  0.6 18.7 %copy-start.2 = (bf16[1,192,2048]{2,1,0:T(8,128)(2,1)S(1)}, bf16[1,192,2048]{2,1,0:T(8,128)(2,1)}, u32[]{:S(2)}) copy-start(bf16[1,192,2048]{2,1,0:T(8,128)(2,1)} %param.11) | copy-start | bytes 2359300
  0.7 18.7 %copy-start.1 = (bf16[1,192,2048]{2,1,0:T(8,128)(2,1)S(1)}, bf16[1,192,2048]{2,1,0:T(8,128)(2,1)}, u32[]{:S(2)}) copy-start(bf16[1,192,2048]{2,1,0:T(8,128)(2,1)} %param.10) | copy-start | bytes 2359300
  2.3 34.0 %all-to-all-start = ((bf16[16,24,512]{2,1,0:T(8,128)(2,1)}), bf16[16,24,512]{2,1,0:T(8,128)(2,1)}, u32[]{:S(2)}, u32[]{:S(2)}) async-start(bf16[16,24,512]{2,1,0:T(8,128)(2,1)} %broadcast_in_dim.16), calls=%async_computation | async-start | bytes 786432 | tf_op jit(solution)/shard_map/all_to_all | solution.py:348
  19.4 1.1 copy-start.3
  36.3 11.6 %copy-start.8 = (f32[3072]{0:T(1024)S(1)}, f32[3072]{0:T(1024)}, u32[]{:S(2)}) copy-start(f32[3072]{0:T(1024)} %param.18) | copy-start | bytes 36868
  36.3 57.0 %all-to-all-start.1 = ((bf16[16,576,128]{2,1,0:T(8,128)(2,1)}), bf16[16,576,128]{2,1,0:T(8,128)(2,1)}, u32[]{:S(2)}, u32[]{:S(2)}) async-start(bf16[16,576,128]{2,1,0:T(8,128)(2,1)} %prepare.1), calls=%async_computation.1 | async-start | bytes 4718592 | tf_op jit(solution)/shard_map/all_to_all | solution.py:352
  48.1 37.1 %collective-permute-start.4 = (bf16[384,512]{1,0:T(8,128)(2,1)}, bf16[384,512]{1,0:T(8,128)(2,1)}, u32[]{:S(2)}, u32[]{:S(2)}) collective-permute-start(bf16[384,512]{1,0:T(8,128)(2,1)} %bitcast.6), channel_id=1, source_target_pairs={{0,24},{1,7},{2,26},{3,5},{4,28},{5,3},{6,30},{7,1},{8,16},{9,15},... | collective-permute-start | bytes 1179656 | tf_op jit(solution)/shard_map/ppermute | solution.py:152
  52.6 32.7 %collective-permute-start.3 = (bf16[384,512]{1,0:T(8,128)(2,1)}, bf16[384,512]{1,0:T(8,128)(2,1)}, u32[]{:S(2)}, u32[]{:S(2)}) collective-permute-start(bf16[384,512]{1,0:T(8,128)(2,1)} %bitcast.6), channel_id=1, source_target_pairs={{0,16},{1,5},{2,18},{3,7},{4,20},{5,1},{6,22},{7,3},{8,24},{9,13},... | collective-permute-start | bytes 1179656 | tf_op jit(solution)/shard_map/ppermute | solution.py:152
  54.8 30.5 %collective-permute-start.2 = (bf16[384,512]{1,0:T(8,128)(2,1)}, bf16[384,512]{1,0:T(8,128)(2,1)}, u32[]{:S(2)}, u32[]{:S(2)}) collective-permute-start(bf16[384,512]{1,0:T(8,128)(2,1)} %bitcast.6), channel_id=1, source_target_pairs={{0,8},{1,3},{2,10},{3,1},{4,12},{5,7},{6,14},{7,5},{8,0},{9,11},{1... | collective-permute-start | bytes 1179656 | tf_op jit(solution)/shard_map/ppermute | solution.py:152
  59.3 2.2 %copy-start.9 = (f32[64]{0:T(128)S(1)}, f32[64]{0:T(128)}, u32[]{:S(2)}) copy-start(f32[64]{0:T(128)} %param.15) | copy-start | bytes 772
  59.7 0.9 copy-start.4
  60.6 0.9 copy-start.6
  86.8 34.5 %collective-permute-start.6 = (bf16[4,384,512]{2,1,0:T(8,128)(2,1)S(1)}, bf16[4,384,512]{2,1,0:T(8,128)(2,1)}, u32[]{:S(2)}, u32[]{:S(2)}) collective-permute-start(bf16[4,384,512]{2,1,0:T(8,128)(2,1)S(1)} %pad_maximum_fusion.w0), channel_id=1, source_target_pairs={{0,2},{1,9},{2,4},{3,11},{4,6},{5,13},{6,0},{7,15},{8,10},{9,17},{... | collective-permute-start | bytes 4718600 | tf_op jit(solution)/shard_map/ppermute | solution.py:152
  89.7 36.8 %collective-permute-start.5 = (bf16[4,384,512]{2,1,0:T(8,128)(2,1)S(1)}, bf16[4,384,512]{2,1,0:T(8,128)(2,1)}, u32[]{:S(2)}, u32[]{:S(2)}) collective-permute-start(bf16[4,384,512]{2,1,0:T(8,128)(2,1)S(1)} %pad_maximum_fusion.w0), channel_id=1, source_target_pairs={{0,6},{1,25},{2,0},{3,27},{4,2},{5,29},{6,4},{7,31},{8,14},{9,1},{... | collective-permute-start | bytes 4718600 | tf_op jit(solution)/shard_map/ppermute | solution.py:152
  101.4 6.2 %collective-permute-start = (bf16[1536,128]{1,0:T(8,128)(2,1)S(1)}, bf16[1536,128]{1,0:T(8,128)(2,1)S(1)}, u32[]{:S(2)}, u32[]{:S(2)}) collective-permute-start(bf16[1536,128]{1,0:T(8,128)(2,1)S(1)} %attend_first.1), channel_id=1, source_target_pairs={{0,1},{1,0},{2,3},{3,2},{4,5},{5,4},{6,7},{7,6},{8,9},{9,8},{10,11... | collective-permute-start | bytes 1179656 | tf_op jit(solution)/shard_map/ppermute | solution.py:152
  116.4 15.5 %all-to-all-start.2 = ((bf16[32,48,128]{2,1,0:T(8,128)(2,1)}), bf16[32,48,128]{2,1,0:T(8,128)(2,1)}, u32[]{:S(2)}, u32[]{:S(2)}) async-start(bf16[32,48,128]{2,1,0:T(8,128)(2,1)} %bitcast.17), calls=%async_computation.2 | async-start | bytes 786432 | tf_op jit(solution)/shard_map/all_to_all | solution.py:378
  123.4 15.9 %collective-permute-start.8 = (bf16[2,384,512]{2,1,0:T(8,128)(2,1)}, bf16[2,384,512]{2,1,0:T(8,128)(2,1)S(1)}, u32[]{:S(2)}, u32[]{:S(2)}) collective-permute-start(bf16[2,384,512]{2,1,0:T(8,128)(2,1)} %slice.9), channel_id=1, source_target_pairs={{0,2},{1,9},{2,4},{3,11},{4,6},{5,13},{6,0},{7,15},{8,10},{9,17},{... | collective-permute-start | bytes 2359304 | tf_op jit(solution)/shard_map/ppermute | solution.py:152
  128.5 13.3 %collective-permute-start.7 = (bf16[2,384,512]{2,1,0:T(8,128)(2,1)}, bf16[2,384,512]{2,1,0:T(8,128)(2,1)}, u32[]{:S(2)}, u32[]{:S(2)}) collective-permute-start(bf16[2,384,512]{2,1,0:T(8,128)(2,1)} %slice.8), channel_id=1, source_target_pairs={{0,6},{1,25},{2,0},{3,27},{4,2},{5,29},{6,4},{7,31},{8,14},{9,1},{... | collective-permute-start | bytes 2359304 | tf_op jit(solution)/shard_map/ppermute | solution.py:152
  133.0 8.8 %collective-permute-start.1 = (bf16[48,1024]{1,0:T(8,128)(2,1)S(1)}, bf16[48,1024]{1,0:T(8,128)(2,1)S(1)}, u32[]{:S(2)}, u32[]{:S(2)}) collective-permute-start(bf16[48,1024]{1,0:T(8,128)(2,1)S(1)} %get-tuple-element.21), channel_id=1, source_target_pairs={{0,1},{1,0},{2,3},{3,2},{4,5},{5,4},{6,7},{7,6},{8,9},{9,8},{10,11... | collective-permute-start | bytes 294920 | tf_op jit(solution)/shard_map/ppermute | solution.py:152
  141.9 9.2 %copy-start.5 = (f32[48,3072]{1,0:T(8,128)S(1)}, f32[48,3072]{1,0:T(8,128)}, u32[]{:S(2)}) copy-start(f32[48,3072]{1,0:T(8,128)} %copy-done.4) | copy-start | bytes 1769476
  141.9 9.2 %copy-start.7 = (f32[48,3072]{1,0:T(8,128)S(1)}, f32[48,3072]{1,0:T(8,128)}, u32[]{:S(2)}) copy-start(f32[48,3072]{1,0:T(8,128)} %copy-done.6) | copy-start | bytes 1769476
  146.2 4.9 %collective-permute-start.9 = (bf16[48,3072]{1,0:T(8,128)(2,1)S(1)}, bf16[48,3072]{1,0:T(8,128)(2,1)S(1)}, u32[]{:S(2)}, u32[]{:S(2)}) collective-permute-start(bf16[48,3072]{1,0:T(8,128)(2,1)S(1)} %get-tuple-element.24), channel_id=1, source_target_pairs={{0,1},{1,0},{2,3},{3,2},{4,5},{5,4},{6,7},{7,6},{8,9},{9,8},{10,11... | collective-permute-start | bytes 884744 | tf_op jit(solution)/shard_map/ppermute | solution.py:152
  153.1 3.5 %collective-permute-start.10 = (bf16[48,3072]{1,0:T(8,128)(2,1)S(1)}, bf16[48,3072]{1,0:T(8,128)(2,1)S(1)}, u32[]{:S(2)}, u32[]{:S(2)}) collective-permute-start(bf16[48,3072]{1,0:T(8,128)(2,1)S(1)} %get-tuple-element.29.grad_ref), channel_id=1, source_target_pairs={{0,1},{1,0},{2,3},{3,2},{4,5},{5,4},{6,7},{7,6},{8,9},{9,8},{10,11... | collective-permute-start | bytes 884744 | tf_op jit(solution)/shard_map/ppermute | solution.py:152

commit v7 on v6

--- a/solution.py
+++ b/solution.py
@@ -186,18 +186,19 @@
     return x_there & 1, y_there * 2 + (x_there >> 1)
 
 
-BUFFERS = ((0, 0, 4), (1, 0, 4), (3, 0, 4), (2, 0, 2), (2, 2, 2))
+BUFFERS = tuple((offset, begin, 2) for offset in (0, 1, 3, 2) for begin in (0, 2))
 
 
 def project(place, keep, received, weights):
     share, rows = keep.shape
     _, columns, features = weights[0].shape
 
-    def kernel(place_ref, keep_ref, received_ref, w0, w1, w2, w3, w4, own_ref, send_ref, m_ref, a_ref):
+    def kernel(place_ref, keep_ref, received_ref, *refs):
+        *w_refs, own_ref, send_ref, m_ref, a_ref = refs
         m_ref[0:share, :] = keep_ref[...]
         m_ref[share:, :] = received_ref[...]
         a_ref[...] = jnp.zeros_like(a_ref)
-        for w_ref, (offset, begin, count) in zip((w0, w1, w2, w3, w4), BUFFERS):
+        for w_ref, (offset, begin, count) in zip(w_refs, BUFFERS):
             for inner in range(count):
                 row, column = weight_block(place_ref, offset, begin + inner)
                 m = m_ref[:, pl.ds(pl.multiple_of(row * features, features), features)]
@@ -215,7 +216,7 @@
             jax.ShapeDtypeStruct((share, 8 * columns), BF16),
         ),
         in_specs=[pl.BlockSpec(memory_space=pltpu.SMEM)]
-        + [pl.BlockSpec(memory_space=pltpu.VMEM)] * 7,
+        + [pl.BlockSpec(memory_space=pltpu.VMEM)] * (2 + len(weights)),
         out_specs=(pl.BlockSpec(memory_space=pltpu.VMEM),) * 2,
         scratch_shapes=[
             pltpu.VMEM((2 * share, rows), BF16),
@@ -276,12 +277,13 @@
     share, width = grad.shape
     _, columns, features = weights[0].shape
 
-    def kernel(place_ref, grad_ref, received_ref, w0, w1, w2, w3, w4, o_ref, g_ref, a_ref):
+    def kernel(place_ref, grad_ref, received_ref, *refs):
+        *w_refs, o_ref, g_ref, a_ref = refs
         core = place_ref[0]
         g_ref[pl.ds(pl.multiple_of(core * share, share), share), :] = grad_ref[...]
         g_ref[pl.ds(pl.multiple_of((1 - core) * share, share), share), :] = received_ref[...]
         a_ref[...] = jnp.zeros_like(a_ref)
-        for w_ref, (offset, begin, count) in zip((w0, w1, w2, w3, w4), BUFFERS):
+        for w_ref, (offset, begin, count) in zip(w_refs, BUFFERS):
             for inner in range(count):
                 row, column = weight_block(place_ref, offset, begin + inner)
                 g = g_ref[:, pl.ds(pl.multiple_of(column * columns, columns), columns)]
@@ -293,7 +295,7 @@
         kernel,
         out_shape=jax.ShapeDtypeStruct((2 * share, 2 * features), BF16),
         in_specs=[pl.BlockSpec(memory_space=pltpu.SMEM)]
-        + [pl.BlockSpec(memory_space=pltpu.VMEM)] * 7,
+        + [pl.BlockSpec(memory_space=pltpu.VMEM)] * (2 + len(weights)),
         out_specs=pl.BlockSpec(memory_space=pltpu.VMEM),
         scratch_shapes=[
             pltpu.VMEM((2 * share, width), BF16),
@@ -351,7 +353,7 @@
     w, blocks = lax.optimization_barrier((w, blocks))
     blocks = lax.all_to_all(blocks, CLIP, 0, 0, tiled=True)
     arrived = [exchange(w, lambda i: i ^ (r << (3 if i % 2 == 0 else 1))) for r in range(1, 4)]
-    w = jnp.stack([w] + arrived)
+    low, high = jnp.stack([w, arrived[0]]), jnp.stack(arrived[1:])
 
     def along(step):
         def partner(i):
@@ -360,8 +362,10 @@
 
         return partner
 
-    up, down = exchange(w, along(-1)), exchange(w, along(1))
-    weights = [w, up, down, exchange(up[:2], along(-1)), exchange(down[2:], along(1))]
+    up_low, down_high = exchange(low, along(-1)), exchange(high, along(1))
+    up_high, down_low = exchange(high, along(-1)), exchange(low, along(1))
+    far_low, far_high = exchange(up_low, along(-1)), exchange(down_high, along(1))
+    weights = [low, high, up_low, up_high, down_low, down_high, far_low, far_high]
 
     def columns_first(v):
         v = v.reshape(v.shape[0], 16, 8, own)

time: 172 us -> 178 us (1.035)
  local copies, waits for them, and re-layouts: 11.4 us -> 25.4 us
  waiting for transfers between devices: 45.6 us -> 34.3 us
  starting transfers between devices: 67.4 us -> 72.8 us
  Pallas kernels: 32.2 us -> 28.9 us
    ppermute x11 -> x13, waiting for transfers between devices: 32.5 us -> 17.7 us  [exchange(): lax.ppermute(x, SEQ + BRANCH, [(i, partner(i)) for i in range(count)])]
    unnamed x22 -> x34, local copies, waits for them, and re-layouts: 4.61 us -> 11.5 us
    ppermute x11 -> x13, starting transfers between devices: 35.9 us -> 41.5 us  [exchange(): lax.ppermute(x, SEQ + BRANCH, [(i, partner(i)) for i in range(count)])]
    transpose x3, local copies, waits for them, and re-layouts: 0.19 us -> 5.7 us  [columns_first(): return jnp.transpose(v, (0, 2, 1, 3)).reshape(v.shape[0], -1)]
    reshape x3, local copies, waits for them, and re-layouts: 0.64 us -> 5.13 us  [columns_first(): return jnp.transpose(v, (0, 2, 1, 3)).reshape(v.shape[0], -1)]
    slice x2 -> x0, local copies, waits for them, and re-layouts: 4.19 us -> none  [the longest x1 2.13 us: on_device(): down[2:]]
    all_to_all x1, waiting for transfers between devices: 0.01 us -> 3.56 us  [on_device(): blocks = lax.all_to_all(blocks, CLIP, 0, 0, tiled=True)]
    pallas_call x2, Pallas kernels: 16.9 us -> 13.7 us  [attend(): pl.pallas_call(kernel, out_shape=jax.ShapeDtypeStruct((queries, HEAD_DIM)...]
  transfers between devices with their start and end apart: 14 -> 16, of which waited for: 7 -> 8; matrix products, arithmetic and copies ran while one was open for 6% -> 12% of each run, Pallas kernels for 12% -> 10%
where the time goes in v7:
time: 178 us; the launch traced here: 176 us
  starting transfers between devices  72.8 us (41%)
  waiting for transfers between devices  34.3 us (19%)
  Pallas kernels  28.9 us (16%)
  local copies, waits for them, and re-layouts  25.4 us (14%)
  blocking collectives  8.71 us (5%)
  other arithmetic  4.37 us (2%)
    ppermute x13, starting transfers between devices, exchange(): lax.ppermute(x, SEQ + BRANCH, [(i, partner(i)) for i in range(count)])  41.5 us
    ppermute x13, waiting for transfers between devices, exchange(): lax.ppermute(x, SEQ + BRANCH, [(i, partner(i)) for i in range(count)])  17.7 us
    all_to_all x1, starting transfers between devices, on_device(): lax.all_to_all(w, ('c', 'z'), 0, 0, tiled=True).reshape(16 * own, features)  15.8 us
    pallas_call x2, Pallas kernels, attend(): pl.pallas_call(kernel, out_shape=jax.ShapeDtypeStruct((queries, HEAD_DIM)...  13.7 us
    all_to_all x1, waiting for transfers between devices, on_device(): lax.all_to_all(w, ('c', 'z'), 0, 0, tiled=True).reshape(16 * own, features)  13.1 us
    unnamed x34, local copies, waits for them, and re-layouts  11.5 us
    all_to_all x1, starting transfers between devices, on_device(): blocks = lax.all_to_all(blocks, CLIP, 0, 0, tiled=True)  10.9 us
    all_gather x1, blocking collectives, on_device(): parts = lax.all_gather(cot, BRANCH, axis=0, tiled=False)  8.71 us
  transfers between devices with their start and end apart: 16, of which 8 were waited for; matrix products, arithmetic and copies ran while one was open for 12% of the time, Pallas kernels for 10%

profile of v7, /device:TPU:1, one launch (start us, length us, event | category | flops | bytes accessed | tf_op | source)
XLA Modules:
  0.0 176.2 jit_solution(6477229448979294498)
XLA Ops:
  2.3 15.8 %all-to-all-start = ((bf16[16,24,512]{2,1,0:T(8,128)(2,1)}), bf16[16,24,512]{2,1,0:T(8,128)(2,1)}, u32[]{:S(2)}, u32[]{:S(2)}) async-start(bf16[16,24,512]{2,1,0:T(8,128)(2,1)} %broadcast_in_dim.16), calls=%async_computation | async-start | bytes 786432 | tf_op jit(solution)/shard_map/all_to_all | solution.py:350
  20.5 2.6 %prepare.1 = bf16[16,576,128]{2,1,0:T(8,128)(2,1)} custom-call(bf16[192,2048]{1,0:T(8,128)(2,1)S(1)} %bitcast.30, bf16[192,2048]{1,0:T(8,128)(2,1)S(1)} %bitcast.31, bf16[192,2048]{1,0:T(8,128)(2,1)S(1)} %bitcast.32, f32[192,128]{1,0:T(8,128)S(1)} %get-tuple-element.33.c_ref, f32[192,128]{1,0:T(8,128)S(1)} %get-tuple-element.34.s_ref), custom_call_target="tpu_custom_call" | custom-call | tf_op jit(solution)/shard_map/prepare/pallas_call | solution.py:51
  23.2 13.1 %all-to-all-done = bf16[16,24,512]{2,1,0:T(8,128)(2,1)} async-done(((bf16[16,24,512]{2,1,0:T(8,128)(2,1)}), bf16[16,24,512]{2,1,0:T(8,128)(2,1)}, u32[]{:S(2)}, u32[]{:S(2)}) %all-to-all-start) | async-done | bytes 393248 | tf_op jit(solution)/shard_map/all_to_all | solution.py:350
  36.3 10.9 %all-to-all-start.1 = ((bf16[16,576,128]{2,1,0:T(8,128)(2,1)}), bf16[16,576,128]{2,1,0:T(8,128)(2,1)S(1)}, u32[]{:S(2)}, u32[]{:S(2)}) async-start(bf16[16,576,128]{2,1,0:T(8,128)(2,1)} %prepare.1), calls=%async_computation.1 | async-start | bytes 4718592 | tf_op jit(solution)/shard_map/all_to_all | solution.py:354
  51.7 2.1 %copy.20 = bf16[48,3072]{0,1:T(8,128)(2,1)} copy(bf16[48,3072]{1,0:T(8,128)(2,1)} %constant_dynamic-slice_fusion) | data formatting | bytes 589824
  53.9 2.1 %copy.16 = bf16[48,8,16,24]{0,3,2,1:T(8,128)(2,1)} copy(bf16[48,8,16,24]{0,3,1,2:T(8,128)(2,1)} %bitcast.33) | data formatting | bytes 589824 | tf_op jit(solution)/shard_map/transpose | solution.py:372
  58.1 2.1 %copy.13 = bf16[48,3072]{0,1:T(8,128)(2,1)} copy(bf16[48,3072]{1,0:T(8,128)(2,1)} %param.17) | data formatting | bytes 589824 | tf_op args[7]
  60.2 2.1 %copy.14 = bf16[48,8,16,24]{0,3,2,1:T(8,128)(2,1)} copy(bf16[48,8,16,24]{0,3,1,2:T(8,128)(2,1)} %bitcast.36) | data formatting | bytes 589824 | tf_op jit(solution)/shard_map/transpose | solution.py:372
  62.3 2.1 %copy.18.frozen_ref = bf16[48,3072]{1,0:T(8,128)(2,1)} copy(bf16[48,3072]{0,1:T(8,128)(2,1)} %bitcast.35) | data formatting | bytes 589824 | tf_op jit(solution)/shard_map/reshape | solution.py:372
  68.7 2.2 %collective-permute-start.2 = (bf16[384,512]{1,0:T(8,128)(2,1)}, bf16[384,512]{1,0:T(8,128)(2,1)}, u32[]{:S(2)}, u32[]{:S(2)}) collective-permute-start(bf16[384,512]{1,0:T(8,128)(2,1)} %bitcast.6), channel_id=1, source_target_pairs={{0,8},{1,3},{2,10},{3,1},{4,12},{5,7},{6,14},{7,5},{8,0},{9,11},{1... | collective-permute-start | bytes 1179656 | tf_op jit(solution)/shard_map/ppermute | solution.py:152
  70.9 3.6 %all-to-all-done.1.b_ref = bf16[16,576,128]{2,1,0:T(8,128)(2,1)S(1)} async-done(((bf16[16,576,128]{2,1,0:T(8,128)(2,1)}), bf16[16,576,128]{2,1,0:T(8,128)(2,1)S(1)}, u32[]{:S(2)}, u32[]{:S(2)}) %all-to-all-start.1) | async-done | bytes 2359328 | tf_op jit(solution)/shard_map/all_to_all | solution.py:354
  74.5 6.4 %attend_first.1 = bf16[1536,128]{1,0:T(8,128)(2,1)S(1)} custom-call(s32[1]{0:T(128)S(6)} %sub.3.part_ref, f32[1]{0:T(128)} %bitcast.4.scale_ref, bf16[16,576,128]{2,1,0:T(8,128)(2,1)S(1)} %all-to-all-done.1.b_ref), custom_call_target="tpu_custom_call" | custom-call | flops 2415919104 | bytes 2359296 | tf_op jit(solution)/shard_map/attend_first/pallas_call | solution.py:127
  80.9 5.4 %collective-permute-start = (bf16[1536,128]{1,0:T(8,128)(2,1)S(1)}, bf16[1536,128]{1,0:T(8,128)(2,1)S(1)}, u32[]{:S(2)}, u32[]{:S(2)}) collective-permute-start(bf16[1536,128]{1,0:T(8,128)(2,1)S(1)} %attend_first.1), channel_id=1, source_target_pairs={{0,1},{1,0},{2,3},{3,2},{4,5},{5,4},{6,7},{7,6},{8,9},{9,8},{10,11... | collective-permute-start | bytes 1179656 | tf_op jit(solution)/shard_map/ppermute | solution.py:152
  86.3 4.7 %collective-permute-start.4 = (bf16[384,512]{1,0:T(8,128)(2,1)}, bf16[384,512]{1,0:T(8,128)(2,1)S(1)}, u32[]{:S(2)}, u32[]{:S(2)}) collective-permute-start(bf16[384,512]{1,0:T(8,128)(2,1)} %bitcast.6), channel_id=1, source_target_pairs={{0,24},{1,7},{2,26},{3,5},{4,28},{5,3},{6,30},{7,1},{8,16},{9,15},... | collective-permute-start | bytes 1179656 | tf_op jit(solution)/shard_map/ppermute | solution.py:152
  91.0 3.7 %collective-permute-start.3 = (bf16[384,512]{1,0:T(8,128)(2,1)}, bf16[384,512]{1,0:T(8,128)(2,1)S(1)}, u32[]{:S(2)}, u32[]{:S(2)}) collective-permute-start(bf16[384,512]{1,0:T(8,128)(2,1)} %bitcast.6), channel_id=1, source_target_pairs={{0,16},{1,5},{2,18},{3,7},{4,20},{5,1},{6,22},{7,3},{8,24},{9,13},... | collective-permute-start | bytes 1179656 | tf_op jit(solution)/shard_map/ppermute | solution.py:152
  96.0 4.7 %collective-permute-start.5 = (bf16[2,384,512]{2,1,0:T(8,128)(2,1)S(1)}, bf16[2,384,512]{2,1,0:T(8,128)(2,1)S(1)}, u32[]{:S(2)}, u32[]{:S(2)}) collective-permute-start(bf16[2,384,512]{2,1,0:T(8,128)(2,1)S(1)} %pad_maximum_fusion.refs_0_), channel_id=1, source_target_pairs={{0,6},{1,25},{2,0},{3,27},{4,2},{5,29},{6,4},{7,31},{8,14},{9,1},{... | collective-permute-start | bytes 2359304 | tf_op jit(solution)/shard_map/ppermute | solution.py:152
  102.4 7.2 %attend_last.1 = bf16[1536,128]{1,0:T(8,128)(2,1)} custom-call(s32[1]{0:T(128)} %bitcast.part_ref.core_ref, f32[1]{0:T(128)} %bitcast.4.scale_ref, bf16[16,576,128]{2,1,0:T(8,128)(2,1)S(1)} %copy-done.2, bf16[1536,128]{1,0:T(8,128)(2,1)S(1)} %collective-permute-done.refs_0_), custom_call_target="tpu_custom_call" | custom-call | flops 2415919104 | bytes 2359296 | tf_op jit(solution)/shard_map/attend_last/pallas_call | solution.py:127
  109.6 4.6 %all-to-all-start.2 = ((bf16[32,48,128]{2,1,0:T(8,128)(2,1)}), bf16[32,48,128]{2,1,0:T(8,128)(2,1)}, u32[]{:S(2)}, u32[]{:S(2)}) async-start(bf16[32,48,128]{2,1,0:T(8,128)(2,1)} %bitcast.17), calls=%async_computation.2 | async-start | bytes 786432 | tf_op jit(solution)/shard_map/all_to_all | solution.py:382
  116.3 3.0 %collective-permute-start.8 = (bf16[2,384,512]{2,1,0:T(8,128)(2,1)S(1)}, bf16[2,384,512]{2,1,0:T(8,128)(2,1)}, u32[]{:S(2)}, u32[]{:S(2)}) collective-permute-start(bf16[2,384,512]{2,1,0:T(8,128)(2,1)S(1)} %pad_maximum_fusion.1.refs_1_), channel_id=1, source_target_pairs={{0,2},{1,9},{2,4},{3,11},{4,6},{5,13},{6,0},{7,15},{8,10},{9,17},{... | collective-permute-start | bytes 2359304 | tf_op jit(solution)/shard_map/ppermute | solution.py:152
  119.3 3.1 %collective-permute-start.7 = (bf16[2,384,512]{2,1,0:T(8,128)(2,1)S(1)}, bf16[2,384,512]{2,1,0:T(8,128)(2,1)}, u32[]{:S(2)}, u32[]{:S(2)}) collective-permute-start(bf16[2,384,512]{2,1,0:T(8,128)(2,1)S(1)} %pad_maximum_fusion.refs_0_), channel_id=1, source_target_pairs={{0,2},{1,9},{2,4},{3,11},{4,6},{5,13},{6,0},{7,15},{8,10},{9,17},{... | collective-permute-start | bytes 2359304 | tf_op jit(solution)/shard_map/ppermute | solution.py:152
  122.5 3.4 %collective-permute-start.6 = (bf16[2,384,512]{2,1,0:T(8,128)(2,1)S(1)}, bf16[2,384,512]{2,1,0:T(8,128)(2,1)}, u32[]{:S(2)}, u32[]{:S(2)}) collective-permute-start(bf16[2,384,512]{2,1,0:T(8,128)(2,1)S(1)} %pad_maximum_fusion.1.refs_1_), channel_id=1, source_target_pairs={{0,6},{1,25},{2,0},{3,27},{4,2},{5,29},{6,4},{7,31},{8,14},{9,1},{... | collective-permute-start | bytes 2359304 | tf_op jit(solution)/shard_map/ppermute | solution.py:152
  125.8 2.3 %collective-permute-start.9 = (bf16[2,384,512]{2,1,0:T(8,128)(2,1)S(1)}, bf16[2,384,512]{2,1,0:T(8,128)(2,1)}, u32[]{:S(2)}, u32[]{:S(2)}) collective-permute-start(bf16[2,384,512]{2,1,0:T(8,128)(2,1)S(1)} %collective-permute-done.5.refs_2_), channel_id=1, source_target_pairs={{0,6},{1,25},{2,0},{3,27},{4,2},{5,29},{6,4},{7,31},{8,14},{9,1},{... | collective-permute-start | bytes 2359304 | tf_op jit(solution)/shard_map/ppermute | solution.py:152
  128.2 4.3 %collective-permute-done.8.refs_5_ = bf16[2,384,512]{2,1,0:T(8,128)(2,1)} collective-permute-done((bf16[2,384,512]{2,1,0:T(8,128)(2,1)S(1)}, bf16[2,384,512]{2,1,0:T(8,128)(2,1)}, u32[]{:S(2)}, u32[]{:S(2)}) %collective-permute-start.8) | collective-permute-done | bytes 786464 | tf_op jit(solution)/shard_map/ppermute | solution.py:152
  135.4 2.5 %collective-permute-start.1 = (bf16[48,1024]{1,0:T(8,128)(2,1)S(1)}, bf16[48,1024]{1,0:T(8,128)(2,1)S(1)}, u32[]{:S(2)}, u32[]{:S(2)}) collective-permute-start(bf16[48,1024]{1,0:T(8,128)(2,1)S(1)} %get-tuple-element.21), channel_id=1, source_target_pairs={{0,1},{1,0},{2,3},{3,2},{4,5},{5,4},{6,7},{7,6},{8,9},{9,8},{10,11... | collective-permute-start | bytes 294920 | tf_op jit(solution)/shard_map/ppermute | solution.py:152
  138.1 2.8 %collective-permute-done.7.refs_4_ = bf16[2,384,512]{2,1,0:T(8,128)(2,1)} collective-permute-done((bf16[2,384,512]{2,1,0:T(8,128)(2,1)S(1)}, bf16[2,384,512]{2,1,0:T(8,128)(2,1)}, u32[]{:S(2)}, u32[]{:S(2)}) %collective-permute-start.7) | collective-permute-done | bytes 786464 | tf_op jit(solution)/shard_map/ppermute | solution.py:152
  140.9 3.1 %collective-permute-done.9.refs_6_ = bf16[2,384,512]{2,1,0:T(8,128)(2,1)} collective-permute-done((bf16[2,384,512]{2,1,0:T(8,128)(2,1)S(1)}, bf16[2,384,512]{2,1,0:T(8,128)(2,1)}, u32[]{:S(2)}, u32[]{:S(2)}) %collective-permute-start.9) | collective-permute-done | bytes 786464 | tf_op jit(solution)/shard_map/ppermute | solution.py:152
  144.0 5.0 %collective-permute-done.10.refs_7_ = bf16[2,384,512]{2,1,0:T(8,128)(2,1)} collective-permute-done((bf16[2,384,512]{2,1,0:T(8,128)(2,1)}, bf16[2,384,512]{2,1,0:T(8,128)(2,1)}, u32[]{:S(2)}, u32[]{:S(2)}) %collective-permute-start.10) | collective-permute-done | bytes 786464 | tf_op jit(solution)/shard_map/ppermute | solution.py:152
  149.0 4.3 %project.1 = (f32[48,3072]{1,0:T(8,128)S(1)}, bf16[48,3072]{1,0:T(8,128)(2,1)S(1)}) custom-call(s32[3]{0:T(128)S(1)} %pad_add_fusion.place_ref, bf16[48,1024]{1,0:T(8,128)(2,1)S(1)} %get-tuple-element.20.keep_ref, bf16[48,1024]{1,0:T(8,128)(2,1)S(1)} %collective-permute-done.1.received_ref, bf16[2,384,512]{2,1,0:T(8,128)(2,1)S(1)} %pad_maximum_fusion.refs_0_, ...), custom_call_target="tpu_custom_call" | custom-call | tf_op jit(solution)/shard_map/project/pallas_call | solution.py:212
  153.4 2.3 %collective-permute-start.11 = (bf16[48,3072]{1,0:T(8,128)(2,1)S(1)}, bf16[48,3072]{1,0:T(8,128)(2,1)S(1)}, u32[]{:S(2)}, u32[]{:S(2)}) collective-permute-start(bf16[48,3072]{1,0:T(8,128)(2,1)S(1)} %get-tuple-element.24), channel_id=1, source_target_pairs={{0,1},{1,0},{2,3},{3,2},{4,5},{5,4},{6,7},{7,6},{8,9},{9,8},{10,11... | collective-permute-start | bytes 884744 | tf_op jit(solution)/shard_map/ppermute | solution.py:152
  158.9 2.3 %collective-permute-start.12 = (bf16[48,3072]{1,0:T(8,128)(2,1)S(1)}, bf16[48,3072]{1,0:T(8,128)(2,1)S(1)}, u32[]{:S(2)}, u32[]{:S(2)}) collective-permute-start(bf16[48,3072]{1,0:T(8,128)(2,1)S(1)} %get-tuple-element.29.grad_ref), channel_id=1, source_target_pairs={{0,1},{1,0},{2,3},{3,2},{4,5},{5,4},{6,7},{7,6},{8,9},{9,8},{10,11... | collective-permute-start | bytes 884744 | tf_op jit(solution)/shard_map/ppermute | solution.py:152
  162.3 3.5 %project_back.1 = bf16[96,1024]{1,0:T(8,128)(2,1)S(1)} custom-call(s32[3]{0:T(128)S(1)} %pad_add_fusion.place_ref, bf16[48,3072]{1,0:T(8,128)(2,1)S(1)} %get-tuple-element.29.grad_ref, bf16[48,3072]{1,0:T(8,128)(2,1)S(1)} %collective-permute-done.12.received_ref, bf16[2,384,512]{2,1,0:T(8,128)(2,1)S(1)} %pad_maximum_fusion.refs_0_, ...), custom_call_target="tpu_custom_call" | custom-call | tf_op jit(solution)/shard_map/project_back/pallas_call | solution.py:294
  165.8 8.7 %all-gather = bf16[384,1024]{1,0:T(8,128)(2,1)S(1)} all-gather(bf16[96,1024]{1,0:T(8,128)(2,1)S(1)} %project_back.1), channel_id=2, replica_groups=mesh['c'=8,'z'=2,'y'=4,'h'=2,'l'=2,'k'=2] {'l','k'}, dimensions={0}, use_global_device_ids=true | all-gather | bytes 983040 | tf_op jit(solution)/shard_map/all_gather | solution.py:389
  (61 shorter events, 28.4 us)
Async XLA Ops:
  0.6 50.4 %copy-start = (bf16[192,3072]{1,0:T(8,128)(2,1)S(1)}, bf16[192,3072]{1,0:T(8,128)(2,1)}, u32[]{:S(2)}) copy-start(bf16[192,3072]{1,0:T(8,128)(2,1)} %param.19) | copy-start | bytes 3538948
  0.6 18.7 %copy-start.6 = (bf16[1,192,2048]{2,1,0:T(8,128)(2,1)S(1)}, bf16[1,192,2048]{2,1,0:T(8,128)(2,1)}, u32[]{:S(2)}) copy-start(bf16[1,192,2048]{2,1,0:T(8,128)(2,1)} %param.11) | copy-start | bytes 2359300
  0.7 18.7 %copy-start.5 = (bf16[1,192,2048]{2,1,0:T(8,128)(2,1)S(1)}, bf16[1,192,2048]{2,1,0:T(8,128)(2,1)}, u32[]{:S(2)}) copy-start(bf16[1,192,2048]{2,1,0:T(8,128)(2,1)} %param.10) | copy-start | bytes 2359300
  2.3 34.0 %all-to-all-start = ((bf16[16,24,512]{2,1,0:T(8,128)(2,1)}), bf16[16,24,512]{2,1,0:T(8,128)(2,1)}, u32[]{:S(2)}, u32[]{:S(2)}) async-start(bf16[16,24,512]{2,1,0:T(8,128)(2,1)} %broadcast_in_dim.16), calls=%async_computation | async-start | bytes 786432 | tf_op jit(solution)/shard_map/all_to_all | solution.py:350
  19.4 1.1 copy-start.7
  36.3 11.5 %copy-start.14 = (f32[3072]{0:T(1024)S(1)}, f32[3072]{0:T(1024)}, u32[]{:S(2)}) copy-start(f32[3072]{0:T(1024)} %param.18) | copy-start | bytes 36868
  36.3 38.2 %all-to-all-start.1 = ((bf16[16,576,128]{2,1,0:T(8,128)(2,1)}), bf16[16,576,128]{2,1,0:T(8,128)(2,1)S(1)}, u32[]{:S(2)}, u32[]{:S(2)}) async-start(bf16[16,576,128]{2,1,0:T(8,128)(2,1)} %prepare.1), calls=%async_computation.1 | async-start | bytes 4718592 | tf_op jit(solution)/shard_map/all_to_all | solution.py:354
  58.1 10.0 %copy-start.15 = (f32[64]{0:T(128)S(1)}, f32[64]{0:T(128)}, u32[]{:S(2)}) copy-start(f32[64]{0:T(128)} %param.15) | copy-start | bytes 772
  64.4 1.0 copy-start.3
  65.4 1.0 copy-start.4
  66.4 0.8 copy-start.8
  67.2 0.8 copy-start.10
  68.7 26.0 %collective-permute-start.2 = (bf16[384,512]{1,0:T(8,128)(2,1)}, bf16[384,512]{1,0:T(8,128)(2,1)}, u32[]{:S(2)}, u32[]{:S(2)}) collective-permute-start(bf16[384,512]{1,0:T(8,128)(2,1)} %bitcast.6), channel_id=1, source_target_pairs={{0,8},{1,3},{2,10},{3,1},{4,12},{5,7},{6,14},{7,5},{8,0},{9,11},{1... | collective-permute-start | bytes 1179656 | tf_op jit(solution)/shard_map/ppermute | solution.py:152
  74.5 6.4 %copy-start.1 = (bf16[16,576,128]{2,1,0:T(8,128)(2,1)}, bf16[16,576,128]{2,1,0:T(8,128)(2,1)S(1)}, u32[]{:S(2)}) copy-start(bf16[16,576,128]{2,1,0:T(8,128)(2,1)S(1)} %all-to-all-done.1.b_ref) | copy-start | bytes 7077892
  80.9 19.8 %collective-permute-start = (bf16[1536,128]{1,0:T(8,128)(2,1)S(1)}, bf16[1536,128]{1,0:T(8,128)(2,1)S(1)}, u32[]{:S(2)}, u32[]{:S(2)}) collective-permute-start(bf16[1536,128]{1,0:T(8,128)(2,1)S(1)} %attend_first.1), channel_id=1, source_target_pairs={{0,1},{1,0},{2,3},{3,2},{4,5},{5,4},{6,7},{7,6},{8,9},{9,8},{10,11... | collective-permute-start | bytes 1179656 | tf_op jit(solution)/shard_map/ppermute | solution.py:152
  86.3 27.9 %collective-permute-start.4 = (bf16[384,512]{1,0:T(8,128)(2,1)}, bf16[384,512]{1,0:T(8,128)(2,1)S(1)}, u32[]{:S(2)}, u32[]{:S(2)}) collective-permute-start(bf16[384,512]{1,0:T(8,128)(2,1)} %bitcast.6), channel_id=1, source_target_pairs={{0,24},{1,7},{2,26},{3,5},{4,28},{5,3},{6,30},{7,1},{8,16},{9,15},... | collective-permute-start | bytes 1179656 | tf_op jit(solution)/shard_map/ppermute | solution.py:152
  91.0 23.2 %collective-permute-start.3 = (bf16[384,512]{1,0:T(8,128)(2,1)}, bf16[384,512]{1,0:T(8,128)(2,1)S(1)}, u32[]{:S(2)}, u32[]{:S(2)}) collective-permute-start(bf16[384,512]{1,0:T(8,128)(2,1)} %bitcast.6), channel_id=1, source_target_pairs={{0,16},{1,5},{2,18},{3,7},{4,20},{5,1},{6,22},{7,3},{8,24},{9,13},... | collective-permute-start | bytes 1179656 | tf_op jit(solution)/shard_map/ppermute | solution.py:152
  96.0 29.9 %collective-permute-start.5 = (bf16[2,384,512]{2,1,0:T(8,128)(2,1)S(1)}, bf16[2,384,512]{2,1,0:T(8,128)(2,1)S(1)}, u32[]{:S(2)}, u32[]{:S(2)}) collective-permute-start(bf16[2,384,512]{2,1,0:T(8,128)(2,1)S(1)} %pad_maximum_fusion.refs_0_), channel_id=1, source_target_pairs={{0,6},{1,25},{2,0},{3,27},{4,2},{5,29},{6,4},{7,31},{8,14},{9,1},{... | collective-permute-start | bytes 2359304 | tf_op jit(solution)/shard_map/ppermute | solution.py:152
  100.7 1.7 copy-start.2
  109.6 24.7 %all-to-all-start.2 = ((bf16[32,48,128]{2,1,0:T(8,128)(2,1)}), bf16[32,48,128]{2,1,0:T(8,128)(2,1)}, u32[]{:S(2)}, u32[]{:S(2)}) async-start(bf16[32,48,128]{2,1,0:T(8,128)(2,1)} %bitcast.17), calls=%async_computation.2 | async-start | bytes 786432 | tf_op jit(solution)/shard_map/all_to_all | solution.py:382
  114.2 0.8 copy-start.12
  114.3 0.9 copy-start.13
  116.3 16.1 %collective-permute-start.8 = (bf16[2,384,512]{2,1,0:T(8,128)(2,1)S(1)}, bf16[2,384,512]{2,1,0:T(8,128)(2,1)}, u32[]{:S(2)}, u32[]{:S(2)}) collective-permute-start(bf16[2,384,512]{2,1,0:T(8,128)(2,1)S(1)} %pad_maximum_fusion.1.refs_1_), channel_id=1, source_target_pairs={{0,2},{1,9},{2,4},{3,11},{4,6},{5,13},{6,0},{7,15},{8,10},{9,17},{... | collective-permute-start | bytes 2359304 | tf_op jit(solution)/shard_map/ppermute | solution.py:152
  119.3 21.6 %collective-permute-start.7 = (bf16[2,384,512]{2,1,0:T(8,128)(2,1)S(1)}, bf16[2,384,512]{2,1,0:T(8,128)(2,1)}, u32[]{:S(2)}, u32[]{:S(2)}) collective-permute-start(bf16[2,384,512]{2,1,0:T(8,128)(2,1)S(1)} %pad_maximum_fusion.refs_0_), channel_id=1, source_target_pairs={{0,2},{1,9},{2,4},{3,11},{4,6},{5,13},{6,0},{7,15},{8,10},{9,17},{... | collective-permute-start | bytes 2359304 | tf_op jit(solution)/shard_map/ppermute | solution.py:152
  122.5 18.4 %collective-permute-start.6 = (bf16[2,384,512]{2,1,0:T(8,128)(2,1)S(1)}, bf16[2,384,512]{2,1,0:T(8,128)(2,1)}, u32[]{:S(2)}, u32[]{:S(2)}) collective-permute-start(bf16[2,384,512]{2,1,0:T(8,128)(2,1)S(1)} %pad_maximum_fusion.1.refs_1_), channel_id=1, source_target_pairs={{0,6},{1,25},{2,0},{3,27},{4,2},{5,29},{6,4},{7,31},{8,14},{9,1},{... | collective-permute-start | bytes 2359304 | tf_op jit(solution)/shard_map/ppermute | solution.py:152
  125.8 18.2 %collective-permute-start.9 = (bf16[2,384,512]{2,1,0:T(8,128)(2,1)S(1)}, bf16[2,384,512]{2,1,0:T(8,128)(2,1)}, u32[]{:S(2)}, u32[]{:S(2)}) collective-permute-start(bf16[2,384,512]{2,1,0:T(8,128)(2,1)S(1)} %collective-permute-done.5.refs_2_), channel_id=1, source_target_pairs={{0,6},{1,25},{2,0},{3,27},{4,2},{5,29},{6,4},{7,31},{8,14},{9,1},{... | collective-permute-start | bytes 2359304 | tf_op jit(solution)/shard_map/ppermute | solution.py:152
  132.4 16.6 %collective-permute-start.10 = (bf16[2,384,512]{2,1,0:T(8,128)(2,1)}, bf16[2,384,512]{2,1,0:T(8,128)(2,1)}, u32[]{:S(2)}, u32[]{:S(2)}) collective-permute-start(bf16[2,384,512]{2,1,0:T(8,128)(2,1)} %collective-permute-done.8.refs_5_), channel_id=1, source_target_pairs={{0,2},{1,9},{2,4},{3,11},{4,6},{5,13},{6,0},{7,15},{8,10},{9,17},{... | collective-permute-start | bytes 2359304 | tf_op jit(solution)/shard_map/ppermute | solution.py:152
  135.4 13.6 %collective-permute-start.1 = (bf16[48,1024]{1,0:T(8,128)(2,1)S(1)}, bf16[48,1024]{1,0:T(8,128)(2,1)S(1)}, u32[]{:S(2)}, u32[]{:S(2)}) collective-permute-start(bf16[48,1024]{1,0:T(8,128)(2,1)S(1)} %get-tuple-element.21), channel_id=1, source_target_pairs={{0,1},{1,0},{2,3},{3,2},{4,5},{5,4},{6,7},{7,6},{8,9},{9,8},{10,11... | collective-permute-start | bytes 294920 | tf_op jit(solution)/shard_map/ppermute | solution.py:152
  149.0 7.8 %copy-start.9 = (f32[48,3072]{1,0:T(8,128)S(1)}, f32[48,3072]{1,0:T(8,128)}, u32[]{:S(2)}) copy-start(f32[48,3072]{1,0:T(8,128)} %copy-done.8) | copy-start | bytes 1769476
  149.0 7.8 %copy-start.11 = (f32[48,3072]{1,0:T(8,128)S(1)}, f32[48,3072]{1,0:T(8,128)}, u32[]{:S(2)}) copy-start(f32[48,3072]{1,0:T(8,128)} %copy-done.10) | copy-start | bytes 1769476
  153.4 3.5 %collective-permute-start.11 = (bf16[48,3072]{1,0:T(8,128)(2,1)S(1)}, bf16[48,3072]{1,0:T(8,128)(2,1)S(1)}, u32[]{:S(2)}, u32[]{:S(2)}) collective-permute-start(bf16[48,3072]{1,0:T(8,128)(2,1)S(1)} %get-tuple-element.24), channel_id=1, source_target_pairs={{0,1},{1,0},{2,3},{3,2},{4,5},{5,4},{6,7},{7,6},{8,9},{9,8},{10,11... | collective-permute-start | bytes 884744 | tf_op jit(solution)/shard_map/ppermute | solution.py:152
  158.9 3.5 %collective-permute-start.12 = (bf16[48,3072]{1,0:T(8,128)(2,1)S(1)}, bf16[48,3072]{1,0:T(8,128)(2,1)S(1)}, u32[]{:S(2)}, u32[]{:S(2)}) collective-permute-start(bf16[48,3072]{1,0:T(8,128)(2,1)S(1)} %get-tuple-element.29.grad_ref), channel_id=1, source_target_pairs={{0,1},{1,0},{2,3},{3,2},{4,5},{5,4},{6,7},{7,6},{8,9},{9,8},{10,11... | collective-permute-start | bytes 884744 | tf_op jit(solution)/shard_map/ppermute | solution.py:152

commit v8 on v6

--- a/solution.py
+++ b/solution.py
@@ -186,18 +186,18 @@
     return x_there & 1, y_there * 2 + (x_there >> 1)
 
 
-BUFFERS = ((0, 0, 4), (1, 0, 4), (3, 0, 4), (2, 0, 2), (2, 2, 2))
+BUFFERS = ((0, 0, 4), (1, 0, 4), (3, 0, 4), (2, 0, 4))
 
 
 def project(place, keep, received, weights):
     share, rows = keep.shape
     _, columns, features = weights[0].shape
 
-    def kernel(place_ref, keep_ref, received_ref, w0, w1, w2, w3, w4, own_ref, send_ref, m_ref, a_ref):
+    def kernel(place_ref, keep_ref, received_ref, w0, w1, w2, w3, own_ref, send_ref, m_ref, a_ref):
         m_ref[0:share, :] = keep_ref[...]
         m_ref[share:, :] = received_ref[...]
         a_ref[...] = jnp.zeros_like(a_ref)
-        for w_ref, (offset, begin, count) in zip((w0, w1, w2, w3, w4), BUFFERS):
+        for w_ref, (offset, begin, count) in zip((w0, w1, w2, w3), BUFFERS):
             for inner in range(count):
                 row, column = weight_block(place_ref, offset, begin + inner)
                 m = m_ref[:, pl.ds(pl.multiple_of(row * features, features), features)]
@@ -215,7 +215,7 @@
             jax.ShapeDtypeStruct((share, 8 * columns), BF16),
         ),
         in_specs=[pl.BlockSpec(memory_space=pltpu.SMEM)]
-        + [pl.BlockSpec(memory_space=pltpu.VMEM)] * 7,
+        + [pl.BlockSpec(memory_space=pltpu.VMEM)] * 6,
         out_specs=(pl.BlockSpec(memory_space=pltpu.VMEM),) * 2,
         scratch_shapes=[
             pltpu.VMEM((2 * share, rows), BF16),
@@ -276,12 +276,12 @@
     share, width = grad.shape
     _, columns, features = weights[0].shape
 
-    def kernel(place_ref, grad_ref, received_ref, w0, w1, w2, w3, w4, o_ref, g_ref, a_ref):
+    def kernel(place_ref, grad_ref, received_ref, w0, w1, w2, w3, o_ref, g_ref, a_ref):
         core = place_ref[0]
         g_ref[pl.ds(pl.multiple_of(core * share, share), share), :] = grad_ref[...]
         g_ref[pl.ds(pl.multiple_of((1 - core) * share, share), share), :] = received_ref[...]
         a_ref[...] = jnp.zeros_like(a_ref)
-        for w_ref, (offset, begin, count) in zip((w0, w1, w2, w3, w4), BUFFERS):
+        for w_ref, (offset, begin, count) in zip((w0, w1, w2, w3), BUFFERS):
             for inner in range(count):
                 row, column = weight_block(place_ref, offset, begin + inner)
                 g = g_ref[:, pl.ds(pl.multiple_of(column * columns, columns), columns)]
@@ -293,7 +293,7 @@
         kernel,
         out_shape=jax.ShapeDtypeStruct((2 * share, 2 * features), BF16),
         in_specs=[pl.BlockSpec(memory_space=pltpu.SMEM)]
-        + [pl.BlockSpec(memory_space=pltpu.VMEM)] * 7,
+        + [pl.BlockSpec(memory_space=pltpu.VMEM)] * 6,
         out_specs=pl.BlockSpec(memory_space=pltpu.VMEM),
         scratch_shapes=[
             pltpu.VMEM((2 * share, width), BF16),
@@ -360,8 +360,7 @@
 
         return partner
 
-    up, down = exchange(w, along(-1)), exchange(w, along(1))
-    weights = [w, up, down, exchange(up[:2], along(-1)), exchange(down[2:], along(1))]
+    weights = [w] + [exchange(w, along(step)) for step in (-1, 1, 2)]
 
     def columns_first(v):
         v = v.reshape(v.shape[0], 16, 8, own)

time: 172 us -> 182 us (1.058)
  local copies, waits for them, and re-layouts: 11.4 us -> 23.7 us
  Pallas kernels: 32.2 us -> 27.5 us
  waiting for transfers between devices: 45.6 us -> 48 us
    all_to_all x1, waiting for transfers between devices: 0.01 us -> 5.84 us  [on_device(): blocks = lax.all_to_all(blocks, CLIP, 0, 0, tiled=True)]
    transpose x3, local copies, waits for them, and re-layouts: 0.19 us -> 5.7 us  [columns_first(): return jnp.transpose(v, (0, 2, 1, 3)).reshape(v.shape[0], -1)]
    unnamed x22 -> x28, local copies, waits for them, and re-layouts: 4.61 us -> 9.72 us
    reshape x3, local copies, waits for them, and re-layouts: 0.64 us -> 5.12 us  [columns_first(): return jnp.transpose(v, (0, 2, 1, 3)).reshape(v.shape[0], -1)]
    slice x2 -> x0, local copies, waits for them, and re-layouts: 4.19 us -> none  [the longest x1 2.13 us: on_device(): down[2:]]
    pallas_call x2, Pallas kernels: 16.9 us -> 12.7 us  [attend(): pl.pallas_call(kernel, out_shape=jax.ShapeDtypeStruct((queries, HEAD_DIM)...]
    ppermute x11 -> x10, waiting for transfers between devices: 32.5 us -> 29 us  [exchange(): lax.ppermute(x, SEQ + BRANCH, [(i, partner(i)) for i in range(count)])]
    ppermute x11 -> x10, starting transfers between devices: 35.9 us -> 35.4 us  [exchange(): lax.ppermute(x, SEQ + BRANCH, [(i, partner(i)) for i in range(count)])]
  transfers between devices with their start and end apart: 14 -> 13, of which waited for: 7 -> 6; matrix products, arithmetic and copies ran while one was open for 6% -> 11% of each run, Pallas kernels for 12% -> 5%
where the time goes in v8:
time: 182 us; the launch traced here: 181 us
  starting transfers between devices  68 us (37%)
  waiting for transfers between devices  48 us (26%)
  Pallas kernels  27.5 us (15%)
  local copies, waits for them, and re-layouts  23.7 us (13%)
  blocking collectives  8.72 us (5%)
  other arithmetic  3.49 us (2%)
    ppermute x10, starting transfers between devices, exchange(): lax.ppermute(x, SEQ + BRANCH, [(i, partner(i)) for i in range(count)])  35.4 us
    ppermute x10, waiting for transfers between devices, exchange(): lax.ppermute(x, SEQ + BRANCH, [(i, partner(i)) for i in range(count)])  29 us
    all_to_all x1, starting transfers between devices, on_device(): lax.all_to_all(w, ('c', 'z'), 0, 0, tiled=True).reshape(16 * own, features)  15.8 us
    all_to_all x1, waiting for transfers between devices, on_device(): lax.all_to_all(w, ('c', 'z'), 0, 0, tiled=True).reshape(16 * own, features)  13.1 us
    pallas_call x2, Pallas kernels, attend(): pl.pallas_call(kernel, out_shape=jax.ShapeDtypeStruct((queries, HEAD_DIM)...  12.7 us
    all_to_all x1, starting transfers between devices, on_device(): blocks = lax.all_to_all(blocks, CLIP, 0, 0, tiled=True)  10.9 us
    unnamed x28, local copies, waits for them, and re-layouts  9.72 us
    all_gather x1, blocking collectives, on_device(): parts = lax.all_gather(cot, BRANCH, axis=0, tiled=False)  8.72 us
  transfers between devices with their start and end apart: 13, of which 6 were waited for; matrix products, arithmetic and copies ran while one was open for 11% of the time, Pallas kernels for 5%

profile of v8, /device:TPU:1, one launch (start us, length us, event | category | flops | bytes accessed | tf_op | source)
XLA Modules:
  0.0 181.0 jit_solution(9090793013347030780)
XLA Ops:
  0.7 1.7 broadcast_in_dim.16
  2.3 15.8 %all-to-all-start = ((bf16[16,24,512]{2,1,0:T(8,128)(2,1)}), bf16[16,24,512]{2,1,0:T(8,128)(2,1)}, u32[]{:S(2)}, u32[]{:S(2)}) async-start(bf16[16,24,512]{2,1,0:T(8,128)(2,1)} %broadcast_in_dim.16), calls=%async_computation | async-start | bytes 786432 | tf_op jit(solution)/shard_map/all_to_all | solution.py:348
  20.5 2.6 %prepare.1 = bf16[16,576,128]{2,1,0:T(8,128)(2,1)} custom-call(bf16[192,2048]{1,0:T(8,128)(2,1)S(1)} %bitcast.30, bf16[192,2048]{1,0:T(8,128)(2,1)S(1)} %bitcast.31, bf16[192,2048]{1,0:T(8,128)(2,1)S(1)} %bitcast.32, f32[192,128]{1,0:T(8,128)S(1)} %get-tuple-element.33.c_ref, f32[192,128]{1,0:T(8,128)S(1)} %get-tuple-element.34.s_ref), custom_call_target="tpu_custom_call" | custom-call | tf_op jit(solution)/shard_map/prepare/pallas_call | solution.py:51
  23.2 13.1 %all-to-all-done = bf16[16,24,512]{2,1,0:T(8,128)(2,1)} async-done(((bf16[16,24,512]{2,1,0:T(8,128)(2,1)}), bf16[16,24,512]{2,1,0:T(8,128)(2,1)}, u32[]{:S(2)}, u32[]{:S(2)}) %all-to-all-start) | async-done | bytes 393248 | tf_op jit(solution)/shard_map/all_to_all | solution.py:348
  36.3 10.9 %all-to-all-start.1 = ((bf16[16,576,128]{2,1,0:T(8,128)(2,1)}), bf16[16,576,128]{2,1,0:T(8,128)(2,1)S(1)}, u32[]{:S(2)}, u32[]{:S(2)}) async-start(bf16[16,576,128]{2,1,0:T(8,128)(2,1)} %prepare.1), calls=%async_computation.1 | async-start | bytes 4718592 | tf_op jit(solution)/shard_map/all_to_all | solution.py:352
  51.7 2.1 %copy.20 = bf16[48,3072]{0,1:T(8,128)(2,1)} copy(bf16[48,3072]{1,0:T(8,128)(2,1)} %constant_dynamic-slice_fusion) | data formatting | bytes 589824
  53.9 2.1 %copy.16 = bf16[48,8,16,24]{0,3,2,1:T(8,128)(2,1)} copy(bf16[48,8,16,24]{0,3,1,2:T(8,128)(2,1)} %bitcast.34) | data formatting | bytes 589824 | tf_op jit(solution)/shard_map/transpose | solution.py:367
  56.0 2.1 %copy.19.upstream_ref = bf16[48,3072]{1,0:T(8,128)(2,1)} copy(bf16[48,3072]{0,1:T(8,128)(2,1)} %bitcast.35) | data formatting | bytes 589824 | tf_op jit(solution)/shard_map/reshape | solution.py:367
  58.0 2.1 %copy.13 = bf16[48,3072]{0,1:T(8,128)(2,1)} copy(bf16[48,3072]{1,0:T(8,128)(2,1)} %param.17) | data formatting | bytes 589824 | tf_op args[7]
  60.2 2.1 %copy.14 = bf16[48,8,16,24]{0,3,2,1:T(8,128)(2,1)} copy(bf16[48,8,16,24]{0,3,1,2:T(8,128)(2,1)} %bitcast.37) | data formatting | bytes 589824 | tf_op jit(solution)/shard_map/transpose | solution.py:367
  62.3 2.1 %copy.18.frozen_ref = bf16[48,3072]{1,0:T(8,128)(2,1)} copy(bf16[48,3072]{0,1:T(8,128)(2,1)} %bitcast.36) | data formatting | bytes 589824 | tf_op jit(solution)/shard_map/reshape | solution.py:367
  68.7 5.8 %all-to-all-done.1.b_ref = bf16[16,576,128]{2,1,0:T(8,128)(2,1)S(1)} async-done(((bf16[16,576,128]{2,1,0:T(8,128)(2,1)}), bf16[16,576,128]{2,1,0:T(8,128)(2,1)S(1)}, u32[]{:S(2)}, u32[]{:S(2)}) %all-to-all-start.1) | async-done | bytes 2359328 | tf_op jit(solution)/shard_map/all_to_all | solution.py:352
  74.5 6.4 %attend_first.1 = bf16[1536,128]{1,0:T(8,128)(2,1)S(1)} custom-call(s32[1]{0:T(128)S(6)} %sub.3.part_ref, f32[1]{0:T(128)} %bitcast.4.scale_ref, bf16[16,576,128]{2,1,0:T(8,128)(2,1)S(1)} %all-to-all-done.1.b_ref), custom_call_target="tpu_custom_call" | custom-call | flops 2415919104 | bytes 2359296 | tf_op jit(solution)/shard_map/attend_first/pallas_call | solution.py:127
  80.9 5.4 %collective-permute-start = (bf16[1536,128]{1,0:T(8,128)(2,1)S(1)}, bf16[1536,128]{1,0:T(8,128)(2,1)S(1)}, u32[]{:S(2)}, u32[]{:S(2)}) collective-permute-start(bf16[1536,128]{1,0:T(8,128)(2,1)S(1)} %attend_first.1), channel_id=1, source_target_pairs={{0,1},{1,0},{2,3},{3,2},{4,5},{5,4},{6,7},{7,6},{8,9},{9,8},{10,11... | collective-permute-start | bytes 1179656 | tf_op jit(solution)/shard_map/ppermute | solution.py:152
  86.3 4.7 %collective-permute-start.4 = (bf16[384,512]{1,0:T(8,128)(2,1)}, bf16[384,512]{1,0:T(8,128)(2,1)}, u32[]{:S(2)}, u32[]{:S(2)}) collective-permute-start(bf16[384,512]{1,0:T(8,128)(2,1)} %bitcast.6), channel_id=1, source_target_pairs={{0,24},{1,7},{2,26},{3,5},{4,28},{5,3},{6,30},{7,1},{8,16},{9,15},... | collective-permute-start | bytes 1179656 | tf_op jit(solution)/shard_map/ppermute | solution.py:152
  91.0 3.7 %collective-permute-start.3 = (bf16[384,512]{1,0:T(8,128)(2,1)}, bf16[384,512]{1,0:T(8,128)(2,1)}, u32[]{:S(2)}, u32[]{:S(2)}) collective-permute-start(bf16[384,512]{1,0:T(8,128)(2,1)} %bitcast.6), channel_id=1, source_target_pairs={{0,16},{1,5},{2,18},{3,7},{4,20},{5,1},{6,22},{7,3},{8,24},{9,13},... | collective-permute-start | bytes 1179656 | tf_op jit(solution)/shard_map/ppermute | solution.py:152
  94.6 2.1 %collective-permute-start.2 = (bf16[384,512]{1,0:T(8,128)(2,1)}, bf16[384,512]{1,0:T(8,128)(2,1)}, u32[]{:S(2)}, u32[]{:S(2)}) collective-permute-start(bf16[384,512]{1,0:T(8,128)(2,1)} %bitcast.6), channel_id=1, source_target_pairs={{0,8},{1,3},{2,10},{3,1},{4,12},{5,7},{6,14},{7,5},{8,0},{9,11},{1... | collective-permute-start | bytes 1179656 | tf_op jit(solution)/shard_map/ppermute | solution.py:152
  96.8 6.4 %attend_last.1 = bf16[1536,128]{1,0:T(8,128)(2,1)S(1)} custom-call(s32[1]{0:T(128)} %bitcast.part_ref.core_ref, f32[1]{0:T(128)} %bitcast.4.scale_ref, bf16[16,576,128]{2,1,0:T(8,128)(2,1)S(1)} %all-to-all-done.1.b_ref, bf16[1536,128]{1,0:T(8,128)(2,1)S(1)} %collective-permute-done.refs_0_), custom_call_target="tpu_custom_call" | custom-call | flops 2415919104 | bytes 2359296 | tf_op jit(solution)/shard_map/attend_last/pallas_call | solution.py:127
  103.9 5.9 %all-to-all-start.2 = ((bf16[32,48,128]{2,1,0:T(8,128)(2,1)}), bf16[32,48,128]{2,1,0:T(8,128)(2,1)S(1)}, u32[]{:S(2)}, u32[]{:S(2)}) async-start(bf16[32,48,128]{2,1,0:T(8,128)(2,1)} %bitcast.33), calls=%async_computation.2 | async-start | bytes 786432 | tf_op jit(solution)/shard_map/all_to_all | solution.py:377
  111.4 4.6 %collective-permute-start.7 = (bf16[4,384,512]{2,1,0:T(8,128)(2,1)S(1)}, bf16[4,384,512]{2,1,0:T(8,128)(2,1)}, u32[]{:S(2)}, u32[]{:S(2)}) collective-permute-start(bf16[4,384,512]{2,1,0:T(8,128)(2,1)S(1)} %pad_maximum_fusion.w0), channel_id=1, source_target_pairs={{0,4},{1,17},{2,6},{3,19},{4,0},{5,21},{6,2},{7,23},{8,12},{9,25},... | collective-permute-start | bytes 4718600 | tf_op jit(solution)/shard_map/ppermute | solution.py:152
  116.1 2.2 %collective-permute-start.6 = (bf16[4,384,512]{2,1,0:T(8,128)(2,1)S(1)}, bf16[4,384,512]{2,1,0:T(8,128)(2,1)}, u32[]{:S(2)}, u32[]{:S(2)}) collective-permute-start(bf16[4,384,512]{2,1,0:T(8,128)(2,1)S(1)} %pad_maximum_fusion.w0), channel_id=1, source_target_pairs={{0,2},{1,9},{2,4},{3,11},{4,6},{5,13},{6,0},{7,15},{8,10},{9,17},{... | collective-permute-start | bytes 4718600 | tf_op jit(solution)/shard_map/ppermute | solution.py:152
  118.3 4.3 %collective-permute-start.5 = (bf16[4,384,512]{2,1,0:T(8,128)(2,1)S(1)}, bf16[4,384,512]{2,1,0:T(8,128)(2,1)}, u32[]{:S(2)}, u32[]{:S(2)}) collective-permute-start(bf16[4,384,512]{2,1,0:T(8,128)(2,1)S(1)} %pad_maximum_fusion.w0), channel_id=1, source_target_pairs={{0,6},{1,25},{2,0},{3,27},{4,2},{5,29},{6,4},{7,31},{8,14},{9,1},{... | collective-permute-start | bytes 4718600 | tf_op jit(solution)/shard_map/ppermute | solution.py:152
  122.7 4.1 %collective-permute-start.1 = (bf16[48,1024]{1,0:T(8,128)(2,1)S(1)}, bf16[48,1024]{1,0:T(8,128)(2,1)S(1)}, u32[]{:S(2)}, u32[]{:S(2)}) collective-permute-start(bf16[48,1024]{1,0:T(8,128)(2,1)S(1)} %get-tuple-element.21), channel_id=1, source_target_pairs={{0,1},{1,0},{2,3},{3,2},{4,5},{5,4},{6,7},{7,6},{8,9},{9,8},{10,11... | collective-permute-start | bytes 294920 | tf_op jit(solution)/shard_map/ppermute | solution.py:152
  126.8 9.7 %collective-permute-done.7.w3 = bf16[4,384,512]{2,1,0:T(8,128)(2,1)} collective-permute-done((bf16[4,384,512]{2,1,0:T(8,128)(2,1)S(1)}, bf16[4,384,512]{2,1,0:T(8,128)(2,1)}, u32[]{:S(2)}, u32[]{:S(2)}) %collective-permute-start.7) | collective-permute-done | bytes 1572896 | tf_op jit(solution)/shard_map/ppermute | solution.py:152
  136.5 16.8 %collective-permute-done.6.w2 = bf16[4,384,512]{2,1,0:T(8,128)(2,1)} collective-permute-done((bf16[4,384,512]{2,1,0:T(8,128)(2,1)S(1)}, bf16[4,384,512]{2,1,0:T(8,128)(2,1)}, u32[]{:S(2)}, u32[]{:S(2)}) %collective-permute-start.6) | collective-permute-done | bytes 1572896 | tf_op jit(solution)/shard_map/ppermute | solution.py:152
  153.3 4.6 %project.1 = (f32[48,3072]{1,0:T(8,128)S(1)}, bf16[48,3072]{1,0:T(8,128)(2,1)S(1)}) custom-call(s32[3]{0:T(128)S(1)} %pad_add_fusion.place_ref, bf16[48,1024]{1,0:T(8,128)(2,1)S(1)} %get-tuple-element.20.keep_ref, bf16[48,1024]{1,0:T(8,128)(2,1)S(1)} %collective-permute-done.1.received_ref, bf16[4,384,512]{2,1,0:T(8,128)(2,1)S(1)} %pad_maximum_fusion.w0, ...), custom_call_target="tpu_custom_call" | custom-call | tf_op jit(solution)/shard_map/project/pallas_call | solution.py:211
  157.9 2.2 %collective-permute-start.8 = (bf16[48,3072]{1,0:T(8,128)(2,1)S(1)}, bf16[48,3072]{1,0:T(8,128)(2,1)S(1)}, u32[]{:S(2)}, u32[]{:S(2)}) collective-permute-start(bf16[48,3072]{1,0:T(8,128)(2,1)S(1)} %get-tuple-element.24), channel_id=1, source_target_pairs={{0,1},{1,0},{2,3},{3,2},{4,5},{5,4},{6,7},{7,6},{8,9},{9,8},{10,11... | collective-permute-start | bytes 884744 | tf_op jit(solution)/shard_map/ppermute | solution.py:152
  161.4 2.0 %normalize.1 = (bf16[48,3072]{1,0:T(8,128)(2,1)}, bf16[48,3072]{1,0:T(8,128)(2,1)S(1)}) custom-call(f32[48,3072]{1,0:T(8,128)S(1)} %get-tuple-element.23.own_ref, bf16[48,3072]{1,0:T(8,128)(2,1)S(1)} %collective-permute-done.8.received_ref, f32[48,3072]{1,0:T(8,128)S(1)} %copy-done.7, f32[48,3072]{1,0:T(8,128)S(1)} %copy-done.9, f32[1,3072]{1,0:T(1,128)S(1)} %reshape.43.gain_ref), custom_call_target="tpu_custom_call" | custom-call | tf_op jit(solution)/shard_map/normalize/pallas_call | solution.py:264
  163.4 2.2 %collective-permute-start.9 = (bf16[48,3072]{1,0:T(8,128)(2,1)S(1)}, bf16[48,3072]{1,0:T(8,128)(2,1)S(1)}, u32[]{:S(2)}, u32[]{:S(2)}) collective-permute-start(bf16[48,3072]{1,0:T(8,128)(2,1)S(1)} %get-tuple-element.29.grad_ref), channel_id=1, source_target_pairs={{0,1},{1,0},{2,3},{3,2},{4,5},{5,4},{6,7},{7,6},{8,9},{9,8},{10,11... | collective-permute-start | bytes 884744 | tf_op jit(solution)/shard_map/ppermute | solution.py:152
  166.9 3.8 %project_back.1 = bf16[96,1024]{1,0:T(8,128)(2,1)S(1)} custom-call(s32[3]{0:T(128)S(1)} %pad_add_fusion.place_ref, bf16[48,3072]{1,0:T(8,128)(2,1)S(1)} %get-tuple-element.29.grad_ref, bf16[48,3072]{1,0:T(8,128)(2,1)S(1)} %collective-permute-done.9.received_ref, bf16[4,384,512]{2,1,0:T(8,128)(2,1)S(1)} %pad_maximum_fusion.w0, ...), custom_call_target="tpu_custom_call" | custom-call | tf_op jit(solution)/shard_map/project_back/pallas_call | solution.py:292
  170.6 8.7 %all-gather = bf16[384,1024]{1,0:T(8,128)(2,1)S(1)} all-gather(bf16[96,1024]{1,0:T(8,128)(2,1)S(1)} %project_back.1), channel_id=2, replica_groups=mesh['c'=8,'z'=2,'y'=4,'h'=2,'l'=2,'k'=2] {'l','k'}, dimensions={0}, use_global_device_ids=true | all-gather | bytes 983040 | tf_op jit(solution)/shard_map/all_gather | solution.py:384
  179.4 1.6 scatter_scaled.1
  (48 shorter events, 15.6 us)
Async XLA Ops:
  0.6 50.4 %copy-start = (bf16[192,3072]{1,0:T(8,128)(2,1)S(1)}, bf16[192,3072]{1,0:T(8,128)(2,1)}, u32[]{:S(2)}) copy-start(bf16[192,3072]{1,0:T(8,128)(2,1)} %param.19) | copy-start | bytes 3538948
  0.6 18.7 %copy-start.4 = (bf16[1,192,2048]{2,1,0:T(8,128)(2,1)S(1)}, bf16[1,192,2048]{2,1,0:T(8,128)(2,1)}, u32[]{:S(2)}) copy-start(bf16[1,192,2048]{2,1,0:T(8,128)(2,1)} %param.11) | copy-start | bytes 2359300
  0.7 18.7 %copy-start.3 = (bf16[1,192,2048]{2,1,0:T(8,128)(2,1)S(1)}, bf16[1,192,2048]{2,1,0:T(8,128)(2,1)}, u32[]{:S(2)}) copy-start(bf16[1,192,2048]{2,1,0:T(8,128)(2,1)} %param.10) | copy-start | bytes 2359300
  2.3 34.0 %all-to-all-start = ((bf16[16,24,512]{2,1,0:T(8,128)(2,1)}), bf16[16,24,512]{2,1,0:T(8,128)(2,1)}, u32[]{:S(2)}, u32[]{:S(2)}) async-start(bf16[16,24,512]{2,1,0:T(8,128)(2,1)} %broadcast_in_dim.16), calls=%async_computation | async-start | bytes 786432 | tf_op jit(solution)/shard_map/all_to_all | solution.py:348
  19.4 1.1 copy-start.5
  36.3 11.5 %copy-start.11 = (f32[3072]{0:T(1024)S(1)}, f32[3072]{0:T(1024)}, u32[]{:S(2)}) copy-start(f32[3072]{0:T(1024)} %param.18) | copy-start | bytes 36868
  36.3 38.2 %all-to-all-start.1 = ((bf16[16,576,128]{2,1,0:T(8,128)(2,1)}), bf16[16,576,128]{2,1,0:T(8,128)(2,1)S(1)}, u32[]{:S(2)}, u32[]{:S(2)}) async-start(bf16[16,576,128]{2,1,0:T(8,128)(2,1)} %prepare.1), calls=%async_computation.1 | async-start | bytes 4718592 | tf_op jit(solution)/shard_map/all_to_all | solution.py:352
  60.2 7.9 %copy-start.12 = (f32[64]{0:T(128)S(1)}, f32[64]{0:T(128)}, u32[]{:S(2)}) copy-start(f32[64]{0:T(128)} %param.15) | copy-start | bytes 772
  64.4 1.0 copy-start.1
  65.3 1.0 copy-start.2
  66.4 0.8 copy-start.6
  67.2 0.8 copy-start.8
  80.9 15.9 %collective-permute-start = (bf16[1536,128]{1,0:T(8,128)(2,1)S(1)}, bf16[1536,128]{1,0:T(8,128)(2,1)S(1)}, u32[]{:S(2)}, u32[]{:S(2)}) collective-permute-start(bf16[1536,128]{1,0:T(8,128)(2,1)S(1)} %attend_first.1), channel_id=1, source_target_pairs={{0,1},{1,0},{2,3},{3,2},{4,5},{5,4},{6,7},{7,6},{8,9},{9,8},{10,11... | collective-permute-start | bytes 1179656 | tf_op jit(solution)/shard_map/ppermute | solution.py:152
  86.3 23.6 %collective-permute-start.4 = (bf16[384,512]{1,0:T(8,128)(2,1)}, bf16[384,512]{1,0:T(8,128)(2,1)}, u32[]{:S(2)}, u32[]{:S(2)}) collective-permute-start(bf16[384,512]{1,0:T(8,128)(2,1)} %bitcast.6), channel_id=1, source_target_pairs={{0,24},{1,7},{2,26},{3,5},{4,28},{5,3},{6,30},{7,1},{8,16},{9,15},... | collective-permute-start | bytes 1179656 | tf_op jit(solution)/shard_map/ppermute | solution.py:152
  91.0 18.9 %collective-permute-start.3 = (bf16[384,512]{1,0:T(8,128)(2,1)}, bf16[384,512]{1,0:T(8,128)(2,1)}, u32[]{:S(2)}, u32[]{:S(2)}) collective-permute-start(bf16[384,512]{1,0:T(8,128)(2,1)} %bitcast.6), channel_id=1, source_target_pairs={{0,16},{1,5},{2,18},{3,7},{4,20},{5,1},{6,22},{7,3},{8,24},{9,13},... | collective-permute-start | bytes 1179656 | tf_op jit(solution)/shard_map/ppermute | solution.py:152
  94.6 15.2 %collective-permute-start.2 = (bf16[384,512]{1,0:T(8,128)(2,1)}, bf16[384,512]{1,0:T(8,128)(2,1)}, u32[]{:S(2)}, u32[]{:S(2)}) collective-permute-start(bf16[384,512]{1,0:T(8,128)(2,1)} %bitcast.6), channel_id=1, source_target_pairs={{0,8},{1,3},{2,10},{3,1},{4,12},{5,7},{6,14},{7,5},{8,0},{9,11},{1... | collective-permute-start | bytes 1179656 | tf_op jit(solution)/shard_map/ppermute | solution.py:152
  103.2 0.8 copy-start.10
  103.9 18.7 %all-to-all-start.2 = ((bf16[32,48,128]{2,1,0:T(8,128)(2,1)}), bf16[32,48,128]{2,1,0:T(8,128)(2,1)S(1)}, u32[]{:S(2)}, u32[]{:S(2)}) async-start(bf16[32,48,128]{2,1,0:T(8,128)(2,1)} %bitcast.33), calls=%async_computation.2 | async-start | bytes 786432 | tf_op jit(solution)/shard_map/all_to_all | solution.py:377
  111.4 25.1 %collective-permute-start.7 = (bf16[4,384,512]{2,1,0:T(8,128)(2,1)S(1)}, bf16[4,384,512]{2,1,0:T(8,128)(2,1)}, u32[]{:S(2)}, u32[]{:S(2)}) collective-permute-start(bf16[4,384,512]{2,1,0:T(8,128)(2,1)S(1)} %pad_maximum_fusion.w0), channel_id=1, source_target_pairs={{0,4},{1,17},{2,6},{3,19},{4,0},{5,21},{6,2},{7,23},{8,12},{9,25},... | collective-permute-start | bytes 4718600 | tf_op jit(solution)/shard_map/ppermute | solution.py:152
  116.1 37.2 %collective-permute-start.6 = (bf16[4,384,512]{2,1,0:T(8,128)(2,1)S(1)}, bf16[4,384,512]{2,1,0:T(8,128)(2,1)}, u32[]{:S(2)}, u32[]{:S(2)}) collective-permute-start(bf16[4,384,512]{2,1,0:T(8,128)(2,1)S(1)} %pad_maximum_fusion.w0), channel_id=1, source_target_pairs={{0,2},{1,9},{2,4},{3,11},{4,6},{5,13},{6,0},{7,15},{8,10},{9,17},{... | collective-permute-start | bytes 4718600 | tf_op jit(solution)/shard_map/ppermute | solution.py:152
  118.3 35.0 %collective-permute-start.5 = (bf16[4,384,512]{2,1,0:T(8,128)(2,1)S(1)}, bf16[4,384,512]{2,1,0:T(8,128)(2,1)}, u32[]{:S(2)}, u32[]{:S(2)}) collective-permute-start(bf16[4,384,512]{2,1,0:T(8,128)(2,1)S(1)} %pad_maximum_fusion.w0), channel_id=1, source_target_pairs={{0,6},{1,25},{2,0},{3,27},{4,2},{5,29},{6,4},{7,31},{8,14},{9,1},{... | collective-permute-start | bytes 4718600 | tf_op jit(solution)/shard_map/ppermute | solution.py:152
  122.7 30.6 %collective-permute-start.1 = (bf16[48,1024]{1,0:T(8,128)(2,1)S(1)}, bf16[48,1024]{1,0:T(8,128)(2,1)S(1)}, u32[]{:S(2)}, u32[]{:S(2)}) collective-permute-start(bf16[48,1024]{1,0:T(8,128)(2,1)S(1)} %get-tuple-element.21), channel_id=1, source_target_pairs={{0,1},{1,0},{2,3},{3,2},{4,5},{5,4},{6,7},{7,6},{8,9},{9,8},{10,11... | collective-permute-start | bytes 294920 | tf_op jit(solution)/shard_map/ppermute | solution.py:152
  153.3 8.1 %copy-start.7 = (f32[48,3072]{1,0:T(8,128)S(1)}, f32[48,3072]{1,0:T(8,128)}, u32[]{:S(2)}) copy-start(f32[48,3072]{1,0:T(8,128)} %copy-done.6) | copy-start | bytes 1769476
  153.3 8.1 %copy-start.9 = (f32[48,3072]{1,0:T(8,128)S(1)}, f32[48,3072]{1,0:T(8,128)}, u32[]{:S(2)}) copy-start(f32[48,3072]{1,0:T(8,128)} %copy-done.8) | copy-start | bytes 1769476
  157.9 3.5 %collective-permute-start.8 = (bf16[48,3072]{1,0:T(8,128)(2,1)S(1)}, bf16[48,3072]{1,0:T(8,128)(2,1)S(1)}, u32[]{:S(2)}, u32[]{:S(2)}) collective-permute-start(bf16[48,3072]{1,0:T(8,128)(2,1)S(1)} %get-tuple-element.24), channel_id=1, source_target_pairs={{0,1},{1,0},{2,3},{3,2},{4,5},{5,4},{6,7},{7,6},{8,9},{9,8},{10,11... | collective-permute-start | bytes 884744 | tf_op jit(solution)/shard_map/ppermute | solution.py:152
  163.4 3.5 %collective-permute-start.9 = (bf16[48,3072]{1,0:T(8,128)(2,1)S(1)}, bf16[48,3072]{1,0:T(8,128)(2,1)S(1)}, u32[]{:S(2)}, u32[]{:S(2)}) collective-permute-start(bf16[48,3072]{1,0:T(8,128)(2,1)S(1)} %get-tuple-element.29.grad_ref), channel_id=1, source_target_pairs={{0,1},{1,0},{2,3},{3,2},{4,5},{5,4},{6,7},{7,6},{8,9},{9,8},{10,11... | collective-permute-start | bytes 884744 | tf_op jit(solution)/shard_map/ppermute | solution.py:152

commit v9 on v6

--- a/solution.py
+++ b/solution.py
@@ -189,41 +189,56 @@
 BUFFERS = ((0, 0, 4), (1, 0, 4), (3, 0, 4), (2, 0, 2), (2, 2, 2))
 
 
-def project(place, keep, received, weights):
+def project(place, keep, received, weights, buffers, before=None):
     share, rows = keep.shape
     _, columns, features = weights[0].shape
-
-    def kernel(place_ref, keep_ref, received_ref, w0, w1, w2, w3, w4, own_ref, send_ref, m_ref, a_ref):
+    count = len(weights)
+
+    def kernel(place_ref, keep_ref, received_ref, *refs):
+        w_refs, refs = refs[:count], refs[count:]
+        m_ref = refs[-1]
         m_ref[0:share, :] = keep_ref[...]
         m_ref[share:, :] = received_ref[...]
-        a_ref[...] = jnp.zeros_like(a_ref)
-        for w_ref, (offset, begin, count) in zip((w0, w1, w2, w3, w4), BUFFERS):
-            for inner in range(count):
+        if before is None:
+            a_ref = refs[0]
+            a_ref[...] = jnp.zeros_like(a_ref)
+        else:
+            before_ref, own_ref, send_ref, a_ref = refs[:4]
+            a_ref[...] = before_ref[...]
+        for w_ref, (offset, begin, pieces) in zip(w_refs, buffers):
+            for inner in range(pieces):
                 row, column = weight_block(place_ref, offset, begin + inner)
                 m = m_ref[:, pl.ds(pl.multiple_of(row * features, features), features)]
                 at = pl.ds(pl.multiple_of(column * columns, columns), columns)
                 a_ref[:, at] += lax.dot_general(
                     m, w_ref[inner], NT, preferred_element_type=F32
                 )
-        own_ref[...] = a_ref[0:share, :]
-        send_ref[...] = a_ref[share:, :].astype(BF16)
-
-    return pl.pallas_call(
-        kernel,
-        out_shape=(
+        if before is not None:
+            own_ref[...] = a_ref[0:share, :]
+            send_ref[...] = a_ref[share:, :].astype(BF16)
+
+    vmem = pl.BlockSpec(memory_space=pltpu.VMEM)
+    total = (2 * share, 8 * columns)
+    mixed = pltpu.VMEM((2 * share, rows), BF16)
+    if before is None:
+        extra, out = (), jax.ShapeDtypeStruct(total, F32)
+        out_specs, scratch = vmem, [mixed]
+    else:
+        extra = (before,)
+        out = (
             jax.ShapeDtypeStruct((share, 8 * columns), F32),
             jax.ShapeDtypeStruct((share, 8 * columns), BF16),
-        ),
-        in_specs=[pl.BlockSpec(memory_space=pltpu.SMEM)]
-        + [pl.BlockSpec(memory_space=pltpu.VMEM)] * 7,
-        out_specs=(pl.BlockSpec(memory_space=pltpu.VMEM),) * 2,
-        scratch_shapes=[
-            pltpu.VMEM((2 * share, rows), BF16),
-            pltpu.VMEM((2 * share, 8 * columns), F32),
-        ],
+        )
+        out_specs, scratch = (vmem, vmem), [pltpu.VMEM(total, F32), mixed]
+    return pl.pallas_call(
+        kernel,
+        out_shape=out,
+        in_specs=[pl.BlockSpec(memory_space=pltpu.SMEM)] + [vmem] * (2 + count + len(extra)),
+        out_specs=out_specs,
+        scratch_shapes=scratch,
         compiler_params=pltpu.CompilerParams(vmem_limit_bytes=16 << 20),
-        name="project",
-    )(place, keep, received, *weights)
+        name="project_near" if before is None else "project_far",
+    )(place, keep, received, *weights, *extra)
 
 
 def widen(frozen, upstream, gain):
@@ -379,7 +394,9 @@
         attended.reshape(HEADS * 2, share, HEAD_DIM), CLIP + ("l",), 0, 0, tiled=True
     )
     keep, send = sum_pieces(pieces, core)
-    own_part, send = project(place, keep, to_partner(send), weights)
+    received = to_partner(send)
+    near = project(place, keep, received, weights[:3], BUFFERS[:3])
+    own_part, send = project(place, keep, received, weights[3:], BUFFERS[3:], near)
     normed, grad = normalize(own_part, to_partner(send), frozen, upstream, gain, own)
     cot = project_back(place, grad, to_partner(grad), weights)
     parts = lax.all_gather(cot, BRANCH, axis=0, tiled=False)

time: 172 us -> 169 us (0.983)
  waiting for transfers between devices: 45.6 us -> 42.1 us
    ppermute x11, waiting for transfers between devices: 32.5 us -> 29 us  [exchange(): lax.ppermute(x, SEQ + BRANCH, [(i, partner(i)) for i in range(count)])]
    pallas_call x1 -> x2, Pallas kernels: 4.28 us -> 5.3 us  [project(): pl.pallas_call(kernel, out_shape=out, in_specs=[pl.BlockSpec(memory_space...]
  transfers between devices with their start and end apart: 14 -> 14, of which waited for: 7 -> 7; matrix products, arithmetic and copies ran while one was open for 6% -> 6% of each run, Pallas kernels for 12% -> 14%
where the time goes in v9:
time: 169 us; the launch traced here: 168 us
  starting transfers between devices  67.4 us (40%)
  waiting for transfers between devices  42.1 us (25%)
  Pallas kernels  33.2 us (20%)
  local copies, waits for them, and re-layouts  11.4 us (7%)
  blocking collectives  8.78 us (5%)
  other arithmetic  3.54 us (2%)
    ppermute x11, starting transfers between devices, exchange(): lax.ppermute(x, SEQ + BRANCH, [(i, partner(i)) for i in range(count)])  35.9 us
    ppermute x11, waiting for transfers between devices, exchange(): lax.ppermute(x, SEQ + BRANCH, [(i, partner(i)) for i in range(count)])  29 us
    pallas_call x2, Pallas kernels, attend(): pl.pallas_call(kernel, out_shape=jax.ShapeDtypeStruct((queries, HEAD_DIM)...  16.9 us
    all_to_all x1, starting transfers between devices, on_device(): lax.all_to_all(w, ('c', 'z'), 0, 0, tiled=True).reshape(16 * own, features)  15.8 us
    all_to_all x1, waiting for transfers between devices, on_device(): lax.all_to_all(w, ('c', 'z'), 0, 0, tiled=True).reshape(16 * own, features)  13.1 us
    all_to_all x1, starting transfers between devices, on_device(): blocks = lax.all_to_all(blocks, CLIP, 0, 0, tiled=True)  10.9 us
    all_gather x1, blocking collectives, on_device(): parts = lax.all_gather(cot, BRANCH, axis=0, tiled=False)  8.78 us
    pallas_call x2, Pallas kernels, project(): pl.pallas_call(kernel, out_shape=out, in_specs=[pl.BlockSpec(memory_space...  5.3 us
  transfers between devices with their start and end apart: 14, of which 7 were waited for; matrix products, arithmetic and copies ran while one was open for 6% of the time, Pallas kernels for 14%

profile of v9, /device:TPU:1, one launch (start us, length us, event | category | flops | bytes accessed | tf_op | source)
XLA Modules:
  0.0 168.1 jit_solution(4908211608938720549)
XLA Ops:
  0.7 1.7 broadcast_in_dim.16
  2.3 15.8 %all-to-all-start = ((bf16[16,24,512]{2,1,0:T(8,128)(2,1)}), bf16[16,24,512]{2,1,0:T(8,128)(2,1)}, u32[]{:S(2)}, u32[]{:S(2)}) async-start(bf16[16,24,512]{2,1,0:T(8,128)(2,1)} %broadcast_in_dim.16), calls=%async_computation | async-start | bytes 786432 | tf_op jit(solution)/shard_map/all_to_all | solution.py:363
  20.5 2.7 %prepare.1 = bf16[16,576,128]{2,1,0:T(8,128)(2,1)} custom-call(bf16[192,2048]{1,0:T(8,128)(2,1)S(1)} %bitcast.30, bf16[192,2048]{1,0:T(8,128)(2,1)S(1)} %bitcast.31, bf16[192,2048]{1,0:T(8,128)(2,1)S(1)} %bitcast.32, f32[192,128]{1,0:T(8,128)S(1)} %get-tuple-element.33.c_ref, f32[192,128]{1,0:T(8,128)S(1)} %get-tuple-element.34.s_ref), custom_call_target="tpu_custom_call" | custom-call | tf_op jit(solution)/shard_map/prepare/pallas_call | solution.py:51
  23.2 13.1 %all-to-all-done = bf16[16,24,512]{2,1,0:T(8,128)(2,1)} async-done(((bf16[16,24,512]{2,1,0:T(8,128)(2,1)}), bf16[16,24,512]{2,1,0:T(8,128)(2,1)}, u32[]{:S(2)}, u32[]{:S(2)}) %all-to-all-start) | async-done | bytes 393248 | tf_op jit(solution)/shard_map/all_to_all | solution.py:363
  36.3 10.9 %all-to-all-start.1 = ((bf16[16,576,128]{2,1,0:T(8,128)(2,1)}), bf16[16,576,128]{2,1,0:T(8,128)(2,1)}, u32[]{:S(2)}, u32[]{:S(2)}) async-start(bf16[16,576,128]{2,1,0:T(8,128)(2,1)} %prepare.1), calls=%async_computation.1 | async-start | bytes 4718592 | tf_op jit(solution)/shard_map/all_to_all | solution.py:367
  48.1 4.5 %collective-permute-start.4 = (bf16[384,512]{1,0:T(8,128)(2,1)}, bf16[384,512]{1,0:T(8,128)(2,1)}, u32[]{:S(2)}, u32[]{:S(2)}) collective-permute-start(bf16[384,512]{1,0:T(8,128)(2,1)} %bitcast.6), channel_id=1, source_target_pairs={{0,24},{1,7},{2,26},{3,5},{4,28},{5,3},{6,30},{7,1},{8,16},{9,15},... | collective-permute-start | bytes 1179656 | tf_op jit(solution)/shard_map/ppermute | solution.py:152
  52.6 2.2 %collective-permute-start.3 = (bf16[384,512]{1,0:T(8,128)(2,1)}, bf16[384,512]{1,0:T(8,128)(2,1)}, u32[]{:S(2)}, u32[]{:S(2)}) collective-permute-start(bf16[384,512]{1,0:T(8,128)(2,1)} %bitcast.6), channel_id=1, source_target_pairs={{0,16},{1,5},{2,18},{3,7},{4,20},{5,1},{6,22},{7,3},{8,24},{9,13},... | collective-permute-start | bytes 1179656 | tf_op jit(solution)/shard_map/ppermute | solution.py:152
  54.8 2.3 %collective-permute-start.2 = (bf16[384,512]{1,0:T(8,128)(2,1)}, bf16[384,512]{1,0:T(8,128)(2,1)}, u32[]{:S(2)}, u32[]{:S(2)}) collective-permute-start(bf16[384,512]{1,0:T(8,128)(2,1)} %bitcast.6), channel_id=1, source_target_pairs={{0,8},{1,3},{2,10},{3,1},{4,12},{5,7},{6,14},{7,5},{8,0},{9,11},{1... | collective-permute-start | bytes 1179656 | tf_op jit(solution)/shard_map/ppermute | solution.py:152
  57.9 1.3 copy.13
  62.1 23.1 %collective-permute-done.4 = bf16[384,512]{1,0:T(8,128)(2,1)} collective-permute-done((bf16[384,512]{1,0:T(8,128)(2,1)}, bf16[384,512]{1,0:T(8,128)(2,1)}, u32[]{:S(2)}, u32[]{:S(2)}) %collective-permute-start.4) | collective-permute-done | bytes 393248 | tf_op jit(solution)/shard_map/ppermute | solution.py:152
  85.2 1.5 pad_maximum_fusion.refs_0_.w0
  86.8 2.9 %collective-permute-start.7 = (bf16[4,384,512]{2,1,0:T(8,128)(2,1)S(1)}, bf16[4,384,512]{2,1,0:T(8,128)(2,1)}, u32[]{:S(2)}, u32[]{:S(2)}) collective-permute-start(bf16[4,384,512]{2,1,0:T(8,128)(2,1)S(1)} %pad_maximum_fusion.refs_0_.w0), channel_id=1, source_target_pairs={{0,2},{1,9},{2,4},{3,11},{4,6},{5,13},{6,0},{7,15},{8,10},{9,17},{... | collective-permute-start | bytes 4718600 | tf_op jit(solution)/shard_map/ppermute | solution.py:152
  89.7 3.6 %collective-permute-start.5 = (bf16[4,384,512]{2,1,0:T(8,128)(2,1)S(1)}, bf16[4,384,512]{2,1,0:T(8,128)(2,1)}, u32[]{:S(2)}, u32[]{:S(2)}) collective-permute-start(bf16[4,384,512]{2,1,0:T(8,128)(2,1)S(1)} %pad_maximum_fusion.refs_0_.w0), channel_id=1, source_target_pairs={{0,6},{1,25},{2,0},{3,27},{4,2},{5,29},{6,4},{7,31},{8,14},{9,1},{... | collective-permute-start | bytes 4718600 | tf_op jit(solution)/shard_map/ppermute | solution.py:152
  93.3 8.0 %attend_first.1 = bf16[1536,128]{1,0:T(8,128)(2,1)S(1)} custom-call(s32[1]{0:T(128)S(6)} %sub.3.part_ref, f32[1]{0:T(128)} %bitcast.4.scale_ref, bf16[16,576,128]{2,1,0:T(8,128)(2,1)} %all-to-all-done.1.b_ref), custom_call_target="tpu_custom_call" | custom-call | flops 2415919104 | bytes 2359296 | tf_op jit(solution)/shard_map/attend_first/pallas_call | solution.py:127
  101.4 5.1 %collective-permute-start = (bf16[1536,128]{1,0:T(8,128)(2,1)S(1)}, bf16[1536,128]{1,0:T(8,128)(2,1)S(1)}, u32[]{:S(2)}, u32[]{:S(2)}) collective-permute-start(bf16[1536,128]{1,0:T(8,128)(2,1)S(1)} %attend_first.1), channel_id=1, source_target_pairs={{0,1},{1,0},{2,3},{3,2},{4,5},{5,4},{6,7},{7,6},{8,9},{9,8},{10,11... | collective-permute-start | bytes 1179656 | tf_op jit(solution)/shard_map/ppermute | solution.py:152
  107.6 8.8 %attend_last.1 = bf16[1536,128]{1,0:T(8,128)(2,1)} custom-call(s32[1]{0:T(128)} %bitcast.part_ref.core_ref, f32[1]{0:T(128)} %bitcast.4.scale_ref, bf16[16,576,128]{2,1,0:T(8,128)(2,1)} %all-to-all-done.1.b_ref, bf16[1536,128]{1,0:T(8,128)(2,1)S(1)} %collective-permute-done.refs_0_), custom_call_target="tpu_custom_call" | custom-call | flops 2415919104 | bytes 2359296 | tf_op jit(solution)/shard_map/attend_last/pallas_call | solution.py:127
  116.4 4.8 %all-to-all-start.2 = ((bf16[32,48,128]{2,1,0:T(8,128)(2,1)}), bf16[32,48,128]{2,1,0:T(8,128)(2,1)}, u32[]{:S(2)}, u32[]{:S(2)}) async-start(bf16[32,48,128]{2,1,0:T(8,128)(2,1)} %bitcast.17), calls=%async_computation.2 | async-start | bytes 786432 | tf_op jit(solution)/shard_map/all_to_all | solution.py:393
  121.3 2.1 %slice.9 = bf16[2,384,512]{2,1,0:T(8,128)(2,1)} slice(bf16[4,384,512]{2,1,0:T(8,128)(2,1)} %collective-permute-done.7.refs_2_.w2), slice={[2:4], [0:384], [0:512]} | slice | bytes 1572864 | tf_op jit(solution)/shard_map/slice | solution.py:379
  123.4 3.1 %collective-permute-start.8 = (bf16[2,384,512]{2,1,0:T(8,128)(2,1)}, bf16[2,384,512]{2,1,0:T(8,128)(2,1)S(1)}, u32[]{:S(2)}, u32[]{:S(2)}) collective-permute-start(bf16[2,384,512]{2,1,0:T(8,128)(2,1)} %slice.9), channel_id=1, source_target_pairs={{0,2},{1,9},{2,4},{3,11},{4,6},{5,13},{6,0},{7,15},{8,10},{9,17},{... | collective-permute-start | bytes 2359304 | tf_op jit(solution)/shard_map/ppermute | solution.py:152
  126.5 2.1 %slice.8 = bf16[2,384,512]{2,1,0:T(8,128)(2,1)} slice(bf16[4,384,512]{2,1,0:T(8,128)(2,1)} %collective-permute-done.5.refs_1_.w1), slice={[0:2], [0:384], [0:512]} | slice | bytes 1572864 | tf_op jit(solution)/shard_map/slice | solution.py:379
  128.5 3.4 %collective-permute-start.6 = (bf16[2,384,512]{2,1,0:T(8,128)(2,1)}, bf16[2,384,512]{2,1,0:T(8,128)(2,1)}, u32[]{:S(2)}, u32[]{:S(2)}) collective-permute-start(bf16[2,384,512]{2,1,0:T(8,128)(2,1)} %slice.8), channel_id=1, source_target_pairs={{0,6},{1,25},{2,0},{3,27},{4,2},{5,29},{6,4},{7,31},{8,14},{9,1},{... | collective-permute-start | bytes 2359304 | tf_op jit(solution)/shard_map/ppermute | solution.py:152
  133.0 2.9 %collective-permute-start.1 = (bf16[48,1024]{1,0:T(8,128)(2,1)S(1)}, bf16[48,1024]{1,0:T(8,128)(2,1)S(1)}, u32[]{:S(2)}, u32[]{:S(2)}) collective-permute-start(bf16[48,1024]{1,0:T(8,128)(2,1)S(1)} %get-tuple-element.21), channel_id=1, source_target_pairs={{0,1},{1,0},{2,3},{3,2},{4,5},{5,4},{6,7},{7,6},{8,9},{9,8},{10,11... | collective-permute-start | bytes 294920 | tf_op jit(solution)/shard_map/ppermute | solution.py:152
  136.8 3.4 %project_near.1.refs_2_ = f32[96,3072]{1,0:T(8,128)S(1)} custom-call(s32[3]{0:T(128)S(1)} %pad_add_fusion.place_ref, bf16[48,1024]{1,0:T(8,128)(2,1)S(1)} %get-tuple-element.20.keep_ref, bf16[48,1024]{1,0:T(8,128)(2,1)S(1)} %collective-permute-done.1.received_ref, bf16[4,384,512]{2,1,0:T(8,128)(2,1)S(1)} %pad_maximum_fusion.refs_0_.w0, ...), custom_call_target="tpu_custom_call" | custom-call | tf_op jit(solution)/shard_map/project_near/pallas_call | solution.py:233
  140.3 1.6 collective-permute-done.6.refs_0_.w3
  141.9 1.9 %project_far.1 = (f32[48,3072]{1,0:T(8,128)S(1)}, bf16[48,3072]{1,0:T(8,128)(2,1)S(1)}) custom-call(s32[3]{0:T(128)S(1)} %pad_add_fusion.place_ref, bf16[48,1024]{1,0:T(8,128)(2,1)S(1)} %get-tuple-element.20.keep_ref, bf16[48,1024]{1,0:T(8,128)(2,1)S(1)} %collective-permute-done.1.received_ref, bf16[2,384,512]{2,1,0:T(8,128)(2,1)} %collective-permute-done.6.refs_0_.w3, ...), custom_call_target="tpu_custom_call" | custom-call | tf_op jit(solution)/shard_map/project_far/pallas_call | solution.py:233
  143.7 3.7 %collective-permute-start.9 = (bf16[48,3072]{1,0:T(8,128)(2,1)S(1)}, bf16[48,3072]{1,0:T(8,128)(2,1)S(1)}, u32[]{:S(2)}, u32[]{:S(2)}) collective-permute-start(bf16[48,3072]{1,0:T(8,128)(2,1)S(1)} %get-tuple-element.24), channel_id=1, source_target_pairs={{0,1},{1,0},{2,3},{3,2},{4,5},{5,4},{6,7},{7,6},{8,9},{9,8},{10,11... | collective-permute-start | bytes 884744 | tf_op jit(solution)/shard_map/ppermute | solution.py:152
  147.5 1.2 collective-permute-done.9.received_ref
  148.7 2.0 %normalize.1 = (bf16[48,3072]{1,0:T(8,128)(2,1)}, bf16[48,3072]{1,0:T(8,128)(2,1)S(1)}) custom-call(f32[48,3072]{1,0:T(8,128)S(1)} %get-tuple-element.23.own_ref, bf16[48,3072]{1,0:T(8,128)(2,1)S(1)} %collective-permute-done.9.received_ref, f32[48,3072]{1,0:T(8,128)S(1)} %copy-done.5, f32[48,3072]{1,0:T(8,128)S(1)} %copy-done.7, f32[1,3072]{1,0:T(1,128)S(1)} %reshape.43.gain_ref), custom_call_target="tpu_custom_call" | custom-call | tf_op jit(solution)/shard_map/normalize/pallas_call | solution.py:279
  150.7 2.3 %collective-permute-start.10 = (bf16[48,3072]{1,0:T(8,128)(2,1)S(1)}, bf16[48,3072]{1,0:T(8,128)(2,1)S(1)}, u32[]{:S(2)}, u32[]{:S(2)}) collective-permute-start(bf16[48,3072]{1,0:T(8,128)(2,1)S(1)} %get-tuple-element.29.grad_ref), channel_id=1, source_target_pairs={{0,1},{1,0},{2,3},{3,2},{4,5},{5,4},{6,7},{7,6},{8,9},{9,8},{10,11... | collective-permute-start | bytes 884744 | tf_op jit(solution)/shard_map/ppermute | solution.py:152
  154.2 3.5 %project_back.1 = bf16[96,1024]{1,0:T(8,128)(2,1)S(1)} custom-call(s32[3]{0:T(128)S(1)} %pad_add_fusion.place_ref, bf16[48,3072]{1,0:T(8,128)(2,1)S(1)} %get-tuple-element.29.grad_ref, bf16[48,3072]{1,0:T(8,128)(2,1)S(1)} %collective-permute-done.10.received_ref, bf16[4,384,512]{2,1,0:T(8,128)(2,1)S(1)} %pad_maximum_fusion.refs_0_.w0, ...), custom_call_target="tpu_custom_call" | custom-call | tf_op jit(solution)/shard_map/project_back/pallas_call | solution.py:307
  157.7 8.8 %all-gather = bf16[384,1024]{1,0:T(8,128)(2,1)S(1)} all-gather(bf16[96,1024]{1,0:T(8,128)(2,1)S(1)} %project_back.1), channel_id=2, replica_groups=mesh['c'=8,'z'=2,'y'=4,'h'=2,'l'=2,'k'=2] {'l','k'}, dimensions={0}, use_global_device_ids=true | all-gather | bytes 983040 | tf_op jit(solution)/shard_map/all_gather | solution.py:402
  166.5 1.7 scatter_scaled.1
  (47 shorter events, 10.5 us)
Async XLA Ops:
  0.6 56.5 %copy-start = (bf16[192,3072]{1,0:T(8,128)(2,1)S(1)}, bf16[192,3072]{1,0:T(8,128)(2,1)}, u32[]{:S(2)}) copy-start(bf16[192,3072]{1,0:T(8,128)(2,1)} %param.19) | copy-start | bytes 3538948
  0.6 18.7 %copy-start.2 = (bf16[1,192,2048]{2,1,0:T(8,128)(2,1)S(1)}, bf16[1,192,2048]{2,1,0:T(8,128)(2,1)}, u32[]{:S(2)}) copy-start(bf16[1,192,2048]{2,1,0:T(8,128)(2,1)} %param.11) | copy-start | bytes 2359300
  0.7 18.7 %copy-start.1 = (bf16[1,192,2048]{2,1,0:T(8,128)(2,1)S(1)}, bf16[1,192,2048]{2,1,0:T(8,128)(2,1)}, u32[]{:S(2)}) copy-start(bf16[1,192,2048]{2,1,0:T(8,128)(2,1)} %param.10) | copy-start | bytes 2359300
  2.3 34.0 %all-to-all-start = ((bf16[16,24,512]{2,1,0:T(8,128)(2,1)}), bf16[16,24,512]{2,1,0:T(8,128)(2,1)}, u32[]{:S(2)}, u32[]{:S(2)}) async-start(bf16[16,24,512]{2,1,0:T(8,128)(2,1)} %broadcast_in_dim.16), calls=%async_computation | async-start | bytes 786432 | tf_op jit(solution)/shard_map/all_to_all | solution.py:363
  19.4 1.1 copy-start.3
  36.3 11.6 %copy-start.8 = (f32[3072]{0:T(1024)S(1)}, f32[3072]{0:T(1024)}, u32[]{:S(2)}) copy-start(f32[3072]{0:T(1024)} %param.18) | copy-start | bytes 36868
  36.3 57.0 %all-to-all-start.1 = ((bf16[16,576,128]{2,1,0:T(8,128)(2,1)}), bf16[16,576,128]{2,1,0:T(8,128)(2,1)}, u32[]{:S(2)}, u32[]{:S(2)}) async-start(bf16[16,576,128]{2,1,0:T(8,128)(2,1)} %prepare.1), calls=%async_computation.1 | async-start | bytes 4718592 | tf_op jit(solution)/shard_map/all_to_all | solution.py:367
  48.1 37.1 %collective-permute-start.4 = (bf16[384,512]{1,0:T(8,128)(2,1)}, bf16[384,512]{1,0:T(8,128)(2,1)}, u32[]{:S(2)}, u32[]{:S(2)}) collective-permute-start(bf16[384,512]{1,0:T(8,128)(2,1)} %bitcast.6), channel_id=1, source_target_pairs={{0,24},{1,7},{2,26},{3,5},{4,28},{5,3},{6,30},{7,1},{8,16},{9,15},... | collective-permute-start | bytes 1179656 | tf_op jit(solution)/shard_map/ppermute | solution.py:152
  52.6 32.7 %collective-permute-start.3 = (bf16[384,512]{1,0:T(8,128)(2,1)}, bf16[384,512]{1,0:T(8,128)(2,1)}, u32[]{:S(2)}, u32[]{:S(2)}) collective-permute-start(bf16[384,512]{1,0:T(8,128)(2,1)} %bitcast.6), channel_id=1, source_target_pairs={{0,16},{1,5},{2,18},{3,7},{4,20},{5,1},{6,22},{7,3},{8,24},{9,13},... | collective-permute-start | bytes 1179656 | tf_op jit(solution)/shard_map/ppermute | solution.py:152
  54.8 30.5 %collective-permute-start.2 = (bf16[384,512]{1,0:T(8,128)(2,1)}, bf16[384,512]{1,0:T(8,128)(2,1)}, u32[]{:S(2)}, u32[]{:S(2)}) collective-permute-start(bf16[384,512]{1,0:T(8,128)(2,1)} %bitcast.6), channel_id=1, source_target_pairs={{0,8},{1,3},{2,10},{3,1},{4,12},{5,7},{6,14},{7,5},{8,0},{9,11},{1... | collective-permute-start | bytes 1179656 | tf_op jit(solution)/shard_map/ppermute | solution.py:152
  59.3 2.2 %copy-start.9 = (f32[64]{0:T(128)S(1)}, f32[64]{0:T(128)}, u32[]{:S(2)}) copy-start(f32[64]{0:T(128)} %param.15) | copy-start | bytes 772
  59.7 0.9 copy-start.4
  60.6 0.9 copy-start.6
  86.8 34.5 %collective-permute-start.7 = (bf16[4,384,512]{2,1,0:T(8,128)(2,1)S(1)}, bf16[4,384,512]{2,1,0:T(8,128)(2,1)}, u32[]{:S(2)}, u32[]{:S(2)}) collective-permute-start(bf16[4,384,512]{2,1,0:T(8,128)(2,1)S(1)} %pad_maximum_fusion.refs_0_.w0), channel_id=1, source_target_pairs={{0,2},{1,9},{2,4},{3,11},{4,6},{5,13},{6,0},{7,15},{8,10},{9,17},{... | collective-permute-start | bytes 4718600 | tf_op jit(solution)/shard_map/ppermute | solution.py:152
  89.7 36.8 %collective-permute-start.5 = (bf16[4,384,512]{2,1,0:T(8,128)(2,1)S(1)}, bf16[4,384,512]{2,1,0:T(8,128)(2,1)}, u32[]{:S(2)}, u32[]{:S(2)}) collective-permute-start(bf16[4,384,512]{2,1,0:T(8,128)(2,1)S(1)} %pad_maximum_fusion.refs_0_.w0), channel_id=1, source_target_pairs={{0,6},{1,25},{2,0},{3,27},{4,2},{5,29},{6,4},{7,31},{8,14},{9,1},{... | collective-permute-start | bytes 4718600 | tf_op jit(solution)/shard_map/ppermute | solution.py:152
  101.4 6.2 %collective-permute-start = (bf16[1536,128]{1,0:T(8,128)(2,1)S(1)}, bf16[1536,128]{1,0:T(8,128)(2,1)S(1)}, u32[]{:S(2)}, u32[]{:S(2)}) collective-permute-start(bf16[1536,128]{1,0:T(8,128)(2,1)S(1)} %attend_first.1), channel_id=1, source_target_pairs={{0,1},{1,0},{2,3},{3,2},{4,5},{5,4},{6,7},{7,6},{8,9},{9,8},{10,11... | collective-permute-start | bytes 1179656 | tf_op jit(solution)/shard_map/ppermute | solution.py:152
  116.4 15.5 %all-to-all-start.2 = ((bf16[32,48,128]{2,1,0:T(8,128)(2,1)}), bf16[32,48,128]{2,1,0:T(8,128)(2,1)}, u32[]{:S(2)}, u32[]{:S(2)}) async-start(bf16[32,48,128]{2,1,0:T(8,128)(2,1)} %bitcast.17), calls=%async_computation.2 | async-start | bytes 786432 | tf_op jit(solution)/shard_map/all_to_all | solution.py:393
  123.4 16.9 %collective-permute-start.8 = (bf16[2,384,512]{2,1,0:T(8,128)(2,1)}, bf16[2,384,512]{2,1,0:T(8,128)(2,1)S(1)}, u32[]{:S(2)}, u32[]{:S(2)}) collective-permute-start(bf16[2,384,512]{2,1,0:T(8,128)(2,1)} %slice.9), channel_id=1, source_target_pairs={{0,2},{1,9},{2,4},{3,11},{4,6},{5,13},{6,0},{7,15},{8,10},{9,17},{... | collective-permute-start | bytes 2359304 | tf_op jit(solution)/shard_map/ppermute | solution.py:152
  128.5 13.3 %collective-permute-start.6 = (bf16[2,384,512]{2,1,0:T(8,128)(2,1)}, bf16[2,384,512]{2,1,0:T(8,128)(2,1)}, u32[]{:S(2)}, u32[]{:S(2)}) collective-permute-start(bf16[2,384,512]{2,1,0:T(8,128)(2,1)} %slice.8), channel_id=1, source_target_pairs={{0,6},{1,25},{2,0},{3,27},{4,2},{5,29},{6,4},{7,31},{8,14},{9,1},{... | collective-permute-start | bytes 2359304 | tf_op jit(solution)/shard_map/ppermute | solution.py:152
  133.0 3.8 %collective-permute-start.1 = (bf16[48,1024]{1,0:T(8,128)(2,1)S(1)}, bf16[48,1024]{1,0:T(8,128)(2,1)S(1)}, u32[]{:S(2)}, u32[]{:S(2)}) collective-permute-start(bf16[48,1024]{1,0:T(8,128)(2,1)S(1)} %get-tuple-element.21), channel_id=1, source_target_pairs={{0,1},{1,0},{2,3},{3,2},{4,5},{5,4},{6,7},{7,6},{8,9},{9,8},{10,11... | collective-permute-start | bytes 294920 | tf_op jit(solution)/shard_map/ppermute | solution.py:152
  140.3 8.4 %copy-start.5 = (f32[48,3072]{1,0:T(8,128)S(1)}, f32[48,3072]{1,0:T(8,128)}, u32[]{:S(2)}) copy-start(f32[48,3072]{1,0:T(8,128)} %copy-done.4) | copy-start | bytes 1769476
  140.3 8.4 %copy-start.7 = (f32[48,3072]{1,0:T(8,128)S(1)}, f32[48,3072]{1,0:T(8,128)}, u32[]{:S(2)}) copy-start(f32[48,3072]{1,0:T(8,128)} %copy-done.6) | copy-start | bytes 1769476
  143.7 4.9 %collective-permute-start.9 = (bf16[48,3072]{1,0:T(8,128)(2,1)S(1)}, bf16[48,3072]{1,0:T(8,128)(2,1)S(1)}, u32[]{:S(2)}, u32[]{:S(2)}) collective-permute-start(bf16[48,3072]{1,0:T(8,128)(2,1)S(1)} %get-tuple-element.24), channel_id=1, source_target_pairs={{0,1},{1,0},{2,3},{3,2},{4,5},{5,4},{6,7},{7,6},{8,9},{9,8},{10,11... | collective-permute-start | bytes 884744 | tf_op jit(solution)/shard_map/ppermute | solution.py:152
  150.7 3.5 %collective-permute-start.10 = (bf16[48,3072]{1,0:T(8,128)(2,1)S(1)}, bf16[48,3072]{1,0:T(8,128)(2,1)S(1)}, u32[]{:S(2)}, u32[]{:S(2)}) collective-permute-start(bf16[48,3072]{1,0:T(8,128)(2,1)S(1)} %get-tuple-element.29.grad_ref), channel_id=1, source_target_pairs={{0,1},{1,0},{2,3},{3,2},{4,5},{5,4},{6,7},{7,6},{8,9},{9,8},{10,11... | collective-permute-start | bytes 884744 | tf_op jit(solution)/shard_map/ppermute | solution.py:152
